TPU v7x, 128 devices: a whole 4x4x4 slice. The times are simulated.
128 devices in a mesh: row: 8 (over x, core), col: 16 (over z, y).
Axes of the slice: x: 4, y: 4, z: 4, core: 2. Of those that a mesh axis runs over, the one named last changes fastest.
Arguments:
- tiles: bfloat16 [8, 16, 384, 128, 128], P('row', 'col'), may hold values from -0.15625 to 0.15625
- tile_row: int32 [8, 16, 384], P('row', 'col'), may hold values from 0 to 511, as said below
- tile_col: int32 [8, 16, 384], P('row', 'col'), may hold values from 0 to 255
- tile_count: int32 [8, 16], P('row', 'col'), may hold values from 96 to 384, as said below
- vectors: bfloat16 [32, 8, 16, 4096], P(None, 'row', 'col'), may hold values from -6 to 6
Outputs:
- image: bfloat16 [32, 524288], P(None, ('row', 'col'))
- back_image: bfloat16 [32, 8, 16, 4096], P(None, 'row', 'col')
Inputs may be any that keep to these rules, and one draw needn't show every extreme that they name: `tile_count`: some device has exactly 384 live slots. `tile_row`: the slots of each device, live or not, name exactly 12 distinct block rows in each aligned run of 32 block rows.
All inputs are finite; a program needn't handle non-finite values.
Results may differ from a plain program's by a relative error of at most 0.0041.
Values may be sent and summed in bfloat16 or wider, within the bound.
No kernel may reach another device: no remote copies, remote signals or barrier semaphores. Data moves between devices by JAX's collectives and lax.ppermute only.
A program may use at most 128 MiB of HBM per device.

v0:
```python
import jax
import jax.numpy as jnp
from jax import lax
from jax.sharding import PartitionSpec as P


def per_device(tiles, tile_row, tile_col, tile_count, vectors):
    vec_cols = vectors.shape[0]
    tile_size = tiles.shape[-1]
    slot_count = tiles.shape[2]
    local_tiles = tiles[0, 0]
    rows_local = tile_row[0, 0]
    cols_local = tile_col[0, 0]
    live_count = tile_count[0, 0]
    live_mask = (jnp.arange(slot_count, dtype=jnp.int32) < live_count).astype(jnp.float32)
    row_devices = lax.axis_size("row")
    col_devices = lax.axis_size("col")
    gathered = lax.all_gather(vectors, "row", axis=1, tiled=True)
    blk_cols = gathered.shape[1] * gathered.shape[3] // tile_size
    blk_rows = blk_cols * col_devices // row_devices
    col_vectors = gathered.reshape(vec_cols, blk_cols, tile_size)

    def slot_group():
        return (local_tiles, rows_local, cols_local, live_mask)

    def forward_terms(totals, start_slot, group_size):
        tile_block, row_index, col_index, slot_mask = slot_group()
        picked = jnp.take(col_vectors, col_index, axis=1)
        product = jnp.einsum("ksj,sij->ksi", picked, tile_block, preferred_element_type=jnp.float32)
        return totals.at[:, row_index].add(product * slot_mask[None, :, None])

    def sweep(term_fn, totals_zero):
        return term_fn(totals_zero, 0, slot_count)

    forward_sum = sweep(forward_terms, jnp.zeros((vec_cols, blk_rows, tile_size), jnp.float32))
    partial_rows = forward_sum.reshape(vec_cols, blk_rows * tile_size)
    share_sum = lax.psum_scatter(partial_rows, "col", scatter_dimension=1, tiled=True)
    image = share_sum.astype(jnp.bfloat16)
    row_image = lax.all_gather(image, "col", axis=1, tiled=True)
    row_blocks = row_image.reshape(vec_cols, blk_rows, tile_size)

    def backward_terms(totals, start_slot, group_size):
        tile_block, row_index, col_index, slot_mask = slot_group()
        picked = jnp.take(row_blocks, row_index, axis=1)
        product = jnp.einsum("ksi,sij->ksj", picked, tile_block, preferred_element_type=jnp.float32)
        return totals.at[:, col_index].add(product * slot_mask[None, :, None])

    backward_sum = sweep(backward_terms, jnp.zeros((vec_cols, blk_cols, tile_size), jnp.float32))
    partial_cols = backward_sum.reshape(vec_cols, row_devices, 1, vectors.shape[3])
    back_sum = lax.psum_scatter(partial_cols, "row", scatter_dimension=1, tiled=True)
    return (image, back_sum.astype(jnp.bfloat16))


def solution(mesh):
    return jax.shard_map(
        per_device,
        mesh=mesh,
        in_specs=(
            P("row", "col", None, None, None),
            P("row", "col", None),
            P("row", "col", None),
            P("row", "col"),
            P(None, "row", "col", None),
        ),
        out_specs=(P(None, ("row", "col")), P(None, "row", "col", None)),
        check_vma=False,
    )
```

profile of v0, /device:TPU:1, one launch (start us, length us, event | category | flops | bytes accessed | tf_op | source)
XLA Modules:
  0.0 398.2 jit_solution(5015955300966419793)
XLA Ops:
  8.6 0.7 reduce.1
  10.0 0.7 fusion.21
  10.7 27.8 %all-gather.3.cloned.1.call-done = bf16[32,8,1,4096]{3,0,2,1:T(8,128)(2,1)} async-done(((bf16[32,1,1,4096]{3,0,2,1:T(8,128)(2,1)}), bf16[32,8,1,4096]{3,0,2,1:T(8,128)(2,1)}) %all-gather.3.cloned.1.call-update) | async-done | bytes 2097168 | tf_op jit(solution)/shard_map/all_gather | solution.py:18
  38.5 2.7 copy.18
  41.2 2.4 reshape.89
  43.6 2.9 copy.19
  46.6 3.2 gather_fusion
  49.7 14.9 %broadcast_multiply_fusion.1 = f32[384,32,128]{2,1,0:T(8,128)} fusion(f32[384]{0:T(512)S(1)} %get-tuple-element.6, bf16[1,1,384,128,128]{4,3,2,1,0:T(8,128)(2,1)} %param.5, bf16[384,32,128]{2,1,0:T(8,128)(2,1)} %gather_fusion, pred[384]{0:T(512)(128)(4,1)S(1)} %get-tuple-element.7), kind=kOutput, calls=%fused_computation.15 | convolution fusion | flops 405798912 | bytes 22022016 | tf_op jit(solution)/shard_map/ksj,sij->ksi/dot_general | solution.py:29
  64.7 4.3 %broadcast_in_dim.28 = f32[32,512,128]{2,0,1:T(8,128)} broadcast(f32[]{:T(128)} %constant.18.clone.1), dimensions={} | broadcast | bytes 8388612 | tf_op jit(solution)/shard_map/broadcast_in_dim | solution.py:35
  69.0 51.2 %scatter_fusion = f32[32,512,128]{2,0,1:T(8,128)} fusion(f32[32,512,128]{2,0,1:T(8,128)} %broadcast_in_dim.28, s32[384]{0:T(512)S(1)} %fusion.21, f32[384,32,128]{2,1,0:T(8,128)} %broadcast_multiply_fusion.1), kind=kCustom, calls=%fused_computation.2 | custom fusion | flops 1572864 | bytes 18875904 | tf_op jit(solution)/shard_map/scatter-add | solution.py:30
  120.2 7.1 %copy_bitcast_fusion = f32[32,65536]{1,0:T(8,128)} fusion(f32[32,512,128]{2,0,1:T(8,128)} %scatter_fusion), kind=kLoop, calls=%fused_computation.8 | loop fusion | bytes 16777216 | tf_op jit(solution)/shard_map/reshape | solution.py:36
  127.4 83.6 %reduce-scatter.3.cloned.1.call-done = f32[32,4096]{1,0:T(8,128)} async-done(((f32[32,65536]{1,0:T(8,128)}), f32[32,4096]{1,0:T(8,128)}) %reduce-scatter.3.cloned.1.call-update) | async-done | bytes 524304 | tf_op jit(solution)/shard_map/reduce_scatter | solution.py:37
  211.0 1.8 convert_element_type.14
  213.1 52.9 %all-gather.5.cloned.1.call-done = bf16[32,65536]{1,0:T(8,128)(2,1)} async-done(((bf16[32,4096]{1,0:T(8,128)(2,1)}), bf16[32,65536]{1,0:T(8,128)(2,1)}) %all-gather.5.cloned.1.call-update) | async-done | bytes 4194320 | tf_op jit(solution)/shard_map/all_gather | solution.py:39
  266.0 4.9 %copy_bitcast_fusion.1 = bf16[32,512,128]{2,0,1:T(8,128)(2,1)} fusion(bf16[32,65536]{1,0:T(8,128)(2,1)} %all-gather.5.cloned.1.call-done), kind=kLoop, calls=%fused_computation.9 | loop fusion | bytes 8388608 | tf_op jit(solution)/shard_map/reshape | solution.py:40
  270.9 3.4 gather_fusion.1
  274.3 9.0 %broadcast_multiply_fusion = f32[384,32,128]{2,1,0:T(8,128)} fusion(f32[384]{0:T(512)S(1)} %get-tuple-element.6, bf16[1,1,384,128,128]{4,3,2,1,0:T(8,128)(2,1)} %param.5, bf16[384,32,128]{2,1,0:T(8,128)(2,1)S(1)} %gather_fusion.1, pred[384]{0:T(512)(128)(4,1)S(1)} %compare_and_fusion), kind=kOutput, calls=%fused_computation.14 | convolution fusion | flops 405798912 | bytes 22022016 | tf_op jit(solution)/shard_map/ksi,sij->ksj/dot_general | solution.py:45
  283.3 2.6 broadcast_in_dim.31
  285.9 51.3 %scatter_fusion.1 = f32[32,256,128]{2,0,1:T(8,128)} fusion(f32[32,256,128]{2,0,1:T(8,128)} %broadcast_in_dim.31, s32[384]{0:T(512)S(1)} %fusion.22, f32[384,32,128]{2,1,0:T(8,128)} %broadcast_multiply_fusion), kind=kCustom, calls=%fused_computation.3 | custom fusion | flops 1572864 | bytes 18875904 | tf_op jit(solution)/shard_map/scatter-add | solution.py:46
  337.2 6.5 %copy.22 = f32[32,256,128]{2,1,0:T(8,128)} copy(f32[32,256,128]{2,0,1:T(8,128)} %scatter_fusion.1) | data formatting | bytes 8388608 | tf_op jit(solution)/shard_map/scatter-add | solution.py:46
  343.7 5.0 %reshape.92 = f32[32,8,1,4096]{3,1,0,2:T(8,128)} reshape(f32[32,256,128]{2,1,0:T(8,128)} %copy.22) | data formatting | bytes 8388608 | tf_op jit(solution)/shard_map/reshape | solution.py:49
  348.7 6.5 %copy.23 = f32[32,8,1,4096]{3,0,2,1:T(8,128)} copy(f32[32,8,1,4096]{3,1,0,2:T(8,128)} %reshape.92) | data formatting | bytes 8388608 | tf_op jit(solution)/shard_map/reshape | solution.py:49
  355.3 34.7 %reduce-scatter.5.cloned.1.call-done = f32[32,1,1,4096]{3,0,2,1:T(8,128)} async-done(((f32[32,8,1,4096]{3,0,2,1:T(8,128)}), f32[32,1,1,4096]{3,0,2,1:T(8,128)}) %reduce-scatter.5.cloned.1.call-update) | async-done | bytes 524304 | tf_op jit(solution)/shard_map/reduce_scatter | solution.py:50
  389.9 1.8 convert_element_type.15
  (16 shorter events, 1.8 us)
Async XLA Ops:
  7.2 31.3 %all-gather.3.cloned.1.call-start = ((), (), s32[]{:S(2)}) async-start(), calls=%async_computation.2 | async-start | bytes 2359296 | tf_op jit(solution)/shard_map/all_gather | solution.py:18
  7.9 203.1 %reduce-scatter.3.cloned.1.call-start = ((), (), s32[]{:S(2)}) async-start(), calls=%async_computation.3 | async-start | bytes 8912896 | tf_op jit(solution)/shard_map/reduce_scatter | solution.py:37
  127.3 85.7 %copy-start = (s32[1,1,384]{2,1,0:T(1,128)S(1)}, s32[1,1,384]{2,1,0:T(1,128)}, u32[]{:S(2)}) copy-start(s32[1,1,384]{2,1,0:T(1,128)} %param.6) | copy-start | bytes 4612
  127.3 138.6 %all-gather.5.cloned.1.call-start = ((), (), s32[]{:S(2)}) async-start(), calls=%async_computation.4 | async-start | bytes 4456448 | tf_op jit(solution)/shard_map/all_gather | solution.py:39
  212.8 177.1 %reduce-scatter.5.cloned.1.call-start = ((), (), s32[]{:S(2)}) async-start(), calls=%async_computation.5 | async-start | bytes 4718592 | tf_op jit(solution)/shard_map/reduce_scatter | solution.py:50
Sparse Core Ops, SparseCore 0:
  9.7 28.7 all-gather.2
  127.5 83.4 reduce-scatter.2
  213.7 52.2 all-gather.4
  355.4 34.4 reduce-scatter.4
where the time goes:
time: 402 us; the launch traced here: 398 us
  waiting for transfers between devices  200 us (50%)
  other arithmetic  108 us (27%)
  local copies, waits for them, and re-layouts  51.6 us (13%)
  matrix products  24 us (6%)
  between operations  14.4 us (4%)
    reduce_scatter x1, waiting for transfers between devices, per_device(): lax.psum_scatter(partial_rows, 'col', scatter_dimension=1, tiled=True)  83.6 us
    all_gather x1, waiting for transfers between devices, per_device(): row_image = lax.all_gather(image, 'col', axis=1, tiled=True)  52.9 us
    scatter-add x1, other arithmetic, backward_terms(): return totals.at[:, col_index].add(product * slot_mask[None, :, None])  51.3 us
    scatter-add x1, other arithmetic, forward_terms(): return totals.at[:, row_index].add(product * slot_mask[None, :, None])  51.2 us
    reduce_scatter x1, waiting for transfers between devices, per_device(): lax.psum_scatter(partial_cols, 'row', scatter_dimension=1, tiled=True)  34.7 us
    all_gather x1, waiting for transfers between devices, per_device(): gathered = lax.all_gather(vectors, 'row', axis=1, tiled=True)  27.8 us
    dot_general x1, matrix products, forward_terms(): jnp.einsum('ksj,sij->ksi', picked, tile_block, preferred_element_type=jnp...  14.9 us
    reshape x2, local copies, waits for them, and re-layouts, per_device(): backward_sum.reshape(vec_cols, row_devices, 1, vectors.shape[3])  11.5 us
  transfers between devices with their start and end apart: 4, of which 4 were waited for; matrix products, arithmetic and copies ran while one was open for 1% of the time, Pallas kernels for 0%

commit v1 on v0

v1 whole, which is shorter than its diff:
```python
import jax
import jax.numpy as jnp
from jax import lax
from jax.experimental import pallas as pl
from jax.experimental.pallas import tpu as pltpu
from jax.sharding import PartitionSpec as P

TILE = 128
K = 32
SHARE = 32
CAP = 12
N_COL = 16
N_X = 4
RUN_ROWS = CAP * K
PAY_ROWS = RUN_ROWS + 16
N_NAMED = N_COL * CAP
GROUP = 8
CHUNK = 32
VMEM_LIMIT = 56 << 20


def tile_copy(tiles, buf, sems, chunk):
    span = pl.ds(chunk * CHUNK, CHUNK)
    return pltpu.make_async_copy(tiles.at[span], buf.at[span], sems.at[chunk])


def start_tiles(tiles, buf, sems, live):
    for chunk in range(tiles.shape[0] // CHUNK):
        @pl.when(chunk * CHUNK < live)
        def _():
            tile_copy(tiles, buf, sems, chunk).start()


def sweep(live, tiles, buf, sems, left, left_index, total, total_index, dims):
    def group(g, _):
        @pl.when(g % (CHUNK // GROUP) == 0)
        def _():
            tile_copy(tiles, buf, sems, g // (CHUNK // GROUP)).wait()

        base = g * GROUP
        products = [
            lax.dot_general(
                left[left_index[base + u]],
                buf[base + u],
                (((1,), (dims,)), ((), ())),
                preferred_element_type=jnp.float32,
            )
            for u in range(GROUP)
        ]
        for u in range(GROUP):
            total[total_index[base + u]] += products[u]
        return 0

    lax.fori_loop(0, (live + GROUP - 1) // GROUP, group, 0)


def forward_kernel(rowc, cols, scal, tiles, ids, *refs):
    pieces, (send, vec, total, buf, sems) = refs[:8], refs[8:]
    live, x, core = scal[0], scal[1], scal[2]
    start_tiles(tiles, buf, sems, live)
    for d in range(N_X):
        for other in range(2):
            piece = pieces[d + N_X * other]
            first = (((x + d) % N_X) * 2 + (core + other) % 2) * SHARE
            for b in range(SHARE):
                vec[first + b] = piece[:, b * TILE:(b + 1) * TILE]

    def clear(p, _):
        total[p] = jnp.zeros((K, TILE), jnp.float32)
        return 0

    lax.fori_loop(0, N_NAMED, clear, 0, unroll=8)
    sweep(live, tiles, buf, sems, vec, cols, total, rowc, 1)

    def pack(c, _):
        for q in range(CAP):
            send[c, q * K:(q + 1) * K] = total[c * CAP + q].astype(jnp.bfloat16)
        send[c, RUN_ROWS:] = ids[c]
        return 0

    lax.fori_loop(0, N_COL, pack, 0)


def reduce_kernel(recv, image, send, total, blocks, wide_ids, ids, sem):
    for c in range(N_COL):
        wide_ids[c:c + 1] = recv[c, RUN_ROWS:][0:1].astype(jnp.float32).astype(jnp.int32)
    copy = pltpu.make_async_copy(wide_ids, ids, sem)
    copy.start()
    for b in range(SHARE):
        total[b] = jnp.zeros((K, TILE), jnp.float32)
    copy.wait()

    def add(c, _):
        for q in range(CAP):
            total[ids[c, q]] += recv[c, q * K:(q + 1) * K].astype(jnp.float32)
        return 0

    lax.fori_loop(0, N_COL, add, 0)
    for b in range(SHARE):
        block = total[b].astype(jnp.bfloat16)
        blocks[b] = block
        image[:, b * TILE:(b + 1) * TILE] = block

    def spread(c, _):
        for q in range(CAP):
            send[c, q * K:(q + 1) * K] = blocks[ids[c, q]]
        return 0

    lax.fori_loop(0, N_COL, spread, 0)


def backward_kernel(rowc, colx, scal, tiles, recv, keep, give, total, buf, sems):
    live, core = scal[0], scal[2]
    start_tiles(tiles, buf, sems, live)

    def clear(p, _):
        total[p] = jnp.zeros((K, TILE), jnp.float32)
        return 0

    lax.fori_loop(0, 2 * N_X * SHARE, clear, 0, unroll=8)
    sweep(live, tiles, buf, sems, recv, rowc, total, colx, 0)

    def split(b, _):
        for x in range(N_X):
            keep[x, b] = total[(x * 2 + core) * SHARE + b]
            give[x, b] = total[(x * 2 + 1 - core) * SHARE + b].astype(give.dtype)
        return 0

    lax.fori_loop(0, SHARE, split, 0, unroll=4)


def pair_kernel(scal, keep, got, own, one, two, three):
    x = scal[1]

    def step(b, _):
        for d, out in enumerate((own, one, two, three)):
            to = (x + d) % N_X
            out[b] = (keep[to, b] + got[to, b].astype(jnp.float32)).astype(out.dtype)
        return 0

    lax.fori_loop(0, SHARE, step, 0, unroll=2)


def final_kernel(own, one, two, three, out):
    for b in range(SHARE):
        total = own[b] + one[b].astype(jnp.float32)
        total = total + two[b].astype(jnp.float32) + three[b].astype(jnp.float32)
        out[:, b * TILE:(b + 1) * TILE] = total.astype(jnp.bfloat16)


def call(kernel, outs, scalars, arrays, scratch=(), tiles=False):
    spec_any = pl.BlockSpec(memory_space=pl.ANY)
    spec_vmem = pl.BlockSpec(memory_space=pltpu.VMEM)
    spec_smem = pl.BlockSpec(memory_space=pltpu.SMEM)
    specs = [spec_smem] * len(scalars)
    specs += [spec_any if tiles and i == 0 else spec_vmem for i in range(len(arrays))]
    single = not isinstance(outs, (list, tuple))
    return pl.pallas_call(
        kernel,
        out_shape=outs,
        in_specs=specs,
        out_specs=spec_vmem if single else [spec_vmem] * len(outs),
        scratch_shapes=list(scratch),
        compiler_params=pltpu.CompilerParams(vmem_limit_bytes=VMEM_LIMIT),
    )(*scalars, *arrays)


def named_rows(rows):
    hits = rows[:, None] == jnp.arange(N_COL * SHARE, dtype=jnp.int32)[None, :]
    present = jnp.any(hits, axis=0).astype(jnp.int32).reshape(N_COL, SHARE)
    place = jnp.arange(SHARE, dtype=jnp.int32)
    rank = jnp.sum(jnp.where(place[:, None] < place[None, :], present[:, :, None], 0), axis=1)
    match = (rank[:, None, :] == jnp.arange(CAP, dtype=jnp.int32)[None, :, None]) & (present[:, None, :] > 0)
    ids = jnp.sum(jnp.where(match, place[None, None, :], 0), axis=2)
    position = (rank + CAP * jnp.arange(N_COL, dtype=jnp.int32)[:, None]).reshape(-1)
    rowc = jnp.sum(jnp.where(hits, position[None, :], 0), axis=1)
    return ids, rowc


def per_device(tiles, tile_row, tile_col, tile_count, vectors):
    bf16, f32 = jnp.bfloat16, jnp.float32
    shape = jax.ShapeDtypeStruct
    local = tiles[0, 0]
    slots = local.shape[0]
    rows, cols, live = tile_row[0, 0], tile_col[0, 0], tile_count[0, 0]
    row_at = lax.axis_index("row")
    scal = jnp.stack([live, row_at // 2, row_at % 2]).astype(jnp.int32)

    def along_x(value, d):
        return lax.ppermute(value, "row", [(i, (i - 2 * d) % 8) for i in range(8)])

    def swap_core(value):
        return lax.ppermute(value, "row", [(i, i ^ 1) for i in range(8)])

    mine = vectors.reshape(K, SHARE * TILE)
    near = [mine] + [along_x(mine, d) for d in range(1, N_X)]
    pieces = near + [swap_core(v) for v in near]

    ids, rowc = named_rows(rows)
    alive = jnp.arange(slots, dtype=jnp.int32) < live
    row_to = jnp.where(alive, rowc, N_NAMED)
    col_to = jnp.where(alive, cols, 2 * N_X * SHARE)
    lanes = jnp.pad(ids, ((0, 0), (0, TILE - CAP))).astype(bf16)
    id_rows = jnp.broadcast_to(lanes[:, None, :], (N_COL, 16, TILE))

    tile_scratch = [pltpu.VMEM((slots, TILE, TILE), bf16), pltpu.SemaphoreType.DMA((slots // CHUNK,))]
    send = call(
        forward_kernel,
        shape((N_COL, PAY_ROWS, TILE), bf16),
        [row_to, cols, scal],
        [local, id_rows] + pieces,
        [pltpu.VMEM((2 * N_X * SHARE, K, TILE), bf16), pltpu.VMEM((N_NAMED + 1, K, TILE), f32)] + tile_scratch,
        tiles=True,
    )
    recv = lax.all_to_all(send, "col", 0, 0, tiled=True)
    image, spread = call(
        reduce_kernel,
        [shape((K, SHARE * TILE), bf16), shape((N_COL, RUN_ROWS, TILE), bf16)],
        [],
        [recv],
        [
            pltpu.VMEM((SHARE, K, TILE), f32),
            pltpu.VMEM((SHARE, K, TILE), bf16),
            pltpu.VMEM((N_COL, TILE), jnp.int32),
            pltpu.SMEM((N_COL, TILE), jnp.int32),
            pltpu.SemaphoreType.DMA,
        ],
    )
    named = lax.all_to_all(spread, "col", 0, 0, tiled=True).reshape(N_NAMED, K, TILE)
    keep, give = call(
        backward_kernel,
        [shape((N_X, SHARE, K, TILE), f32), shape((N_X, SHARE, K, TILE), bf16)],
        [rowc, col_to, scal],
        [local, named],
        [pltpu.VMEM((2 * N_X * SHARE + 1, K, TILE), f32)] + tile_scratch,
        tiles=True,
    )
    got = swap_core(give)
    block = (SHARE, K, TILE)
    own, *away = call(
        pair_kernel, [shape(block, f32)] + [shape(block, bf16)] * 3, [scal], [keep, got]
    )
    parts = [lax.ppermute(v, "row", [(i, (i + 2 * d) % 8) for i in range(8)]) for d, v in enumerate(away, 1)]
    back = call(final_kernel, shape((K, SHARE * TILE), bf16), [], [own] + parts)
    return image, back.reshape(vectors.shape)


def solution(mesh):
    return jax.shard_map(
        per_device,
        mesh=mesh,
        in_specs=(
            P("row", "col", None, None, None),
            P("row", "col", None),
            P("row", "col", None),
            P("row", "col"),
            P(None, "row", "col", None),
        ),
        out_specs=(P(None, ("row", "col")), P(None, "row", "col", None)),
        check_vma=False,
    )
```

time: 402 us -> 143 us (0.36)
  waiting for transfers between devices: 200 us -> 43.5 us
  other arithmetic: 108 us -> 4.71 us
  local copies, waits for them, and re-layouts: 51.6 us -> 4.19 us
  blocking collectives: 0 us -> 37.8 us
  Pallas kernels: 0 us -> 30.9 us
  matrix products: 24 us -> 0 us
  starting transfers between devices: 0.34 us -> 18.1 us
  between operations: 14.4 us -> 1.44 us
    reduce_scatter x2 -> x0, waiting for transfers between devices: 118 us -> none  [the longest x1 83.6 us: per_device(): lax.psum_scatter(partial_rows, 'col', scatter_dimension=1, tiled=True)]
    scatter-add x2 -> x0, other arithmetic: 102 us -> none  [the longest x1 51.3 us: backward_terms(): return totals.at[:, col_index].add(product * slot_mask[None, :, None])]
    all_gather x2 -> x0, waiting for transfers between devices: 80.7 us -> none  [the longest x1 52.9 us: per_device(): row_image = lax.all_gather(image, 'col', axis=1, tiled=True)]
    all_to_all x0 -> x1, blocking collectives: none -> 37.8 us  [per_device(): recv = lax.all_to_all(send, 'col', 0, 0, tiled=True)]
    pallas_call x0 -> x5, Pallas kernels: none -> 30.9 us  [call(): pl.pallas_call(kernel, out_shape=outs, in_specs=specs, out_specs=spec_vme...]
    reshape x6 -> x0, local copies, waits for them, and re-layouts: 28.8 us -> none  [the longest x2 11.5 us: per_device(): backward_sum.reshape(vec_cols, row_devices, 1, vectors.shape[3])]
    dot_general x2 -> x0, matrix products: 24 us -> none  [the longest x1 14.9 us: forward_terms(): jnp.einsum('ksj,sij->ksi', picked, tile_block, preferred_element_type=jnp...]
    all_to_all x0 -> x1, waiting for transfers between devices: none -> 23.3 us  [per_device(): lax.all_to_all(spread, 'col', 0, 0, tiled=True).reshape(N_NAMED, K, TILE)]
  transfers between devices with their start and end apart: 4 -> 12, of which waited for: 4 -> 6; matrix products, arithmetic and copies ran while one was open for 1% -> 4% of each run, Pallas kernels for 0% -> 0%
where the time goes in v1:
time: 143 us; the launch traced here: 141 us
  waiting for transfers between devices  43.5 us (30%)
  blocking collectives  37.8 us (26%)
  Pallas kernels  30.9 us (22%)
  starting transfers between devices  18.1 us (13%)
  other arithmetic  4.71 us (3%)
  local copies, waits for them, and re-layouts  4.19 us (3%)
  between operations  1.44 us (1%)
    all_to_all x1, blocking collectives, per_device(): recv = lax.all_to_all(send, 'col', 0, 0, tiled=True)  37.8 us
    pallas_call x5, Pallas kernels, call(): pl.pallas_call(kernel, out_shape=outs, in_specs=specs, out_specs=spec_vme...  30.9 us
    all_to_all x1, waiting for transfers between devices, per_device(): lax.all_to_all(spread, 'col', 0, 0, tiled=True).reshape(N_NAMED, K, TILE)  23.3 us
    ppermute x3, waiting for transfers between devices, per_device(): lax.ppermute(v, 'row', [(i, (i + 2 * d) % 8) for i in range(8)])  9.93 us
    ppermute x3, waiting for transfers between devices, along_x(): return lax.ppermute(value, 'row', [(i, (i - 2 * d) % 8) for i in range(8)])  7.73 us
    ppermute x3, starting transfers between devices, per_device(): lax.ppermute(v, 'row', [(i, (i + 2 * d) % 8) for i in range(8)])  5.8 us
    ppermute x3, starting transfers between devices, along_x(): return lax.ppermute(value, 'row', [(i, (i - 2 * d) % 8) for i in range(8)])  4.91 us
    all_to_all x1, starting transfers between devices, per_device(): lax.all_to_all(spread, 'col', 0, 0, tiled=True).reshape(N_NAMED, K, TILE)  3.72 us
  transfers between devices with their start and end apart: 12, of which 6 were waited for; matrix products, arithmetic and copies ran while one was open for 4% of the time, Pallas kernels for 0%

profile of v1, /device:TPU:1, one launch (start us, length us, event | category | flops | bytes accessed | tf_op | source)
XLA Modules:
  0.0 140.7 jit_solution(8502323177138584719)
XLA Ops:
  0.6 1.5 %collective-permute-start.3 = (bf16[32,4096]{1,0:T(8,128)(2,1)}, bf16[32,4096]{1,0:T(8,128)(2,1)S(1)}, u32[]{:S(2)}, u32[]{:S(2)}) collective-permute-start(bf16[32,4096]{1,0:T(8,128)(2,1)} %bitcast.14), channel_id=1, source_target_pairs={{0,16},{16,0},{32,48},{48,32},{64,80},{80,64},{96,112},{112,96},{1... | collective-permute-start | bytes 786440 | tf_op jit(solution)/shard_map/ppermute | solution.py:193
  2.1 1.3 collective-permute-start.2
  3.4 2.5 %collective-permute-start.1 = (bf16[32,4096]{1,0:T(8,128)(2,1)}, bf16[32,4096]{1,0:T(8,128)(2,1)S(1)}, u32[]{:S(2)}, u32[]{:S(2)}) collective-permute-start(bf16[32,4096]{1,0:T(8,128)(2,1)} %bitcast.16), channel_id=1, source_target_pairs={{0,64},{16,80},{32,96},{48,112},{64,0},{80,16},{96,32},{112,48},{1... | collective-permute-start | bytes 786440 | tf_op jit(solution)/shard_map/ppermute | solution.py:190
  5.9 1.2 collective-permute-start
  9.5 1.9 %collective-permute-done.2.refs_3_ = bf16[32,4096]{1,0:T(8,128)(2,1)S(1)} collective-permute-done((bf16[32,4096]{1,0:T(8,128)(2,1)}, bf16[32,4096]{1,0:T(8,128)(2,1)S(1)}, u32[]{:S(2)}, u32[]{:S(2)}) %collective-permute-start.2) | collective-permute-done | bytes 262176 | tf_op jit(solution)/shard_map/ppermute | solution.py:190
  11.4 0.9 collective-permute-start.6
  12.3 5.8 %collective-permute-done.1.refs_2_ = bf16[32,4096]{1,0:T(8,128)(2,1)S(1)} collective-permute-done((bf16[32,4096]{1,0:T(8,128)(2,1)}, bf16[32,4096]{1,0:T(8,128)(2,1)S(1)}, u32[]{:S(2)}, u32[]{:S(2)}) %collective-permute-start.1) | collective-permute-done | bytes 262176 | tf_op jit(solution)/shard_map/ppermute | solution.py:190
  18.1 0.9 collective-permute-start.5
  19.7 1.3 reduce.1.cols
  22.7 11.2 %shard_map.68 = bf16[16,400,128]{2,1,0:T(8,128)(2,1)} custom-call(s32[384]{0:T(512)} %fusion.3.rowc, s32[384]{0:T(512)} %reduce.1.cols, s32[3]{0:T(128)} %pad_add_fusion.scal, bf16[384,128,128]{2,1,0:T(8,128)(2,1)} %bitcast.11, bf16[16,16,128]{2,1,0:T(8,128)(2,1)} %broadcast_in_dim.68.ids, bf16[32,4096]{1,0:T(8,128)(2,1)} %bitcast.18, ...), custom_call_target="tpu_custom_call" | custom-call | tf_op jit(solution)/shard_map/pallas_call | solution.py:158
  33.9 37.8 %all_to_all.10.recv = bf16[16,400,128]{2,1,0:T(8,128)(2,1)} all-to-all(bf16[16,400,128]{2,1,0:T(8,128)(2,1)} %shard_map.68), channel_id=1, replica_groups=mesh['row'=8,'col'=16] {'col'}, dimensions={0} | all-to-all | bytes 3276800 | tf_op jit(solution)/shard_map/all_to_all | solution.py:215
  71.7 4.4 %shard_map.69 = (bf16[32,4096]{1,0:T(8,128)(2,1)}, bf16[16,384,128]{2,1,0:T(8,128)(2,1)}) custom-call(bf16[16,400,128]{2,1,0:T(8,128)(2,1)} %all_to_all.10.recv), custom_call_target="tpu_custom_call" | custom-call | tf_op jit(solution)/shard_map/pallas_call | solution.py:158
  76.1 3.7 %all-to-all-start.1 = ((bf16[16,384,128]{2,1,0:T(8,128)(2,1)}), bf16[16,384,128]{2,1,0:T(8,128)(2,1)S(1)}, u32[]{:S(2)}, u32[]{:S(2)}) async-start(bf16[16,384,128]{2,1,0:T(8,128)(2,1)} %get-tuple-element.11), calls=%async_computation.1 | async-start | bytes 3145728 | tf_op jit(solution)/shard_map/all_to_all | solution.py:229
  80.5 23.3 %all-to-all-done.1 = bf16[16,384,128]{2,1,0:T(8,128)(2,1)S(1)} async-done(((bf16[16,384,128]{2,1,0:T(8,128)(2,1)}), bf16[16,384,128]{2,1,0:T(8,128)(2,1)S(1)}, u32[]{:S(2)}, u32[]{:S(2)}) %all-to-all-start.1) | async-done | bytes 1572896 | tf_op jit(solution)/shard_map/all_to_all | solution.py:229
  103.7 1.2 copy-done
  104.9 9.9 %shard_map.70 = (f32[4,32,32,128]{3,2,1,0:T(8,128)}, bf16[4,32,32,128]{3,2,1,0:T(8,128)(2,1)}) custom-call(s32[384]{0:T(512)} %copy-done.12, s32[384]{0:T(512)} %fusion.2.colx, s32[3]{0:T(128)} %pad_add_fusion.scal, bf16[384,128,128]{2,1,0:T(8,128)(2,1)} %bitcast.12, bf16[192,32,128]{2,1,0:T(8,128)(2,1)} %bitcast.13), custom_call_target="tpu_custom_call" | custom-call | tf_op jit(solution)/shard_map/pallas_call | solution.py:158
  115.1 2.6 %collective-permute-done.7.got = bf16[4,32,32,128]{3,2,1,0:T(8,128)(2,1)S(1)} collective-permute-done((bf16[4,32,32,128]{3,2,1,0:T(8,128)(2,1)}, bf16[4,32,32,128]{3,2,1,0:T(8,128)(2,1)S(1)}, u32[]{:S(2)}, u32[]{:S(2)}) %collective-permute-start.7) | collective-permute-done | bytes 1048608 | tf_op jit(solution)/shard_map/ppermute | solution.py:193
  117.7 1.0 copy-done.1
  118.7 3.4 %shard_map.71 = (f32[32,32,128]{2,1,0:T(8,128)}, bf16[32,32,128]{2,1,0:T(8,128)(2,1)}, bf16[32,32,128]{2,1,0:T(8,128)(2,1)}, bf16[32,32,128]{2,1,0:T(8,128)(2,1)}) custom-call(s32[3]{0:T(128)} %pad_add_fusion.scal, f32[4,32,32,128]{3,2,1,0:T(8,128)} %get-tuple-element.12.keep, bf16[4,32,32,128]{3,2,1,0:T(8,128)(2,1)} %copy-done.1), custom_call_target="tpu_custom_call" | custom-call | tf_op jit(solution)/shard_map/pallas_call | solution.py:158
  122.0 3.4 %collective-permute-start.8 = (bf16[32,32,128]{2,1,0:T(8,128)(2,1)}, bf16[32,32,128]{2,1,0:T(8,128)(2,1)S(1)}, u32[]{:S(2)}, u32[]{:S(2)}) collective-permute-start(bf16[32,32,128]{2,1,0:T(8,128)(2,1)} %get-tuple-element.15), channel_id=1, source_target_pairs={{0,32},{16,48},{32,64},{48,80},{64,96},{80,112},{96,0},{112,16},{1... | collective-permute-start | bytes 786440 | tf_op jit(solution)/shard_map/ppermute | solution.py:243
  125.9 1.9 %collective-permute-start.10 = (bf16[32,32,128]{2,1,0:T(8,128)(2,1)}, bf16[32,32,128]{2,1,0:T(8,128)(2,1)S(1)}, u32[]{:S(2)}, u32[]{:S(2)}) collective-permute-start(bf16[32,32,128]{2,1,0:T(8,128)(2,1)} %get-tuple-element.17), channel_id=1, source_target_pairs={{0,96},{16,112},{32,0},{48,16},{64,32},{80,48},{96,64},{112,80},{1... | collective-permute-start | bytes 786440 | tf_op jit(solution)/shard_map/ppermute | solution.py:243
  127.8 3.5 %collective-permute-done.8.one = bf16[32,32,128]{2,1,0:T(8,128)(2,1)S(1)} collective-permute-done((bf16[32,32,128]{2,1,0:T(8,128)(2,1)}, bf16[32,32,128]{2,1,0:T(8,128)(2,1)S(1)}, u32[]{:S(2)}, u32[]{:S(2)}) %collective-permute-start.8) | collective-permute-done | bytes 262176 | tf_op jit(solution)/shard_map/ppermute | solution.py:243
  131.3 6.4 %collective-permute-done.9.two = bf16[32,32,128]{2,1,0:T(8,128)(2,1)S(1)} collective-permute-done((bf16[32,32,128]{2,1,0:T(8,128)(2,1)}, bf16[32,32,128]{2,1,0:T(8,128)(2,1)S(1)}, u32[]{:S(2)}, u32[]{:S(2)}) %collective-permute-start.9) | collective-permute-done | bytes 262176 | tf_op jit(solution)/shard_map/ppermute | solution.py:243
  138.6 2.1 %shard_map.72 = bf16[32,4096]{1,0:T(8,128)(2,1)} custom-call(f32[32,32,128]{2,1,0:T(8,128)} %get-tuple-element.14.own, bf16[32,32,128]{2,1,0:T(8,128)(2,1)} %copy-done.9, bf16[32,32,128]{2,1,0:T(8,128)(2,1)} %copy-done.10, bf16[32,32,128]{2,1,0:T(8,128)(2,1)} %copy-done.11), custom_call_target="tpu_custom_call" | custom-call | tf_op jit(solution)/shard_map/pallas_call | solution.py:158
  (54 shorter events, 6.4 us)
Async XLA Ops:
  0.6 21.0 %collective-permute-start.3 = (bf16[32,4096]{1,0:T(8,128)(2,1)}, bf16[32,4096]{1,0:T(8,128)(2,1)S(1)}, u32[]{:S(2)}, u32[]{:S(2)}) collective-permute-start(bf16[32,4096]{1,0:T(8,128)(2,1)} %bitcast.14), channel_id=1, source_target_pairs={{0,16},{16,0},{32,48},{48,32},{64,80},{80,64},{96,112},{112,96},{1... | collective-permute-start | bytes 786440 | tf_op jit(solution)/shard_map/ppermute | solution.py:193
  2.1 9.3 %collective-permute-start.2 = (bf16[32,4096]{1,0:T(8,128)(2,1)}, bf16[32,4096]{1,0:T(8,128)(2,1)S(1)}, u32[]{:S(2)}, u32[]{:S(2)}) collective-permute-start(bf16[32,4096]{1,0:T(8,128)(2,1)} %bitcast.15), channel_id=1, source_target_pairs={{0,32},{16,48},{32,64},{48,80},{64,96},{80,112},{96,0},{112,16},{1... | collective-permute-start | bytes 786440 | tf_op jit(solution)/shard_map/ppermute | solution.py:190
  3.4 14.7 %collective-permute-start.1 = (bf16[32,4096]{1,0:T(8,128)(2,1)}, bf16[32,4096]{1,0:T(8,128)(2,1)S(1)}, u32[]{:S(2)}, u32[]{:S(2)}) collective-permute-start(bf16[32,4096]{1,0:T(8,128)(2,1)} %bitcast.16), channel_id=1, source_target_pairs={{0,64},{16,80},{32,96},{48,112},{64,0},{80,16},{96,32},{112,48},{1... | collective-permute-start | bytes 786440 | tf_op jit(solution)/shard_map/ppermute | solution.py:190
  5.9 13.1 %collective-permute-start = (bf16[32,4096]{1,0:T(8,128)(2,1)}, bf16[32,4096]{1,0:T(8,128)(2,1)S(1)}, u32[]{:S(2)}, u32[]{:S(2)}) collective-permute-start(bf16[32,4096]{1,0:T(8,128)(2,1)} %bitcast.17), channel_id=1, source_target_pairs={{0,96},{16,112},{32,0},{48,16},{64,32},{80,48},{96,64},{112,80},{1... | collective-permute-start | bytes 786440 | tf_op jit(solution)/shard_map/ppermute | solution.py:190
  9.5 24.4 %copy-start.12 = (s32[384]{0:T(512)}, s32[384]{0:T(512)S(1)}, u32[]{:S(2)}) copy-start(s32[384]{0:T(512)S(1)} %select_reduce_fusion.rowc) | copy-start | bytes 4612
  11.4 11.0 %copy-start.3 = (bf16[32,4096]{1,0:T(8,128)(2,1)}, bf16[32,4096]{1,0:T(8,128)(2,1)S(1)}, u32[]{:S(2)}) copy-start(bf16[32,4096]{1,0:T(8,128)(2,1)S(1)} %collective-permute-done.2.refs_3_) | copy-start | bytes 786436
  11.4 10.2 %collective-permute-start.6 = (bf16[32,4096]{1,0:T(8,128)(2,1)S(1)}, bf16[32,4096]{1,0:T(8,128)(2,1)S(1)}, u32[]{:S(2)}, u32[]{:S(2)}) collective-permute-start(bf16[32,4096]{1,0:T(8,128)(2,1)S(1)} %collective-permute-done.2.refs_3_), channel_id=1, source_target_pairs={{0,16},{16,0},{32,48},{48,32},{64,80},{80,64},{96,112},{112,96},{1... | collective-permute-start | bytes 786440 | tf_op jit(solution)/shard_map/ppermute | solution.py:193
  18.1 4.4 %copy-start.4 = (bf16[32,4096]{1,0:T(8,128)(2,1)}, bf16[32,4096]{1,0:T(8,128)(2,1)S(1)}, u32[]{:S(2)}) copy-start(bf16[32,4096]{1,0:T(8,128)(2,1)S(1)} %collective-permute-done.1.refs_2_) | copy-start | bytes 786436
  18.1 3.6 %collective-permute-start.5 = (bf16[32,4096]{1,0:T(8,128)(2,1)S(1)}, bf16[32,4096]{1,0:T(8,128)(2,1)S(1)}, u32[]{:S(2)}, u32[]{:S(2)}) collective-permute-start(bf16[32,4096]{1,0:T(8,128)(2,1)S(1)} %collective-permute-done.1.refs_2_), channel_id=1, source_target_pairs={{0,16},{16,0},{32,48},{48,32},{64,80},{80,64},{96,112},{112,96},{1... | collective-permute-start | bytes 786440 | tf_op jit(solution)/shard_map/ppermute | solution.py:193
  19.0 3.5 %copy-start.5 = (bf16[32,4096]{1,0:T(8,128)(2,1)}, bf16[32,4096]{1,0:T(8,128)(2,1)S(1)}, u32[]{:S(2)}) copy-start(bf16[32,4096]{1,0:T(8,128)(2,1)S(1)} %collective-permute-done.refs_1_) | copy-start | bytes 786436
  19.0 2.7 %collective-permute-start.4 = (bf16[32,4096]{1,0:T(8,128)(2,1)S(1)}, bf16[32,4096]{1,0:T(8,128)(2,1)S(1)}, u32[]{:S(2)}, u32[]{:S(2)}) collective-permute-start(bf16[32,4096]{1,0:T(8,128)(2,1)S(1)} %collective-permute-done.refs_1_), channel_id=1, source_target_pairs={{0,16},{16,0},{32,48},{48,32},{64,80},{80,64},{96,112},{112,96},{1... | collective-permute-start | bytes 786440 | tf_op jit(solution)/shard_map/ppermute | solution.py:193
  21.7 0.8 copy-start.2
  21.7 0.8 copy-start.6
  21.7 0.9 copy-start.7
  21.7 1.0 copy-start.8
  76.1 3.7 %copy-start.13 = (s32[384]{0:T(512)S(1)}, s32[384]{0:T(512)}, u32[]{:S(2)}) copy-start(s32[384]{0:T(512)} %reduce.1.cols) | copy-start | bytes 4612
  76.1 27.6 %all-to-all-start.1 = ((bf16[16,384,128]{2,1,0:T(8,128)(2,1)}), bf16[16,384,128]{2,1,0:T(8,128)(2,1)S(1)}, u32[]{:S(2)}, u32[]{:S(2)}) async-start(bf16[16,384,128]{2,1,0:T(8,128)(2,1)} %get-tuple-element.11), calls=%async_computation.1 | async-start | bytes 3145728 | tf_op jit(solution)/shard_map/all_to_all | solution.py:229
  103.7 1.2 copy-start
  114.8 3.0 %collective-permute-start.7 = (bf16[4,32,32,128]{3,2,1,0:T(8,128)(2,1)}, bf16[4,32,32,128]{3,2,1,0:T(8,128)(2,1)S(1)}, u32[]{:S(2)}, u32[]{:S(2)}) collective-permute-start(bf16[4,32,32,128]{3,2,1,0:T(8,128)(2,1)} %get-tuple-element.13), channel_id=1, source_target_pairs={{0,16},{16,0},{32,48},{48,32},{64,80},{80,64},{96,112},{112,96},{1... | collective-permute-start | bytes 3145736 | tf_op jit(solution)/shard_map/ppermute | solution.py:193
  117.7 1.0 copy-start.1
  122.0 9.3 %collective-permute-start.8 = (bf16[32,32,128]{2,1,0:T(8,128)(2,1)}, bf16[32,32,128]{2,1,0:T(8,128)(2,1)S(1)}, u32[]{:S(2)}, u32[]{:S(2)}) collective-permute-start(bf16[32,32,128]{2,1,0:T(8,128)(2,1)} %get-tuple-element.15), channel_id=1, source_target_pairs={{0,32},{16,48},{32,64},{48,80},{64,96},{80,112},{96,0},{112,16},{1... | collective-permute-start | bytes 786440 | tf_op jit(solution)/shard_map/ppermute | solution.py:243
  125.4 12.3 %collective-permute-start.9 = (bf16[32,32,128]{2,1,0:T(8,128)(2,1)}, bf16[32,32,128]{2,1,0:T(8,128)(2,1)S(1)}, u32[]{:S(2)}, u32[]{:S(2)}) collective-permute-start(bf16[32,32,128]{2,1,0:T(8,128)(2,1)} %get-tuple-element.16), channel_id=1, source_target_pairs={{0,64},{16,80},{32,96},{48,112},{64,0},{80,16},{96,32},{112,48},{1... | collective-permute-start | bytes 786440 | tf_op jit(solution)/shard_map/ppermute | solution.py:243
  125.9 11.9 %collective-permute-start.10 = (bf16[32,32,128]{2,1,0:T(8,128)(2,1)}, bf16[32,32,128]{2,1,0:T(8,128)(2,1)S(1)}, u32[]{:S(2)}, u32[]{:S(2)}) collective-permute-start(bf16[32,32,128]{2,1,0:T(8,128)(2,1)} %get-tuple-element.17), channel_id=1, source_target_pairs={{0,96},{16,112},{32,0},{48,16},{64,32},{80,48},{96,64},{112,80},{1... | collective-permute-start | bytes 786440 | tf_op jit(solution)/shard_map/ppermute | solution.py:243
  131.3 6.5 %copy-start.9 = (bf16[32,32,128]{2,1,0:T(8,128)(2,1)}, bf16[32,32,128]{2,1,0:T(8,128)(2,1)S(1)}, u32[]{:S(2)}) copy-start(bf16[32,32,128]{2,1,0:T(8,128)(2,1)S(1)} %collective-permute-done.8.one) | copy-start | bytes 786436
  (2 other events, 1.5 us)

commit v2 on v1

v2 whole, which is shorter than its diff:
```python
import jax
import jax.numpy as jnp
from jax import lax
from jax.experimental import pallas as pl
from jax.experimental.pallas import tpu as pltpu
from jax.sharding import PartitionSpec as P

TILE = 128
K = 32
SHARE = 32
CAP = 12
N_COL = 16
N_X = 4
RUN_ROWS = CAP * K
PAY_ROWS = RUN_ROWS + 16
N_NAMED = N_COL * CAP
GROUP = 32
CHUNK = 32
NEAR = (0, 1, 3)


def fetch_kernel(scal, tiles, out, sems):
    live = scal[0]

    def copy(chunk):
        span = pl.ds(chunk * CHUNK, CHUNK)
        return pltpu.make_async_copy(tiles.at[span], out.at[span], sems.at[chunk])

    chunks = range(tiles.shape[0] // CHUNK)
    for chunk in chunks:
        @pl.when(chunk * CHUNK < live)
        def _():
            copy(chunk).start()
    for chunk in chunks:
        @pl.when(chunk * CHUNK < live)
        def _():
            copy(chunk).wait()


def code_parts(code):
    return code & 511, (code >> 9) & 255, (code >> 17) & 255, code >> 25


def sweep(count, codes, tiles, left, total, spots, dims):
    def group(g, _):
        base = g * GROUP
        products, places = [], []
        for u in range(GROUP):
            slot, source, place = spots(*code_parts(codes[base + u]))
            places.append(place)
            products.append(
                lax.dot_general(
                    left[source],
                    tiles[slot],
                    (((1,), (dims,)), ((), ())),
                    preferred_element_type=jnp.float32,
                )
            )
        for place, product in zip(places, products):
            total[place] += product
        return 0

    lax.fori_loop(0, (count + GROUP - 1) // GROUP, group, 0)


def clear_blocks(total, count):
    def clear(p, _):
        total[p] = jnp.zeros((K, TILE), jnp.float32)
        return 0

    lax.fori_loop(0, count, clear, 0, unroll=8)


def forward_spots(blocks):
    return lambda slot, row, col, spare: (slot, col & (blocks - 1), row + N_NAMED * spare)


def forward_near_kernel(codes, scal, tiles, *refs):
    pieces, (total, vec) = refs[:6], refs[6:]
    x, core = scal[1], scal[2]
    for i, d in enumerate(NEAR):
        for other in range(2):
            piece = pieces[i + 3 * other]
            first = (((x + d) % N_X) * 2 + (core + other) % 2) * SHARE
            for b in range(SHARE):
                vec[first + b] = piece[:, b * TILE:(b + 1) * TILE]
    clear_blocks(total, N_NAMED)
    sweep(scal[3], codes, tiles, vec, total, forward_spots(2 * N_X * SHARE), 1)


def forward_far_kernel(codes, scal, tiles, ids, here, there, begun, send, total, vec):
    core = scal[2]
    for other, piece in enumerate((here, there)):
        first = ((core + other) % 2) * SHARE
        for b in range(SHARE):
            vec[first + b] = piece[:, b * TILE:(b + 1) * TILE]
    sweep(scal[4], codes, tiles, vec, total, forward_spots(2 * SHARE), 1)

    def pack(c, _):
        for q in range(CAP):
            send[c, q * K:(q + 1) * K] = total[c * CAP + q].astype(jnp.bfloat16)
        send[c, RUN_ROWS:] = ids[c]
        return 0

    lax.fori_loop(0, N_COL, pack, 0)


def reduce_kernel(recv, image, send, total, blocks, wide_ids, ids, sem):
    for c in range(N_COL):
        wide_ids[c:c + 1] = recv[c, RUN_ROWS:][0:1].astype(jnp.float32).astype(jnp.int32)
    copy = pltpu.make_async_copy(wide_ids, ids, sem)
    copy.start()
    for b in range(SHARE):
        total[b] = jnp.zeros((K, TILE), jnp.float32)
    copy.wait()

    def add(c, _):
        for q in range(CAP):
            total[ids[c, q]] += recv[c, q * K:(q + 1) * K].astype(jnp.float32)
        return 0

    lax.fori_loop(0, N_COL, add, 0)
    for b in range(SHARE):
        block = total[b].astype(jnp.bfloat16)
        blocks[b] = block
        image[:, b * TILE:(b + 1) * TILE] = block

    def spread(c, _):
        for q in range(CAP):
            send[c, q * K:(q + 1) * K] = blocks[ids[c, q]]
        return 0

    lax.fori_loop(0, N_COL, spread, 0)


def backward_spots(blocks):
    return lambda slot, row, col, spare: (slot, row, (col & (blocks - 1)) + blocks * spare)


def backward_far_kernel(codes, scal, tiles, recv, keep, give, total):
    core = scal[2]
    clear_blocks(total, 2 * SHARE)
    sweep(scal[4], codes, tiles, recv, total, backward_spots(2 * SHARE), 0)

    def split(b, _):
        keep[b] = total[core * SHARE + b]
        give[b] = total[(1 - core) * SHARE + b].astype(give.dtype)
        return 0

    lax.fori_loop(0, SHARE, split, 0, unroll=4)


def backward_near_kernel(codes, scal, tiles, recv, keep, give, total):
    x, core = scal[1], scal[2]
    clear_blocks(total, 2 * N_X * SHARE)
    sweep(scal[3], codes, tiles, recv, total, backward_spots(2 * N_X * SHARE), 0)

    def split(b, _):
        for i, d in enumerate(NEAR):
            first = ((x + d) % N_X) * 2 * SHARE + b
            keep[i, b] = total[first + core * SHARE]
            give[i, b] = total[first + (1 - core) * SHARE].astype(give.dtype)
        return 0

    lax.fori_loop(0, SHARE, split, 0, unroll=4)


def far_pair_kernel(keep, got, out):
    def step(b, _):
        out[b] = (keep[b] + got[b].astype(jnp.float32)).astype(out.dtype)
        return 0

    lax.fori_loop(0, SHARE, step, 0, unroll=8)


def near_pair_kernel(keep, got, own, one, three):
    def step(b, _):
        for i, out in enumerate((own, one, three)):
            out[b] = (keep[i, b] + got[i, b].astype(jnp.float32)).astype(out.dtype)
        return 0

    lax.fori_loop(0, SHARE, step, 0, unroll=4)


def final_kernel(own, one, two, three, out):
    for b in range(SHARE):
        total = own[b] + one[b].astype(jnp.float32)
        total = total + two[b].astype(jnp.float32) + three[b].astype(jnp.float32)
        out[:, b * TILE:(b + 1) * TILE] = total.astype(jnp.bfloat16)


def call(kernel, outs, scalars, arrays, scratch=(), limit=8, hbm=False, aliases=None):
    spec_vmem = pl.BlockSpec(memory_space=pltpu.VMEM)
    spec_smem = pl.BlockSpec(memory_space=pltpu.SMEM)
    spec_hbm = pl.BlockSpec(memory_space=pltpu.HBM)
    specs = [spec_smem] * len(scalars) + [spec_hbm if hbm else spec_vmem] * len(arrays)
    single = not isinstance(outs, (list, tuple))
    return pl.pallas_call(
        kernel,
        out_shape=outs,
        in_specs=specs,
        out_specs=spec_vmem if single else [spec_vmem] * len(outs),
        scratch_shapes=list(scratch),
        input_output_aliases=aliases or {},
        compiler_params=pltpu.CompilerParams(vmem_limit_bytes=limit << 20),
    )(*scalars, *arrays)


def slot_lists(rowc, cols, live, x):
    slot = jnp.arange(rowc.shape[0], dtype=jnp.int32)
    code = slot | (rowc << 9) | (cols << 17)
    far = (((cols >> 6) - x) & (N_X - 1)) == 2
    member = jnp.stack([(slot < live) & ~far, (slot < live) & far])
    earlier = slot[:, None] < slot[None, :]
    place = jnp.sum(jnp.where(member[:, :, None] & earlier[None], 1, 0), axis=1)
    match = member[:, :, None] & (place[:, :, None] == slot[None, None, :])
    packed = jnp.sum(jnp.where(match, code[None, :, None], 0), axis=1)
    counts = jnp.sum(member.astype(jnp.int32), axis=1)
    return jnp.where(slot[None, :] < counts[:, None], packed, 1 << 25), counts


def named_rows(rows):
    hits = rows[:, None] == jnp.arange(N_COL * SHARE, dtype=jnp.int32)[None, :]
    present = jnp.any(hits, axis=0).astype(jnp.int32).reshape(N_COL, SHARE)
    place = jnp.arange(SHARE, dtype=jnp.int32)
    rank = jnp.sum(jnp.where(place[:, None] < place[None, :], present[:, :, None], 0), axis=1)
    match = (rank[:, None, :] == jnp.arange(CAP, dtype=jnp.int32)[None, :, None]) & (present[:, None, :] > 0)
    ids = jnp.sum(jnp.where(match, place[None, None, :], 0), axis=2)
    position = (rank + CAP * jnp.arange(N_COL, dtype=jnp.int32)[:, None]).reshape(-1)
    rowc = jnp.sum(jnp.where(hits, position[None, :], 0), axis=1)
    return ids, rowc


def per_device(tiles, tile_row, tile_col, tile_count, vectors):
    bf16, f32 = jnp.bfloat16, jnp.float32
    shape = jax.ShapeDtypeStruct
    local = tiles[0, 0]
    rows, cols, live = tile_row[0, 0], tile_col[0, 0], tile_count[0, 0]
    row_at = lax.axis_index("row")
    x, core = row_at // 2, row_at % 2

    def along_x(value, d):
        return lax.ppermute(value, "row", [(i, (i + 2 * d) % 8) for i in range(8)])

    def swap_core(value):
        return lax.ppermute(value, "row", [(i, i ^ 1) for i in range(8)])

    mine = vectors.reshape(K, SHARE * TILE)
    near = [mine, along_x(mine, -1), along_x(mine, 1)]
    far = along_x(mine, 2)
    first = jnp.stack([live]).astype(jnp.int32)
    held = call(
        fetch_kernel, shape(local.shape, bf16), [first],
        [pltpu.with_memory_space_constraint(local, pltpu.HBM)],
        [pltpu.SemaphoreType.DMA((local.shape[0] // CHUNK,))], limit=1, hbm=True,
    )

    ids, rowc = named_rows(rows)
    codes, counts = slot_lists(rowc, cols, live, x)
    scal = jnp.stack([live, x, core, counts[0], counts[1]]).astype(jnp.int32)
    near_codes, far_codes = codes[0], codes[1]
    lanes = jnp.pad(ids, ((0, 0), (0, TILE - CAP))).astype(bf16)
    id_rows = jnp.broadcast_to(lanes[:, None, :], (N_COL, 16, TILE))
    near, near_codes, far_codes, id_rows, scal, held = lax.optimization_barrier(
        (near, near_codes, far_codes, id_rows, scal, held)
    )

    begun = call(
        forward_near_kernel,
        shape((N_NAMED + 1, K, TILE), f32),
        [near_codes, scal],
        [held] + near + [swap_core(v) for v in near],
        [pltpu.VMEM((2 * N_X * SHARE, K, TILE), bf16)],
    )
    far, begun = lax.optimization_barrier((far, begun))
    send, _ = call(
        forward_far_kernel,
        [shape((N_COL, PAY_ROWS, TILE), bf16), shape((N_NAMED + 1, K, TILE), f32)],
        [far_codes, scal],
        [held, id_rows, far, swap_core(far), begun],
        [pltpu.VMEM((2 * SHARE, K, TILE), bf16)],
        aliases={6: 1},
    )
    recv = lax.all_to_all(send, "col", 0, 0, tiled=True)
    image, spread = call(
        reduce_kernel,
        [shape((K, SHARE * TILE), bf16), shape((N_COL, RUN_ROWS, TILE), bf16)],
        [],
        [recv],
        [
            pltpu.VMEM((SHARE, K, TILE), f32),
            pltpu.VMEM((SHARE, K, TILE), bf16),
            pltpu.VMEM((N_COL, TILE), jnp.int32),
            pltpu.SMEM((N_COL, TILE), jnp.int32),
            pltpu.SemaphoreType.DMA,
        ],
    )
    named = lax.all_to_all(spread, "col", 0, 0, tiled=True).reshape(N_NAMED, K, TILE)

    block = (SHARE, K, TILE)
    keep, give = call(
        backward_far_kernel,
        [shape(block, f32), shape(block, bf16)],
        [far_codes, scal],
        [held, named],
        [pltpu.VMEM((2 * SHARE + 1, K, TILE), f32)],
    )
    away = call(far_pair_kernel, shape(block, bf16), [], [keep, swap_core(give)])
    away, named = lax.optimization_barrier((away, named))
    two = along_x(away, 2)
    keep, give = call(
        backward_near_kernel,
        [shape((3,) + block, f32), shape((3,) + block, bf16)],
        [near_codes, scal],
        [held, named],
        [pltpu.VMEM((2 * N_X * SHARE + 1, K, TILE), f32)],
    )
    own, one, three = call(
        near_pair_kernel,
        [shape(block, f32), shape(block, bf16), shape(block, bf16)],
        [],
        [keep, swap_core(give)],
    )
    one, three = along_x(one, 1), along_x(three, -1)
    back = call(final_kernel, shape((K, SHARE * TILE), bf16), [], [own, one, two, three])
    return image, back.reshape(vectors.shape)


def solution(mesh):
    return jax.shard_map(
        per_device,
        mesh=mesh,
        in_specs=(
            P("row", "col", None, None, None),
            P("row", "col", None),
            P("row", "col", None),
            P("row", "col"),
            P(None, "row", "col", None),
        ),
        out_specs=(P(None, ("row", "col")), P(None, "row", "col", None)),
        check_vma=False,
    )
```

time: 143 us -> 113 us (0.79); the launches traced: 141 us -> 113 us
  waiting for transfers between devices: 43.5 us -> 17.3 us
  blocking collectives: 37.8 us -> 55.6 us
  Pallas kernels: 30.9 us -> 21.8 us
  starting transfers between devices: 18.1 us -> 12.6 us
  local copies, waits for them, and re-layouts: 4.19 us -> 0.29 us
    all_to_all x0 -> x1, blocking collectives: none -> 24.6 us  [per_device(): lax.all_to_all(spread, 'col', 0, 0, tiled=True).reshape(N_NAMED, K, TILE)]
    all_to_all x1 -> x0, waiting for transfers between devices: 23.3 us -> none  [per_device(): lax.all_to_all(spread, 'col', 0, 0, tiled=True).reshape(N_NAMED, K, TILE)]
    pallas_call x5 -> x9, Pallas kernels: 30.9 us -> 21.8 us  [call(): pl.pallas_call(kernel, out_shape=outs, in_specs=specs, out_specs=spec_vme...]
    all_to_all x1, blocking collectives: 37.8 us -> 31 us  [per_device(): recv = lax.all_to_all(send, 'col', 0, 0, tiled=True)]
    ppermute x6, waiting for transfers between devices: 17.7 us -> 12.7 us  [along_x(): return lax.ppermute(value, 'row', [(i, (i + 2 * d) % 8) for i in range(8)])]
    all_to_all x1 -> x0, starting transfers between devices: 3.72 us -> none  [per_device(): lax.all_to_all(spread, 'col', 0, 0, tiled=True).reshape(N_NAMED, K, TILE)]
    ppermute x6, starting transfers between devices: 10.7 us -> 7.24 us  [along_x(): return lax.ppermute(value, 'row', [(i, (i + 2 * d) % 8) for i in range(8)])]
    unnamed x29 -> x3, local copies, waits for them, and re-layouts: 3.29 us -> 0.1 us
  transfers between devices with their start and end apart: 12 -> 12, of which waited for: 6 -> 7; matrix products, arithmetic and copies ran while one was open for 4% -> 4% of each run, Pallas kernels for 0% -> 9%
where the time goes in v2:
time: 113 us
  blocking collectives  55.6 us (49%)
  Pallas kernels  21.8 us (19%)
  waiting for transfers between devices  17.3 us (15%)
  starting transfers between devices  12.6 us (11%)
  other arithmetic  3.96 us (4%)
  between operations  1.44 us (1%)
    all_to_all x1, blocking collectives, per_device(): recv = lax.all_to_all(send, 'col', 0, 0, tiled=True)  31 us
    all_to_all x1, blocking collectives, per_device(): lax.all_to_all(spread, 'col', 0, 0, tiled=True).reshape(N_NAMED, K, TILE)  24.6 us
    pallas_call x9, Pallas kernels, call(): pl.pallas_call(kernel, out_shape=outs, in_specs=specs, out_specs=spec_vme...  21.8 us
    ppermute x6, waiting for transfers between devices, along_x(): return lax.ppermute(value, 'row', [(i, (i + 2 * d) % 8) for i in range(8)])  12.7 us
    ppermute x6, starting transfers between devices, along_x(): return lax.ppermute(value, 'row', [(i, (i + 2 * d) % 8) for i in range(8)])  7.24 us
    ppermute x6, starting transfers between devices, swap_core(): return lax.ppermute(value, 'row', [(i, i ^ 1) for i in range(8)])  5.36 us
    ppermute x6, waiting for transfers between devices, swap_core(): return lax.ppermute(value, 'row', [(i, i ^ 1) for i in range(8)])  4.6 us
  transfers between devices with their start and end apart: 12, of which 7 were waited for; matrix products, arithmetic and copies ran while one was open for 4% of the time, Pallas kernels for 9%

profile of v2, /device:TPU:1, one launch (start us, length us, event | category | flops | bytes accessed | tf_op | source)
XLA Modules:
  0.0 113.0 jit_solution(11178591459471387027)
XLA Ops:
  0.6 2.1 %collective-permute-start.1 = (bf16[32,4096]{1,0:T(8,128)(2,1)}, bf16[32,4096]{1,0:T(8,128)(2,1)S(1)}, u32[]{:S(2)}, u32[]{:S(2)}) collective-permute-start(bf16[32,4096]{1,0:T(8,128)(2,1)} %bitcast.18), channel_id=1, source_target_pairs={{0,32},{16,48},{32,64},{48,80},{64,96},{80,112},{96,0},{112,16},{1... | collective-permute-start | bytes 786440 | tf_op jit(solution)/shard_map/ppermute | solution.py:243
  2.7 1.4 %collective-permute-start = (bf16[32,4096]{1,0:T(8,128)(2,1)}, bf16[32,4096]{1,0:T(8,128)(2,1)S(1)}, u32[]{:S(2)}, u32[]{:S(2)}) collective-permute-start(bf16[32,4096]{1,0:T(8,128)(2,1)} %bitcast.19), channel_id=1, source_target_pairs={{0,96},{16,112},{32,0},{48,16},{64,32},{80,48},{96,64},{112,80},{1... | collective-permute-start | bytes 786440 | tf_op jit(solution)/shard_map/ppermute | solution.py:243
  4.8 0.7 reduce
  5.7 0.7 shift-left_reduce_fusion
  8.9 3.8 %shard_map.68.tiles = bf16[384,128,128]{2,1,0:T(8,128)(2,1)S(1)} custom-call(s32[1]{0:T(128)} %bitcast.15.scal, bf16[384,128,128]{2,1,0:T(8,128)(2,1)} %bitcast.23), custom_call_target="tpu_custom_call" | custom-call | tf_op jit(solution)/shard_map/pallas_call | solution.py:198
  12.9 1.3 %collective-permute-start.3 = (bf16[32,4096]{1,0:T(8,128)(2,1)S(1)}, bf16[32,4096]{1,0:T(8,128)(2,1)S(1)}, u32[]{:S(2)}, u32[]{:S(2)}) collective-permute-start(bf16[32,4096]{1,0:T(8,128)(2,1)S(1)} %bitcast.20), channel_id=1, source_target_pairs={{0,16},{16,0},{32,48},{48,32},{64,80},{80,64},{96,112},{112,96},{1... | collective-permute-start | bytes 786440 | tf_op jit(solution)/shard_map/ppermute | solution.py:246
  14.8 1.0 collective-permute-start.2
  16.2 5.7 %shard_map.69.begun = f32[193,32,128]{2,1,0:T(8,128)S(1)} custom-call(s32[384]{0:T(512)S(1)} %get-tuple-element.28.codes, s32[5]{0:T(128)S(1)} %pad_add_fusion.1.scal, bf16[384,128,128]{2,1,0:T(8,128)(2,1)S(1)} %shard_map.68.tiles, bf16[32,4096]{1,0:T(8,128)(2,1)S(1)} %bitcast.22, bf16[32,4096]{1,0:T(8,128)(2,1)S(1)} %collective-permute-done.refs_1_, ...), custom_call_target="tpu_custom_call" | custom-call | tf_op jit(solution)/shard_map/pallas_call | solution.py:198
  21.9 2.2 %collective-permute-done.2.here = bf16[32,4096]{1,0:T(8,128)(2,1)S(1)} collective-permute-done((bf16[32,4096]{1,0:T(8,128)(2,1)S(1)}, bf16[32,4096]{1,0:T(8,128)(2,1)S(1)}, u32[]{:S(2)}, u32[]{:S(2)}) %collective-permute-start.2) | collective-permute-done | bytes 262176 | tf_op jit(solution)/shard_map/ppermute | solution.py:243
  24.2 0.9 collective-permute-start.6
  25.0 1.2 %collective-permute-done.6.there = bf16[32,4096]{1,0:T(8,128)(2,1)S(1)} collective-permute-done((bf16[32,4096]{1,0:T(8,128)(2,1)S(1)}, bf16[32,4096]{1,0:T(8,128)(2,1)S(1)}, u32[]{:S(2)}, u32[]{:S(2)}) %collective-permute-start.6) | collective-permute-done | bytes 262176 | tf_op jit(solution)/shard_map/ppermute | solution.py:246
  26.2 2.9 %shard_map.70 = (bf16[16,400,128]{2,1,0:T(8,128)(2,1)S(1)}, f32[193,32,128]{2,1,0:T(8,128)S(1)}) custom-call(s32[384]{0:T(512)S(1)} %get-tuple-element.24.codes, s32[5]{0:T(128)S(1)} %pad_add_fusion.1.scal, bf16[384,128,128]{2,1,0:T(8,128)(2,1)S(1)} %shard_map.68.tiles, ...), custom_call_target="tpu_custom_call", output_to_operand_aliasing={{1}: (6, {})} | custom-call | tf_op jit(solution)/shard_map/pallas_call | solution.py:198
  29.1 31.0 %all_to_all.10.recv = bf16[16,400,128]{2,1,0:T(8,128)(2,1)S(1)} all-to-all(bf16[16,400,128]{2,1,0:T(8,128)(2,1)S(1)} %get-tuple-element.34), channel_id=1, replica_groups=mesh['row'=8,'col'=16] {'col'}, dimensions={0} | all-to-all | bytes 3276800 | tf_op jit(solution)/shard_map/all_to_all | solution.py:284
  60.1 2.4 %shard_map.71 = (bf16[32,4096]{1,0:T(8,128)(2,1)}, bf16[16,384,128]{2,1,0:T(8,128)(2,1)S(1)}) custom-call(bf16[16,400,128]{2,1,0:T(8,128)(2,1)S(1)} %all_to_all.10.recv), custom_call_target="tpu_custom_call" | custom-call | tf_op jit(solution)/shard_map/pallas_call | solution.py:198
  62.5 24.6 %all_to_all.11 = bf16[16,384,128]{2,1,0:T(8,128)(2,1)S(1)} all-to-all(bf16[16,384,128]{2,1,0:T(8,128)(2,1)S(1)} %get-tuple-element.36), channel_id=1, replica_groups=mesh['row'=8,'col'=16] {'col'}, dimensions={0} | all-to-all | bytes 3145728 | tf_op jit(solution)/shard_map/all_to_all | solution.py:298
  87.1 2.0 %shard_map.72 = (f32[32,32,128]{2,1,0:T(8,128)S(1)}, bf16[32,32,128]{2,1,0:T(8,128)(2,1)S(1)}) custom-call(s32[384]{0:T(512)S(1)} %get-tuple-element.24.codes, s32[5]{0:T(128)S(1)} %pad_add_fusion.1.scal, bf16[384,128,128]{2,1,0:T(8,128)(2,1)S(1)} %shard_map.68.tiles, bf16[192,32,128]{2,1,0:T(8,128)(2,1)S(1)} %bitcast.16), custom_call_target="tpu_custom_call" | custom-call | tf_op jit(solution)/shard_map/pallas_call | solution.py:198
  89.1 2.2 %collective-permute-start.7 = (bf16[32,32,128]{2,1,0:T(8,128)(2,1)S(1)}, bf16[32,32,128]{2,1,0:T(8,128)(2,1)S(1)}, u32[]{:S(2)}, u32[]{:S(2)}) collective-permute-start(bf16[32,32,128]{2,1,0:T(8,128)(2,1)S(1)} %get-tuple-element.38), channel_id=1, source_target_pairs={{0,16},{16,0},{32,48},{48,32},{64,80},{80,64},{96,112},{112,96},{1... | collective-permute-start | bytes 786440 | tf_op jit(solution)/shard_map/ppermute | solution.py:246
  91.2 1.2 %collective-permute-done.7.got = bf16[32,32,128]{2,1,0:T(8,128)(2,1)S(1)} collective-permute-done((bf16[32,32,128]{2,1,0:T(8,128)(2,1)S(1)}, bf16[32,32,128]{2,1,0:T(8,128)(2,1)S(1)}, u32[]{:S(2)}, u32[]{:S(2)}) %collective-permute-start.7) | collective-permute-done | bytes 262176 | tf_op jit(solution)/shard_map/ppermute | solution.py:246
  92.5 3.9 %shard_map.74 = (f32[3,32,32,128]{3,2,1,0:T(8,128)S(1)}, bf16[3,32,32,128]{3,2,1,0:T(8,128)(2,1)S(1)}) custom-call(s32[384]{0:T(512)S(1)} %get-tuple-element.28.codes, s32[5]{0:T(128)S(1)} %pad_add_fusion.1.scal, bf16[384,128,128]{2,1,0:T(8,128)(2,1)S(1)} %shard_map.68.tiles, bf16[192,32,128]{2,1,0:T(8,128)(2,1)S(1)} %bitcast.17), custom_call_target="tpu_custom_call" | custom-call | tf_op jit(solution)/shard_map/pallas_call | solution.py:198
  96.8 1.9 %collective-permute-done.8.got = bf16[3,32,32,128]{3,2,1,0:T(8,128)(2,1)S(1)} collective-permute-done((bf16[3,32,32,128]{3,2,1,0:T(8,128)(2,1)S(1)}, bf16[3,32,32,128]{3,2,1,0:T(8,128)(2,1)S(1)}, u32[]{:S(2)}, u32[]{:S(2)}) %collective-permute-start.8) | collective-permute-done | bytes 786464 | tf_op jit(solution)/shard_map/ppermute | solution.py:246
  99.5 2.2 %collective-permute-start.11 = (bf16[32,32,128]{2,1,0:T(8,128)(2,1)S(1)}, bf16[32,32,128]{2,1,0:T(8,128)(2,1)S(1)}, u32[]{:S(2)}, u32[]{:S(2)}) collective-permute-start(bf16[32,32,128]{2,1,0:T(8,128)(2,1)S(1)} %get-tuple-element.45), channel_id=1, source_target_pairs={{0,96},{16,112},{32,0},{48,16},{64,32},{80,48},{96,64},{112,80},{1... | collective-permute-start | bytes 786440 | tf_op jit(solution)/shard_map/ppermute | solution.py:243
  101.7 4.4 %collective-permute-done.10.two = bf16[32,32,128]{2,1,0:T(8,128)(2,1)S(1)} collective-permute-done((bf16[32,32,128]{2,1,0:T(8,128)(2,1)S(1)}, bf16[32,32,128]{2,1,0:T(8,128)(2,1)S(1)}, u32[]{:S(2)}, u32[]{:S(2)}) %collective-permute-start.10) | collective-permute-done | bytes 262176 | tf_op jit(solution)/shard_map/ppermute | solution.py:243
  106.2 6.1 %collective-permute-done.9.one = bf16[32,32,128]{2,1,0:T(8,128)(2,1)S(1)} collective-permute-done((bf16[32,32,128]{2,1,0:T(8,128)(2,1)S(1)}, bf16[32,32,128]{2,1,0:T(8,128)(2,1)S(1)}, u32[]{:S(2)}, u32[]{:S(2)}) %collective-permute-start.9) | collective-permute-done | bytes 262176 | tf_op jit(solution)/shard_map/ppermute | solution.py:243
  112.2 0.8 shard_map.76
  (39 shorter events, 5.0 us)
Async XLA Ops:
  0.6 12.3 %collective-permute-start.1 = (bf16[32,4096]{1,0:T(8,128)(2,1)}, bf16[32,4096]{1,0:T(8,128)(2,1)S(1)}, u32[]{:S(2)}, u32[]{:S(2)}) collective-permute-start(bf16[32,4096]{1,0:T(8,128)(2,1)} %bitcast.18), channel_id=1, source_target_pairs={{0,32},{16,48},{32,64},{48,80},{64,96},{80,112},{96,0},{112,16},{1... | collective-permute-start | bytes 786440 | tf_op jit(solution)/shard_map/ppermute | solution.py:243
  2.7 10.2 %collective-permute-start = (bf16[32,4096]{1,0:T(8,128)(2,1)}, bf16[32,4096]{1,0:T(8,128)(2,1)S(1)}, u32[]{:S(2)}, u32[]{:S(2)}) collective-permute-start(bf16[32,4096]{1,0:T(8,128)(2,1)} %bitcast.19), channel_id=1, source_target_pairs={{0,96},{16,112},{32,0},{48,16},{64,32},{80,48},{96,64},{112,80},{1... | collective-permute-start | bytes 786440 | tf_op jit(solution)/shard_map/ppermute | solution.py:243
  8.9 4.0 %copy-start = (bf16[32,1,1,4096]{3,0,2,1:T(8,128)(2,1)S(1)}, bf16[32,1,1,4096]{3,0,2,1:T(8,128)(2,1)}, u32[]{:S(2)}) copy-start(bf16[32,1,1,4096]{3,0,2,1:T(8,128)(2,1)} %param.9) | copy-start | bytes 786436
  12.9 2.9 %collective-permute-start.3 = (bf16[32,4096]{1,0:T(8,128)(2,1)S(1)}, bf16[32,4096]{1,0:T(8,128)(2,1)S(1)}, u32[]{:S(2)}, u32[]{:S(2)}) collective-permute-start(bf16[32,4096]{1,0:T(8,128)(2,1)S(1)} %bitcast.20), channel_id=1, source_target_pairs={{0,16},{16,0},{32,48},{48,32},{64,80},{80,64},{96,112},{112,96},{1... | collective-permute-start | bytes 786440 | tf_op jit(solution)/shard_map/ppermute | solution.py:246
  14.3 1.6 %collective-permute-start.4 = (bf16[32,4096]{1,0:T(8,128)(2,1)S(1)}, bf16[32,4096]{1,0:T(8,128)(2,1)S(1)}, u32[]{:S(2)}, u32[]{:S(2)}) collective-permute-start(bf16[32,4096]{1,0:T(8,128)(2,1)S(1)} %collective-permute-done.refs_1_), channel_id=1, source_target_pairs={{0,16},{16,0},{32,48},{48,32},{64,80},{80,64},{96,112},{112,96},{1... | collective-permute-start | bytes 786440 | tf_op jit(solution)/shard_map/ppermute | solution.py:246
  14.4 1.8 %collective-permute-start.5 = (bf16[32,4096]{1,0:T(8,128)(2,1)S(1)}, bf16[32,4096]{1,0:T(8,128)(2,1)S(1)}, u32[]{:S(2)}, u32[]{:S(2)}) collective-permute-start(bf16[32,4096]{1,0:T(8,128)(2,1)S(1)} %collective-permute-done.1.refs_2_), channel_id=1, source_target_pairs={{0,16},{16,0},{32,48},{48,32},{64,80},{80,64},{96,112},{112,96},{1... | collective-permute-start | bytes 786440 | tf_op jit(solution)/shard_map/ppermute | solution.py:246
  14.8 9.4 %collective-permute-start.2 = (bf16[32,4096]{1,0:T(8,128)(2,1)S(1)}, bf16[32,4096]{1,0:T(8,128)(2,1)S(1)}, u32[]{:S(2)}, u32[]{:S(2)}) collective-permute-start(bf16[32,4096]{1,0:T(8,128)(2,1)S(1)} %bitcast.21), channel_id=1, source_target_pairs={{0,64},{16,80},{32,96},{48,112},{64,0},{80,16},{96,32},{112,48},{1... | collective-permute-start | bytes 786440 | tf_op jit(solution)/shard_map/ppermute | solution.py:243
  24.2 2.0 %collective-permute-start.6 = (bf16[32,4096]{1,0:T(8,128)(2,1)S(1)}, bf16[32,4096]{1,0:T(8,128)(2,1)S(1)}, u32[]{:S(2)}, u32[]{:S(2)}) collective-permute-start(bf16[32,4096]{1,0:T(8,128)(2,1)S(1)} %collective-permute-done.2.here), channel_id=1, source_target_pairs={{0,16},{16,0},{32,48},{48,32},{64,80},{80,64},{96,112},{112,96},{1... | collective-permute-start | bytes 786440 | tf_op jit(solution)/shard_map/ppermute | solution.py:246
  89.1 3.3 %collective-permute-start.7 = (bf16[32,32,128]{2,1,0:T(8,128)(2,1)S(1)}, bf16[32,32,128]{2,1,0:T(8,128)(2,1)S(1)}, u32[]{:S(2)}, u32[]{:S(2)}) collective-permute-start(bf16[32,32,128]{2,1,0:T(8,128)(2,1)S(1)} %get-tuple-element.38), channel_id=1, source_target_pairs={{0,16},{16,0},{32,48},{48,32},{64,80},{80,64},{96,112},{112,96},{1... | collective-permute-start | bytes 786440 | tf_op jit(solution)/shard_map/ppermute | solution.py:246
  96.4 2.4 %collective-permute-start.8 = (bf16[3,32,32,128]{3,2,1,0:T(8,128)(2,1)S(1)}, bf16[3,32,32,128]{3,2,1,0:T(8,128)(2,1)S(1)}, u32[]{:S(2)}, u32[]{:S(2)}) collective-permute-start(bf16[3,32,32,128]{3,2,1,0:T(8,128)(2,1)S(1)} %get-tuple-element.41), channel_id=1, source_target_pairs={{0,16},{16,0},{32,48},{48,32},{64,80},{80,64},{96,112},{112,96},{1... | collective-permute-start | bytes 2359304 | tf_op jit(solution)/shard_map/ppermute | solution.py:246
  96.8 9.3 %collective-permute-start.10 = (bf16[32,32,128]{2,1,0:T(8,128)(2,1)S(1)}, bf16[32,32,128]{2,1,0:T(8,128)(2,1)S(1)}, u32[]{:S(2)}, u32[]{:S(2)}) collective-permute-start(bf16[32,32,128]{2,1,0:T(8,128)(2,1)S(1)} %shard_map.73), channel_id=1, source_target_pairs={{0,64},{16,80},{32,96},{48,112},{64,0},{80,16},{96,32},{112,48},{1... | collective-permute-start | bytes 786440 | tf_op jit(solution)/shard_map/ppermute | solution.py:243
  99.0 13.2 %collective-permute-start.9 = (bf16[32,32,128]{2,1,0:T(8,128)(2,1)S(1)}, bf16[32,32,128]{2,1,0:T(8,128)(2,1)S(1)}, u32[]{:S(2)}, u32[]{:S(2)}) collective-permute-start(bf16[32,32,128]{2,1,0:T(8,128)(2,1)S(1)} %get-tuple-element.43), channel_id=1, source_target_pairs={{0,32},{16,48},{32,64},{48,80},{64,96},{80,112},{96,0},{112,16},{1... | collective-permute-start | bytes 786440 | tf_op jit(solution)/shard_map/ppermute | solution.py:243
  99.5 12.7 %collective-permute-start.11 = (bf16[32,32,128]{2,1,0:T(8,128)(2,1)S(1)}, bf16[32,32,128]{2,1,0:T(8,128)(2,1)S(1)}, u32[]{:S(2)}, u32[]{:S(2)}) collective-permute-start(bf16[32,32,128]{2,1,0:T(8,128)(2,1)S(1)} %get-tuple-element.45), channel_id=1, source_target_pairs={{0,96},{16,112},{32,0},{48,16},{64,32},{80,48},{96,64},{112,80},{1... | collective-permute-start | bytes 786440 | tf_op jit(solution)/shard_map/ppermute | solution.py:243

commit v3 on v2

--- a/solution.py
+++ b/solution.py
@@ -17,33 +17,24 @@
 GROUP = 32
 CHUNK = 32
 NEAR = (0, 1, 3)
-
-
-def fetch_kernel(scal, tiles, out, sems):
-    live = scal[0]
-
-    def copy(chunk):
-        span = pl.ds(chunk * CHUNK, CHUNK)
-        return pltpu.make_async_copy(tiles.at[span], out.at[span], sems.at[chunk])
-
-    chunks = range(tiles.shape[0] // CHUNK)
-    for chunk in chunks:
-        @pl.when(chunk * CHUNK < live)
-        def _():
-            copy(chunk).start()
-    for chunk in chunks:
-        @pl.when(chunk * CHUNK < live)
-        def _():
-            copy(chunk).wait()
+PARTS = 2
+LONG = pl.CostEstimate(flops=1 << 36, transcendentals=0, bytes_accessed=1 << 26)
+
+
+def tile_copy(tiles, held, sems, chunk):
+    span = pl.ds(pl.multiple_of(chunk * CHUNK, CHUNK), CHUNK)
+    return pltpu.make_async_copy(tiles.at[span], held.at[span], sems.at[chunk])
 
 
 def code_parts(code):
     return code & 511, (code >> 9) & 255, (code >> 17) & 255, code >> 25
 
 
-def sweep(count, codes, tiles, left, total, spots, dims):
-    def group(g, _):
+def sweep(count, codes, tiles, left, total, spots, dims, ready=None):
+    def group(g, seen):
         base = g * GROUP
+        if ready is not None:
+            seen = ready(seen, (codes[jnp.minimum(base + GROUP, count) - 1] & 511) // CHUNK + 1)
         products, places = [], []
         for u in range(GROUP):
             slot, source, place = spots(*code_parts(codes[base + u]))
@@ -58,9 +49,9 @@
             )
         for place, product in zip(places, products):
             total[place] += product
-        return 0
-
-    lax.fori_loop(0, (count + GROUP - 1) // GROUP, group, 0)
+        return seen
+
+    return lax.fori_loop(0, (count + GROUP - 1) // GROUP, group, 0)
 
 
 def clear_blocks(total, count):
@@ -76,8 +67,23 @@
 
 
 def forward_near_kernel(codes, scal, tiles, *refs):
-    pieces, (total, vec) = refs[:6], refs[6:]
-    x, core = scal[1], scal[2]
+    pieces, (total, held, vec, sems) = refs[:6], refs[6:]
+    live, x, core = scal[0], scal[1], scal[2]
+    chunks = (live + CHUNK - 1) // CHUNK
+
+    def start(chunk, _):
+        tile_copy(tiles, held, sems, chunk).start()
+        return 0
+
+    def wait(chunk, _):
+        tile_copy(tiles, held, sems, chunk).wait()
+        return 0
+
+    def ready(seen, need):
+        lax.fori_loop(seen, need, wait, 0)
+        return jnp.maximum(seen, need)
+
+    lax.fori_loop(0, chunks, start, 0)
     for i, d in enumerate(NEAR):
         for other in range(2):
             piece = pieces[i + 3 * other]
@@ -85,7 +91,8 @@
             for b in range(SHARE):
                 vec[first + b] = piece[:, b * TILE:(b + 1) * TILE]
     clear_blocks(total, N_NAMED)
-    sweep(scal[3], codes, tiles, vec, total, forward_spots(2 * N_X * SHARE), 1)
+    seen = sweep(scal[3], codes, held, vec, total, forward_spots(2 * N_X * SHARE), 1, ready)
+    lax.fori_loop(seen, chunks, wait, 0)
 
 
 def forward_far_kernel(codes, scal, tiles, ids, here, there, begun, send, total, vec):
@@ -137,22 +144,10 @@
     return lambda slot, row, col, spare: (slot, row, (col & (blocks - 1)) + blocks * spare)
 
 
-def backward_far_kernel(codes, scal, tiles, recv, keep, give, total):
-    core = scal[2]
-    clear_blocks(total, 2 * SHARE)
-    sweep(scal[4], codes, tiles, recv, total, backward_spots(2 * SHARE), 0)
-
-    def split(b, _):
-        keep[b] = total[core * SHARE + b]
-        give[b] = total[(1 - core) * SHARE + b].astype(give.dtype)
-        return 0
-
-    lax.fori_loop(0, SHARE, split, 0, unroll=4)
-
-
 def backward_near_kernel(codes, scal, tiles, recv, keep, give, total):
     x, core = scal[1], scal[2]
-    clear_blocks(total, 2 * N_X * SHARE)
+    for d in NEAR:
+        clear_blocks(total.at[pl.ds(((x + d) % N_X) * 2 * SHARE, 2 * SHARE)], 2 * SHARE)
     sweep(scal[3], codes, tiles, recv, total, backward_spots(2 * N_X * SHARE), 0)
 
     def split(b, _):
@@ -165,12 +160,20 @@
     lax.fori_loop(0, SHARE, split, 0, unroll=4)
 
 
-def far_pair_kernel(keep, got, out):
-    def step(b, _):
-        out[b] = (keep[b] + got[b].astype(jnp.float32)).astype(out.dtype)
-        return 0
-
-    lax.fori_loop(0, SHARE, step, 0, unroll=8)
+def backward_far_kernel(codes, scal, tiles, recv, keep, *rest):
+    gives, total = rest[:-1], rest[-1]
+    core = scal[2]
+    clear_blocks(total, 2 * SHARE)
+    sweep(scal[4], codes, tiles, recv, total, backward_spots(2 * SHARE), 0)
+    part = SHARE // len(gives)
+
+    def split(b, _):
+        for i, give in enumerate(gives):
+            keep[i * part + b] = total[core * SHARE + i * part + b]
+            give[b] = total[(1 - core) * SHARE + i * part + b].astype(give.dtype)
+        return 0
+
+    lax.fori_loop(0, part, split, 0, unroll=2)
 
 
 def near_pair_kernel(keep, got, own, one, three):
@@ -182,18 +185,38 @@
     lax.fori_loop(0, SHARE, step, 0, unroll=4)
 
 
-def final_kernel(own, one, two, three, out):
+def far_pair_kernel(keep, *rest):
+    gots, out = rest[:-1], rest[-1]
+    part = SHARE // len(gots)
+
+    def step(b, _):
+        for i, got in enumerate(gots):
+            out[i * part + b] = (keep[i * part + b] + got[b].astype(jnp.float32)).astype(out.dtype)
+        return 0
+
+    lax.fori_loop(0, part, step, 0, unroll=2)
+
+
+def near_sum_kernel(own, one, three, out):
+    def step(b, _):
+        out[b] = own[b] + one[b].astype(jnp.float32) + three[b].astype(jnp.float32)
+        return 0
+
+    lax.fori_loop(0, SHARE, step, 0, unroll=4)
+
+
+def final_kernel(begun, two, out):
     for b in range(SHARE):
-        total = own[b] + one[b].astype(jnp.float32)
-        total = total + two[b].astype(jnp.float32) + three[b].astype(jnp.float32)
+        total = begun[b] + two[b].astype(jnp.float32)
         out[:, b * TILE:(b + 1) * TILE] = total.astype(jnp.bfloat16)
 
 
-def call(kernel, outs, scalars, arrays, scratch=(), limit=8, hbm=False, aliases=None):
+def call(kernel, outs, scalars, arrays, scratch=(), limit=8, hbm=(), aliases=None, cost=None):
     spec_vmem = pl.BlockSpec(memory_space=pltpu.VMEM)
     spec_smem = pl.BlockSpec(memory_space=pltpu.SMEM)
     spec_hbm = pl.BlockSpec(memory_space=pltpu.HBM)
-    specs = [spec_smem] * len(scalars) + [spec_hbm if hbm else spec_vmem] * len(arrays)
+    specs = [spec_smem] * len(scalars)
+    specs += [spec_hbm if i in hbm else spec_vmem for i in range(len(arrays))]
     single = not isinstance(outs, (list, tuple))
     return pl.pallas_call(
         kernel,
@@ -202,6 +225,7 @@
         out_specs=spec_vmem if single else [spec_vmem] * len(outs),
         scratch_shapes=list(scratch),
         input_output_aliases=aliases or {},
+        cost_estimate=cost,
         compiler_params=pltpu.CompilerParams(vmem_limit_bytes=limit << 20),
     )(*scalars, *arrays)
 
@@ -247,13 +271,6 @@
 
     mine = vectors.reshape(K, SHARE * TILE)
     near = [mine, along_x(mine, -1), along_x(mine, 1)]
-    far = along_x(mine, 2)
-    first = jnp.stack([live]).astype(jnp.int32)
-    held = call(
-        fetch_kernel, shape(local.shape, bf16), [first],
-        [pltpu.with_memory_space_constraint(local, pltpu.HBM)],
-        [pltpu.SemaphoreType.DMA((local.shape[0] // CHUNK,))], limit=1, hbm=True,
-    )
 
     ids, rowc = named_rows(rows)
     codes, counts = slot_lists(rowc, cols, live, x)
@@ -261,16 +278,21 @@
     near_codes, far_codes = codes[0], codes[1]
     lanes = jnp.pad(ids, ((0, 0), (0, TILE - CAP))).astype(bf16)
     id_rows = jnp.broadcast_to(lanes[:, None, :], (N_COL, 16, TILE))
-    near, near_codes, far_codes, id_rows, scal, held = lax.optimization_barrier(
-        (near, near_codes, far_codes, id_rows, scal, held)
-    )
-
-    begun = call(
+    near, near_codes, far_codes, id_rows, scal = lax.optimization_barrier(
+        (near, near_codes, far_codes, id_rows, scal)
+    )
+
+    far = along_x(near[1], -1)
+    begun, held = call(
         forward_near_kernel,
-        shape((N_NAMED + 1, K, TILE), f32),
+        [shape((N_NAMED + 1, K, TILE), f32), shape(local.shape, bf16)],
         [near_codes, scal],
-        [held] + near + [swap_core(v) for v in near],
-        [pltpu.VMEM((2 * N_X * SHARE, K, TILE), bf16)],
+        [pltpu.with_memory_space_constraint(local, pltpu.HBM)] + near + [swap_core(v) for v in near],
+        [
+            pltpu.VMEM((2 * N_X * SHARE, K, TILE), bf16),
+            pltpu.SemaphoreType.DMA((local.shape[0] // CHUNK,)),
+        ],
+        hbm=(0,),
     )
     far, begun = lax.optimization_barrier((far, begun))
     send, _ = call(
@@ -298,16 +320,7 @@
     named = lax.all_to_all(spread, "col", 0, 0, tiled=True).reshape(N_NAMED, K, TILE)
 
     block = (SHARE, K, TILE)
-    keep, give = call(
-        backward_far_kernel,
-        [shape(block, f32), shape(block, bf16)],
-        [far_codes, scal],
-        [held, named],
-        [pltpu.VMEM((2 * SHARE + 1, K, TILE), f32)],
-    )
-    away = call(far_pair_kernel, shape(block, bf16), [], [keep, swap_core(give)])
-    away, named = lax.optimization_barrier((away, named))
-    two = along_x(away, 2)
+    wide, narrow = shape(block, f32), shape(block, bf16)
     keep, give = call(
         backward_near_kernel,
         [shape((3,) + block, f32), shape((3,) + block, bf16)],
@@ -315,14 +328,21 @@
         [held, named],
         [pltpu.VMEM((2 * N_X * SHARE + 1, K, TILE), f32)],
     )
-    own, one, three = call(
-        near_pair_kernel,
-        [shape(block, f32), shape(block, bf16), shape(block, bf16)],
-        [],
-        [keep, swap_core(give)],
-    )
+    own, one, three = call(near_pair_kernel, [wide, narrow, narrow], [], [keep, swap_core(give)])
+    one, three, named = lax.optimization_barrier((one, three, named))
     one, three = along_x(one, 1), along_x(three, -1)
-    back = call(final_kernel, shape((K, SHARE * TILE), bf16), [], [own, one, two, three])
+    keep, *gives = call(
+        backward_far_kernel,
+        [wide] + [shape((SHARE // PARTS, K, TILE), bf16)] * PARTS,
+        [far_codes, scal],
+        [held, named],
+        [pltpu.VMEM((2 * SHARE + 1, K, TILE), f32)],
+        cost=LONG,
+    )
+    away = call(far_pair_kernel, narrow, [], [keep] + [swap_core(v) for v in gives])
+    two = along_x(away, 2)
+    begun = call(near_sum_kernel, wide, [], [own, one, three], cost=LONG)
+    back = call(final_kernel, shape((K, SHARE * TILE), bf16), [], [begun, two])
     return image, back.reshape(vectors.shape)
 
 

time: 113 us -> 110 us (0.973)
  waiting for transfers between devices: 17.3 us -> 12.6 us
  blocking collectives: 55.6 us -> 51.5 us
  starting transfers between devices: 12.6 us -> 16.7 us
    ppermute x6, waiting for transfers between devices: 12.7 us -> 8.17 us  [along_x(): return lax.ppermute(value, 'row', [(i, (i + 2 * d) % 8) for i in range(8)])]
    ppermute x6, starting transfers between devices: 7.24 us -> 11 us  [along_x(): return lax.ppermute(value, 'row', [(i, (i + 2 * d) % 8) for i in range(8)])]
    all_to_all x1, blocking collectives: 31 us -> 28.1 us  [per_device(): recv = lax.all_to_all(send, 'col', 0, 0, tiled=True)]
    all_to_all x1, blocking collectives: 24.6 us -> 23.4 us  [per_device(): lax.all_to_all(spread, 'col', 0, 0, tiled=True).reshape(N_NAMED, K, TILE)]
    ppermute x6 -> x7, starting transfers between devices: 5.36 us -> 5.63 us  [swap_core(): return lax.ppermute(value, 'row', [(i, i ^ 1) for i in range(8)])]
    ppermute x6 -> x7, waiting for transfers between devices: 4.6 us -> 4.47 us  [swap_core(): return lax.ppermute(value, 'row', [(i, i ^ 1) for i in range(8)])]
  transfers between devices with their start and end apart: 12 -> 13, of which waited for: 7 -> 7; matrix products, arithmetic and copies ran while one was open for 4% -> 4% of each run, Pallas kernels for 9% -> 10%
where the time goes in v3:
time: 110 us
  blocking collectives  51.5 us (47%)
  Pallas kernels  22.2 us (20%)
  starting transfers between devices  16.7 us (15%)
  waiting for transfers between devices  12.6 us (11%)
  other arithmetic  3.96 us (4%)
  between operations  1.46 us (1%)
  local copies, waits for them, and re-layouts  1.23 us (1%)
    all_to_all x1, blocking collectives, per_device(): recv = lax.all_to_all(send, 'col', 0, 0, tiled=True)  28.1 us
    all_to_all x1, blocking collectives, per_device(): lax.all_to_all(spread, 'col', 0, 0, tiled=True).reshape(N_NAMED, K, TILE)  23.4 us
    pallas_call x9, Pallas kernels, call(): pl.pallas_call(kernel, out_shape=outs, in_specs=specs, out_specs=spec_vme...  22.2 us
    ppermute x6, starting transfers between devices, along_x(): return lax.ppermute(value, 'row', [(i, (i + 2 * d) % 8) for i in range(8)])  11 us
    ppermute x6, waiting for transfers between devices, along_x(): return lax.ppermute(value, 'row', [(i, (i + 2 * d) % 8) for i in range(8)])  8.17 us
    ppermute x7, starting transfers between devices, swap_core(): return lax.ppermute(value, 'row', [(i, i ^ 1) for i in range(8)])  5.63 us
    ppermute x7, waiting for transfers between devices, swap_core(): return lax.ppermute(value, 'row', [(i, i ^ 1) for i in range(8)])  4.47 us
  transfers between devices with their start and end apart: 13, of which 7 were waited for; matrix products, arithmetic and copies ran while one was open for 4% of the time, Pallas kernels for 10%

profile of v3, /device:TPU:1, one launch (start us, length us, event | category | flops | bytes accessed | tf_op | source)
XLA Modules:
  0.0 109.7 jit_solution(3913646209846573278)
XLA Ops:
  0.6 2.1 %collective-permute-start.1 = (bf16[32,4096]{1,0:T(8,128)(2,1)}, bf16[32,4096]{1,0:T(8,128)(2,1)S(1)}, u32[]{:S(2)}, u32[]{:S(2)}) collective-permute-start(bf16[32,4096]{1,0:T(8,128)(2,1)} %bitcast.17), channel_id=1, source_target_pairs={{0,32},{16,48},{32,64},{48,80},{64,96},{80,112},{96,0},{112,16},{1... | collective-permute-start | bytes 786440 | tf_op jit(solution)/shard_map/ppermute | solution.py:267
  2.7 1.4 %collective-permute-start = (bf16[32,4096]{1,0:T(8,128)(2,1)}, bf16[32,4096]{1,0:T(8,128)(2,1)S(1)}, u32[]{:S(2)}, u32[]{:S(2)}) collective-permute-start(bf16[32,4096]{1,0:T(8,128)(2,1)} %bitcast.18), channel_id=1, source_target_pairs={{0,96},{16,112},{32,0},{48,16},{64,32},{80,48},{96,64},{112,80},{1... | collective-permute-start | bytes 786440 | tf_op jit(solution)/shard_map/ppermute | solution.py:267
  4.8 0.7 reduce
  5.7 0.7 shift-left_reduce_fusion
  9.0 0.8 collective-permute-done.1.refs_2_
  9.8 1.9 %collective-permute-start.2 = (bf16[32,4096]{1,0:T(8,128)(2,1)}, bf16[32,4096]{1,0:T(8,128)(2,1)S(1)}, u32[]{:S(2)}, u32[]{:S(2)}) collective-permute-start(bf16[32,4096]{1,0:T(8,128)(2,1)} %bitcast.19), channel_id=1, source_target_pairs={{0,16},{16,0},{32,48},{48,32},{64,80},{80,64},{96,112},{112,96},{1... | collective-permute-start | bytes 786440 | tf_op jit(solution)/shard_map/ppermute | solution.py:270
  12.3 2.6 %collective-permute-start.5 = (bf16[32,4096]{1,0:T(8,128)(2,1)S(1)}, bf16[32,4096]{1,0:T(8,128)(2,1)S(1)}, u32[]{:S(2)}, u32[]{:S(2)}) collective-permute-start(bf16[32,4096]{1,0:T(8,128)(2,1)S(1)} %collective-permute-done.refs_1_), channel_id=1, source_target_pairs={{0,96},{16,112},{32,0},{48,16},{64,32},{80,48},{96,64},{112,80},{1... | collective-permute-start | bytes 786440 | tf_op jit(solution)/shard_map/ppermute | solution.py:267
  14.9 0.9 copy-done
  15.8 8.2 %shard_map.68 = (f32[193,32,128]{2,1,0:T(8,128)S(1)}, bf16[384,128,128]{2,1,0:T(8,128)(2,1)S(1)}) custom-call(s32[384]{0:T(512)S(1)} %get-tuple-element.29.codes, s32[5]{0:T(128)S(1)} %pad_add_fusion.1.scal, bf16[384,128,128]{2,1,0:T(8,128)(2,1)} %bitcast.21, bf16[32,4096]{1,0:T(8,128)(2,1)S(1)} %bitcast.20, ...), custom_call_target="tpu_custom_call" | custom-call | tf_op jit(solution)/shard_map/pallas_call | solution.py:221
  24.2 1.5 %collective-permute-done.6.there = bf16[32,4096]{1,0:T(8,128)(2,1)S(1)} collective-permute-done((bf16[32,4096]{1,0:T(8,128)(2,1)S(1)}, bf16[32,4096]{1,0:T(8,128)(2,1)S(1)}, u32[]{:S(2)}, u32[]{:S(2)}) %collective-permute-start.6) | collective-permute-done | bytes 262176 | tf_op jit(solution)/shard_map/ppermute | solution.py:270
  25.7 3.6 %shard_map.69 = (bf16[16,400,128]{2,1,0:T(8,128)(2,1)S(1)}, f32[193,32,128]{2,1,0:T(8,128)S(1)}) custom-call(s32[384]{0:T(512)S(1)} %get-tuple-element.27.codes, s32[5]{0:T(128)S(1)} %pad_add_fusion.1.scal, bf16[384,128,128]{2,1,0:T(8,128)(2,1)S(1)} %get-tuple-element.33.tiles, ...), custom_call_target="tpu_custom_call", output_to_operand_aliasing={{1}: (6, {})} | custom-call | tf_op jit(solution)/shard_map/pallas_call | solution.py:221
  29.3 28.1 %all_to_all.10.recv = bf16[16,400,128]{2,1,0:T(8,128)(2,1)S(1)} all-to-all(bf16[16,400,128]{2,1,0:T(8,128)(2,1)S(1)} %get-tuple-element.38), channel_id=1, replica_groups=mesh['row'=8,'col'=16] {'col'}, dimensions={0} | all-to-all | bytes 3276800 | tf_op jit(solution)/shard_map/all_to_all | solution.py:306
  57.4 2.4 %shard_map.70 = (bf16[32,4096]{1,0:T(8,128)(2,1)}, bf16[16,384,128]{2,1,0:T(8,128)(2,1)S(1)}) custom-call(bf16[16,400,128]{2,1,0:T(8,128)(2,1)S(1)} %all_to_all.10.recv), custom_call_target="tpu_custom_call" | custom-call | tf_op jit(solution)/shard_map/pallas_call | solution.py:221
  59.8 23.4 %all_to_all.11 = bf16[16,384,128]{2,1,0:T(8,128)(2,1)S(1)} all-to-all(bf16[16,384,128]{2,1,0:T(8,128)(2,1)S(1)} %get-tuple-element.40), channel_id=1, replica_groups=mesh['row'=8,'col'=16] {'col'}, dimensions={0} | all-to-all | bytes 3145728 | tf_op jit(solution)/shard_map/all_to_all | solution.py:320
  83.2 4.6 %shard_map.71 = (f32[3,32,32,128]{3,2,1,0:T(8,128)S(1)}, bf16[3,32,32,128]{3,2,1,0:T(8,128)(2,1)S(1)}) custom-call(s32[384]{0:T(512)S(1)} %get-tuple-element.29.codes, s32[5]{0:T(128)S(1)} %pad_add_fusion.1.scal, bf16[384,128,128]{2,1,0:T(8,128)(2,1)S(1)} %get-tuple-element.33.tiles, bf16[192,32,128]{2,1,0:T(8,128)(2,1)S(1)} %bitcast.15), custom_call_target="tpu_custom_call" | custom-call | tf_op jit(solution)/shard_map/pallas_call | solution.py:221
  87.8 2.5 %collective-permute-start.7 = (bf16[3,32,32,128]{3,2,1,0:T(8,128)(2,1)S(1)}, bf16[3,32,32,128]{3,2,1,0:T(8,128)(2,1)S(1)}, u32[]{:S(2)}, u32[]{:S(2)}) collective-permute-start(bf16[3,32,32,128]{3,2,1,0:T(8,128)(2,1)S(1)} %get-tuple-element.42), channel_id=1, source_target_pairs={{0,16},{16,0},{32,48},{48,32},{64,80},{80,64},{96,112},{112,96},{1... | collective-permute-start | bytes 2359304 | tf_op jit(solution)/shard_map/ppermute | solution.py:270
  90.3 1.9 %collective-permute-done.7.got = bf16[3,32,32,128]{3,2,1,0:T(8,128)(2,1)S(1)} collective-permute-done((bf16[3,32,32,128]{3,2,1,0:T(8,128)(2,1)S(1)}, bf16[3,32,32,128]{3,2,1,0:T(8,128)(2,1)S(1)}, u32[]{:S(2)}, u32[]{:S(2)}) %collective-permute-start.7) | collective-permute-done | bytes 786464 | tf_op jit(solution)/shard_map/ppermute | solution.py:270
  92.4 1.8 %collective-permute-start.8 = (bf16[32,32,128]{2,1,0:T(8,128)(2,1)S(1)}, bf16[32,32,128]{2,1,0:T(8,128)(2,1)S(1)}, u32[]{:S(2)}, u32[]{:S(2)}) collective-permute-start(bf16[32,32,128]{2,1,0:T(8,128)(2,1)S(1)} %get-tuple-element.46), channel_id=1, source_target_pairs={{0,32},{16,48},{32,64},{48,80},{64,96},{80,112},{96,0},{112,16},{1... | collective-permute-start | bytes 786440 | tf_op jit(solution)/shard_map/ppermute | solution.py:267
  94.2 1.5 %collective-permute-start.9 = (bf16[32,32,128]{2,1,0:T(8,128)(2,1)S(1)}, bf16[32,32,128]{2,1,0:T(8,128)(2,1)S(1)}, u32[]{:S(2)}, u32[]{:S(2)}) collective-permute-start(bf16[32,32,128]{2,1,0:T(8,128)(2,1)S(1)} %get-tuple-element.47), channel_id=1, source_target_pairs={{0,96},{16,112},{32,0},{48,16},{64,32},{80,48},{96,64},{112,80},{1... | collective-permute-start | bytes 786440 | tf_op jit(solution)/shard_map/ppermute | solution.py:267
  95.7 2.4 %shard_map.74 = (f32[32,32,128]{2,1,0:T(8,128)S(1)}, bf16[16,32,128]{2,1,0:T(8,128)(2,1)S(1)}, bf16[16,32,128]{2,1,0:T(8,128)(2,1)S(1)}) custom-call(s32[384]{0:T(512)S(1)} %get-tuple-element.27.codes, s32[5]{0:T(128)S(1)} %pad_add_fusion.1.scal, bf16[384,128,128]{2,1,0:T(8,128)(2,1)S(1)} %get-tuple-element.33.tiles, bf16[192,32,128]{2,1,0:T(8,128)(2,1)S(1)} %bitcast.16), custom_call_target="tpu_custom_call" | custom-call | flops 68719476736 | bytes 67108864 | tf_op jit(solution)/shard_map/pallas_call | solution.py:221
  98.7 0.8 collective-permute-done.10.rest_0_
  99.8 1.7 %collective-permute-start.12 = (bf16[32,32,128]{2,1,0:T(8,128)(2,1)S(1)}, bf16[32,32,128]{2,1,0:T(8,128)(2,1)S(1)}, u32[]{:S(2)}, u32[]{:S(2)}) collective-permute-start(bf16[32,32,128]{2,1,0:T(8,128)(2,1)S(1)} %shard_map.75), channel_id=1, source_target_pairs={{0,64},{16,80},{32,96},{48,112},{64,0},{80,16},{96,32},{112,48},{1... | collective-permute-start | bytes 786440 | tf_op jit(solution)/shard_map/ppermute | solution.py:267
  102.1 6.8 %collective-permute-done.12.two = bf16[32,32,128]{2,1,0:T(8,128)(2,1)S(1)} collective-permute-done((bf16[32,32,128]{2,1,0:T(8,128)(2,1)S(1)}, bf16[32,32,128]{2,1,0:T(8,128)(2,1)S(1)}, u32[]{:S(2)}, u32[]{:S(2)}) %collective-permute-start.12) | collective-permute-done | bytes 262176 | tf_op jit(solution)/shard_map/ppermute | solution.py:267
  108.9 0.8 shard_map.76
  (41 shorter events, 5.1 us)
Async XLA Ops:
  0.6 9.2 %collective-permute-start.1 = (bf16[32,4096]{1,0:T(8,128)(2,1)}, bf16[32,4096]{1,0:T(8,128)(2,1)S(1)}, u32[]{:S(2)}, u32[]{:S(2)}) collective-permute-start(bf16[32,4096]{1,0:T(8,128)(2,1)} %bitcast.17), channel_id=1, source_target_pairs={{0,32},{16,48},{32,64},{48,80},{64,96},{80,112},{96,0},{112,16},{1... | collective-permute-start | bytes 786440 | tf_op jit(solution)/shard_map/ppermute | solution.py:267
  2.7 7.1 %collective-permute-start = (bf16[32,4096]{1,0:T(8,128)(2,1)}, bf16[32,4096]{1,0:T(8,128)(2,1)S(1)}, u32[]{:S(2)}, u32[]{:S(2)}) collective-permute-start(bf16[32,4096]{1,0:T(8,128)(2,1)} %bitcast.18), channel_id=1, source_target_pairs={{0,96},{16,112},{32,0},{48,16},{64,32},{80,48},{96,64},{112,80},{1... | collective-permute-start | bytes 786440 | tf_op jit(solution)/shard_map/ppermute | solution.py:267
  9.8 5.0 %collective-permute-start.2 = (bf16[32,4096]{1,0:T(8,128)(2,1)}, bf16[32,4096]{1,0:T(8,128)(2,1)S(1)}, u32[]{:S(2)}, u32[]{:S(2)}) collective-permute-start(bf16[32,4096]{1,0:T(8,128)(2,1)} %bitcast.19), channel_id=1, source_target_pairs={{0,16},{16,0},{32,48},{48,32},{64,80},{80,64},{96,112},{112,96},{1... | collective-permute-start | bytes 786440 | tf_op jit(solution)/shard_map/ppermute | solution.py:270
  11.8 3.1 %collective-permute-start.4 = (bf16[32,4096]{1,0:T(8,128)(2,1)S(1)}, bf16[32,4096]{1,0:T(8,128)(2,1)S(1)}, u32[]{:S(2)}, u32[]{:S(2)}) collective-permute-start(bf16[32,4096]{1,0:T(8,128)(2,1)S(1)} %collective-permute-done.1.refs_2_), channel_id=1, source_target_pairs={{0,16},{16,0},{32,48},{48,32},{64,80},{80,64},{96,112},{112,96},{1... | collective-permute-start | bytes 786440 | tf_op jit(solution)/shard_map/ppermute | solution.py:270
  11.9 3.0 %collective-permute-start.3 = (bf16[32,4096]{1,0:T(8,128)(2,1)S(1)}, bf16[32,4096]{1,0:T(8,128)(2,1)S(1)}, u32[]{:S(2)}, u32[]{:S(2)}) collective-permute-start(bf16[32,4096]{1,0:T(8,128)(2,1)S(1)} %collective-permute-done.refs_1_), channel_id=1, source_target_pairs={{0,16},{16,0},{32,48},{48,32},{64,80},{80,64},{96,112},{112,96},{1... | collective-permute-start | bytes 786440 | tf_op jit(solution)/shard_map/ppermute | solution.py:270
  12.3 11.8 %collective-permute-start.5 = (bf16[32,4096]{1,0:T(8,128)(2,1)S(1)}, bf16[32,4096]{1,0:T(8,128)(2,1)S(1)}, u32[]{:S(2)}, u32[]{:S(2)}) collective-permute-start(bf16[32,4096]{1,0:T(8,128)(2,1)S(1)} %collective-permute-done.refs_1_), channel_id=1, source_target_pairs={{0,96},{16,112},{32,0},{48,16},{64,32},{80,48},{96,64},{112,80},{1... | collective-permute-start | bytes 786440 | tf_op jit(solution)/shard_map/ppermute | solution.py:267
  14.9 1.0 copy-start
  24.1 1.6 %collective-permute-start.6 = (bf16[32,4096]{1,0:T(8,128)(2,1)S(1)}, bf16[32,4096]{1,0:T(8,128)(2,1)S(1)}, u32[]{:S(2)}, u32[]{:S(2)}) collective-permute-start(bf16[32,4096]{1,0:T(8,128)(2,1)S(1)} %collective-permute-done.5.here), channel_id=1, source_target_pairs={{0,16},{16,0},{32,48},{48,32},{64,80},{80,64},{96,112},{112,96},{1... | collective-permute-start | bytes 786440 | tf_op jit(solution)/shard_map/ppermute | solution.py:270
  87.8 4.4 %collective-permute-start.7 = (bf16[3,32,32,128]{3,2,1,0:T(8,128)(2,1)S(1)}, bf16[3,32,32,128]{3,2,1,0:T(8,128)(2,1)S(1)}, u32[]{:S(2)}, u32[]{:S(2)}) collective-permute-start(bf16[3,32,32,128]{3,2,1,0:T(8,128)(2,1)S(1)} %get-tuple-element.42), channel_id=1, source_target_pairs={{0,16},{16,0},{32,48},{48,32},{64,80},{80,64},{96,112},{112,96},{1... | collective-permute-start | bytes 2359304 | tf_op jit(solution)/shard_map/ppermute | solution.py:270
  92.4 9.6 %collective-permute-start.8 = (bf16[32,32,128]{2,1,0:T(8,128)(2,1)S(1)}, bf16[32,32,128]{2,1,0:T(8,128)(2,1)S(1)}, u32[]{:S(2)}, u32[]{:S(2)}) collective-permute-start(bf16[32,32,128]{2,1,0:T(8,128)(2,1)S(1)} %get-tuple-element.46), channel_id=1, source_target_pairs={{0,32},{16,48},{32,64},{48,80},{64,96},{80,112},{96,0},{112,16},{1... | collective-permute-start | bytes 786440 | tf_op jit(solution)/shard_map/ppermute | solution.py:267
  94.2 7.8 %collective-permute-start.9 = (bf16[32,32,128]{2,1,0:T(8,128)(2,1)S(1)}, bf16[32,32,128]{2,1,0:T(8,128)(2,1)S(1)}, u32[]{:S(2)}, u32[]{:S(2)}) collective-permute-start(bf16[32,32,128]{2,1,0:T(8,128)(2,1)S(1)} %get-tuple-element.47), channel_id=1, source_target_pairs={{0,96},{16,112},{32,0},{48,16},{64,32},{80,48},{96,64},{112,80},{1... | collective-permute-start | bytes 786440 | tf_op jit(solution)/shard_map/ppermute | solution.py:267
  98.1 1.4 %collective-permute-start.10 = (bf16[16,32,128]{2,1,0:T(8,128)(2,1)S(1)}, bf16[16,32,128]{2,1,0:T(8,128)(2,1)S(1)}, u32[]{:S(2)}, u32[]{:S(2)}) collective-permute-start(bf16[16,32,128]{2,1,0:T(8,128)(2,1)S(1)} %get-tuple-element.50), channel_id=1, source_target_pairs={{0,16},{16,0},{32,48},{48,32},{64,80},{80,64},{96,112},{112,96},{1... | collective-permute-start | bytes 393224 | tf_op jit(solution)/shard_map/ppermute | solution.py:270
  98.2 1.5 %collective-permute-start.11 = (bf16[16,32,128]{2,1,0:T(8,128)(2,1)S(1)}, bf16[16,32,128]{2,1,0:T(8,128)(2,1)S(1)}, u32[]{:S(2)}, u32[]{:S(2)}) collective-permute-start(bf16[16,32,128]{2,1,0:T(8,128)(2,1)S(1)} %get-tuple-element.51), channel_id=1, source_target_pairs={{0,16},{16,0},{32,48},{48,32},{64,80},{80,64},{96,112},{112,96},{1... | collective-permute-start | bytes 393224 | tf_op jit(solution)/shard_map/ppermute | solution.py:270
  99.8 9.2 %collective-permute-start.12 = (bf16[32,32,128]{2,1,0:T(8,128)(2,1)S(1)}, bf16[32,32,128]{2,1,0:T(8,128)(2,1)S(1)}, u32[]{:S(2)}, u32[]{:S(2)}) collective-permute-start(bf16[32,32,128]{2,1,0:T(8,128)(2,1)S(1)} %shard_map.75), channel_id=1, source_target_pairs={{0,64},{16,80},{32,96},{48,112},{64,0},{80,16},{96,32},{112,48},{1... | collective-permute-start | bytes 786440 | tf_op jit(solution)/shard_map/ppermute | solution.py:267

commit v4 on v3

--- a/solution.py
+++ b/solution.py
@@ -26,6 +26,10 @@
     return pltpu.make_async_copy(tiles.at[span], held.at[span], sems.at[chunk])
 
 
+def in_hbm(value):
+    return pltpu.with_memory_space_constraint(value, pltpu.HBM)
+
+
 def code_parts(code):
     return code & 511, (code >> 9) & 255, (code >> 17) & 255, code >> 25
 
@@ -35,18 +39,19 @@
         base = g * GROUP
         if ready is not None:
             seen = ready(seen, (codes[jnp.minimum(base + GROUP, count) - 1] & 511) // CHUNK + 1)
-        products, places = [], []
-        for u in range(GROUP):
-            slot, source, place = spots(*code_parts(codes[base + u]))
-            places.append(place)
-            products.append(
-                lax.dot_general(
-                    left[source],
-                    tiles[slot],
-                    (((1,), (dims,)), ((), ())),
-                    preferred_element_type=jnp.float32,
-                )
+        slots, sources, places = zip(*(spots(*code_parts(codes[base + u])) for u in range(GROUP)))
+        blank = jnp.zeros((K, TILE), jnp.bfloat16)
+        products = []
+        for u in range(0, GROUP, 2):
+            above = jnp.concatenate([left[sources[u]], blank], axis=1)
+            below = jnp.concatenate([blank, left[sources[u + 1]]], axis=1)
+            pair = lax.dot_general(
+                jnp.concatenate([above, below], axis=0),
+                jnp.concatenate([tiles[slots[u]], tiles[slots[u + 1]]], axis=dims),
+                (((1,), (dims,)), ((), ())),
+                preferred_element_type=jnp.float32,
             )
+            products += [pair[:K], pair[K:]]
         for place, product in zip(places, products):
             total[place] += product
         return seen
@@ -67,7 +72,8 @@
 
 
 def forward_near_kernel(codes, scal, tiles, *refs):
-    pieces, (total, held, vec, sems) = refs[:6], refs[6:]
+    mine_hbm, (total, held, vec, sems, mine, sem) = refs[0], refs[6:]
+    pieces = (mine,) + refs[1:6]
     live, x, core = scal[0], scal[1], scal[2]
     chunks = (live + CHUNK - 1) // CHUNK
 
@@ -83,14 +89,17 @@
         lax.fori_loop(seen, need, wait, 0)
         return jnp.maximum(seen, need)
 
+    fetch = pltpu.make_async_copy(mine_hbm, mine, sem)
+    fetch.start()
     lax.fori_loop(0, chunks, start, 0)
+    clear_blocks(total, N_NAMED)
+    fetch.wait()
     for i, d in enumerate(NEAR):
         for other in range(2):
             piece = pieces[i + 3 * other]
             first = (((x + d) % N_X) * 2 + (core + other) % 2) * SHARE
             for b in range(SHARE):
                 vec[first + b] = piece[:, b * TILE:(b + 1) * TILE]
-    clear_blocks(total, N_NAMED)
     seen = sweep(scal[3], codes, held, vec, total, forward_spots(2 * N_X * SHARE), 1, ready)
     lax.fori_loop(seen, chunks, wait, 0)
 
@@ -282,24 +291,27 @@
         (near, near_codes, far_codes, id_rows, scal)
     )
 
+    swapped = [swap_core(v) for v in near]
     far = along_x(near[1], -1)
     begun, held = call(
         forward_near_kernel,
         [shape((N_NAMED + 1, K, TILE), f32), shape(local.shape, bf16)],
         [near_codes, scal],
-        [pltpu.with_memory_space_constraint(local, pltpu.HBM)] + near + [swap_core(v) for v in near],
+        [in_hbm(local), in_hbm(mine)] + near[1:] + swapped,
         [
             pltpu.VMEM((2 * N_X * SHARE, K, TILE), bf16),
             pltpu.SemaphoreType.DMA((local.shape[0] // CHUNK,)),
+            pltpu.VMEM((K, SHARE * TILE), bf16),
+            pltpu.SemaphoreType.DMA,
         ],
-        hbm=(0,),
-    )
-    far, begun = lax.optimization_barrier((far, begun))
+        hbm=(0, 1),
+    )
+    far, far_there, begun = lax.optimization_barrier((far, along_x(swapped[2], 1), begun))
     send, _ = call(
         forward_far_kernel,
         [shape((N_COL, PAY_ROWS, TILE), bf16), shape((N_NAMED + 1, K, TILE), f32)],
         [far_codes, scal],
-        [held, id_rows, far, swap_core(far), begun],
+        [held, id_rows, far, far_there, begun],
         [pltpu.VMEM((2 * SHARE, K, TILE), bf16)],
         aliases={6: 1},
     )

time: 110 us -> 109 us (level); the launches traced: 110 us -> 110 us
  Pallas kernels: 22.2 us -> 11.9 us
  waiting for transfers between devices: 12.6 us -> 17.9 us
  blocking collectives: 51.5 us -> 55.4 us
  starting transfers between devices: 16.7 us -> 18.8 us
    pallas_call x9, Pallas kernels: 22.2 us -> 11.9 us  [call(): pl.pallas_call(kernel, out_shape=outs, in_specs=specs, out_specs=spec_vme...]
    ppermute x6 -> x7, waiting for transfers between devices: 8.17 us -> 14.8 us  [along_x(): return lax.ppermute(value, 'row', [(i, (i + 2 * d) % 8) for i in range(8)])]
    ppermute x7 -> x6, starting transfers between devices: 5.63 us -> 9.93 us  [swap_core(): return lax.ppermute(value, 'row', [(i, i ^ 1) for i in range(8)])]
    all_to_all x1, blocking collectives: 28.1 us -> 31.3 us  [per_device(): recv = lax.all_to_all(send, 'col', 0, 0, tiled=True)]
    ppermute x6 -> x7, starting transfers between devices: 11 us -> 8.86 us  [along_x(): return lax.ppermute(value, 'row', [(i, (i + 2 * d) % 8) for i in range(8)])]
    ppermute x7 -> x6, waiting for transfers between devices: 4.47 us -> 3.17 us  [swap_core(): return lax.ppermute(value, 'row', [(i, i ^ 1) for i in range(8)])]
  transfers between devices with their start and end apart: 13 -> 13, of which waited for: 7 -> 8; matrix products, arithmetic and copies ran while one was open for 4% -> 4% of each run, Pallas kernels for 10% -> 5%
where the time goes in v4:
time: 109 us; the launch traced here: 110 us
  blocking collectives  55.4 us (51%)
  starting transfers between devices  18.8 us (17%)
  waiting for transfers between devices  17.9 us (16%)
  Pallas kernels  11.9 us (11%)
  other arithmetic  3.96 us (4%)
  between operations  1.45 us (1%)
    all_to_all x1, blocking collectives, per_device(): recv = lax.all_to_all(send, 'col', 0, 0, tiled=True)  31.3 us
    all_to_all x1, blocking collectives, per_device(): lax.all_to_all(spread, 'col', 0, 0, tiled=True).reshape(N_NAMED, K, TILE)  24.1 us
    ppermute x7, waiting for transfers between devices, along_x(): return lax.ppermute(value, 'row', [(i, (i + 2 * d) % 8) for i in range(8)])  14.8 us
    pallas_call x9, Pallas kernels, call(): pl.pallas_call(kernel, out_shape=outs, in_specs=specs, out_specs=spec_vme...  11.9 us
    ppermute x6, starting transfers between devices, swap_core(): return lax.ppermute(value, 'row', [(i, i ^ 1) for i in range(8)])  9.93 us
    ppermute x7, starting transfers between devices, along_x(): return lax.ppermute(value, 'row', [(i, (i + 2 * d) % 8) for i in range(8)])  8.86 us
    ppermute x6, waiting for transfers between devices, swap_core(): return lax.ppermute(value, 'row', [(i, i ^ 1) for i in range(8)])  3.17 us
  transfers between devices with their start and end apart: 13, of which 8 were waited for; matrix products, arithmetic and copies ran while one was open for 4% of the time, Pallas kernels for 5%

profile of v4, /device:TPU:1, one launch (start us, length us, event | category | flops | bytes accessed | tf_op | source)
XLA Modules:
  0.0 109.8 jit_solution(3614965752159286608)
XLA Ops:
  0.6 2.1 %collective-permute-start.1 = (bf16[32,4096]{1,0:T(8,128)(2,1)}, bf16[32,4096]{1,0:T(8,128)(2,1)S(1)}, u32[]{:S(2)}, u32[]{:S(2)}) collective-permute-start(bf16[32,4096]{1,0:T(8,128)(2,1)} %bitcast.18), channel_id=1, source_target_pairs={{0,32},{16,48},{32,64},{48,80},{64,96},{80,112},{96,0},{112,16},{1... | collective-permute-start | bytes 786440 | tf_op jit(solution)/shard_map/ppermute | solution.py:276
  2.7 1.4 %collective-permute-start = (bf16[32,4096]{1,0:T(8,128)(2,1)}, bf16[32,4096]{1,0:T(8,128)(2,1)S(1)}, u32[]{:S(2)}, u32[]{:S(2)}) collective-permute-start(bf16[32,4096]{1,0:T(8,128)(2,1)} %bitcast.19), channel_id=1, source_target_pairs={{0,96},{16,112},{32,0},{48,16},{64,32},{80,48},{96,64},{112,80},{1... | collective-permute-start | bytes 786440 | tf_op jit(solution)/shard_map/ppermute | solution.py:276
  4.8 0.7 reduce
  5.7 0.7 shift-left_reduce_fusion
  9.0 0.8 collective-permute-done.1.refs_2_
  9.8 1.9 %collective-permute-start.4 = (bf16[32,4096]{1,0:T(8,128)(2,1)S(1)}, bf16[32,4096]{1,0:T(8,128)(2,1)S(1)}, u32[]{:S(2)}, u32[]{:S(2)}) collective-permute-start(bf16[32,4096]{1,0:T(8,128)(2,1)S(1)} %collective-permute-done.1.refs_2_), channel_id=1, source_target_pairs={{0,16},{16,0},{32,48},{48,32},{64,80},{80,64},{96,112},{112,96},{1... | collective-permute-start | bytes 786440 | tf_op jit(solution)/shard_map/ppermute | solution.py:279
  12.3 2.6 %collective-permute-start.5 = (bf16[32,4096]{1,0:T(8,128)(2,1)S(1)}, bf16[32,4096]{1,0:T(8,128)(2,1)S(1)}, u32[]{:S(2)}, u32[]{:S(2)}) collective-permute-start(bf16[32,4096]{1,0:T(8,128)(2,1)S(1)} %collective-permute-done.refs_1_), channel_id=1, source_target_pairs={{0,96},{16,112},{32,0},{48,16},{64,32},{80,48},{96,64},{112,80},{1... | collective-permute-start | bytes 786440 | tf_op jit(solution)/shard_map/ppermute | solution.py:276
  14.9 3.8 %shard_map.68 = (f32[193,32,128]{2,1,0:T(8,128)S(1)}, bf16[384,128,128]{2,1,0:T(8,128)(2,1)S(1)}) custom-call(s32[384]{0:T(512)S(1)} %get-tuple-element.30.codes, s32[5]{0:T(128)S(1)} %pad_add_fusion.1.scal, bf16[384,128,128]{2,1,0:T(8,128)(2,1)} %bitcast.17, bf16[32,4096]{1,0:T(8,128)(2,1)} %bitcast.21, bf16[32,4096]{1,0:T(8,128)(2,1)S(1)} %collective-permute-done.refs_1_, ...), custom_call_target="tpu_custom_call" | custom-call | tf_op jit(solution)/shard_map/pallas_call | solution.py:230
  18.7 1.8 %collective-permute-done.5.here = bf16[32,4096]{1,0:T(8,128)(2,1)S(1)} collective-permute-done((bf16[32,4096]{1,0:T(8,128)(2,1)S(1)}, bf16[32,4096]{1,0:T(8,128)(2,1)S(1)}, u32[]{:S(2)}, u32[]{:S(2)}) %collective-permute-start.5) | collective-permute-done | bytes 262176 | tf_op jit(solution)/shard_map/ppermute | solution.py:276
  20.5 3.1 %collective-permute-done.6.there = bf16[32,4096]{1,0:T(8,128)(2,1)S(1)} collective-permute-done((bf16[32,4096]{1,0:T(8,128)(2,1)S(1)}, bf16[32,4096]{1,0:T(8,128)(2,1)S(1)}, u32[]{:S(2)}, u32[]{:S(2)}) %collective-permute-start.6) | collective-permute-done | bytes 262176 | tf_op jit(solution)/shard_map/ppermute | solution.py:276
  23.6 1.4 %shard_map.69 = (bf16[16,400,128]{2,1,0:T(8,128)(2,1)S(1)}, f32[193,32,128]{2,1,0:T(8,128)S(1)}) custom-call(s32[384]{0:T(512)S(1)} %get-tuple-element.28.codes, s32[5]{0:T(128)S(1)} %pad_add_fusion.1.scal, bf16[384,128,128]{2,1,0:T(8,128)(2,1)S(1)} %get-tuple-element.34.tiles, ...), custom_call_target="tpu_custom_call", output_to_operand_aliasing={{1}: (6, {})} | custom-call | tf_op jit(solution)/shard_map/pallas_call | solution.py:230
  25.0 31.3 %all_to_all.10.recv = bf16[16,400,128]{2,1,0:T(8,128)(2,1)S(1)} all-to-all(bf16[16,400,128]{2,1,0:T(8,128)(2,1)S(1)} %get-tuple-element.40), channel_id=1, replica_groups=mesh['row'=8,'col'=16] {'col'}, dimensions={0} | all-to-all | bytes 3276800 | tf_op jit(solution)/shard_map/all_to_all | solution.py:318
  56.4 2.4 %shard_map.70 = (bf16[32,4096]{1,0:T(8,128)(2,1)}, bf16[16,384,128]{2,1,0:T(8,128)(2,1)S(1)}) custom-call(bf16[16,400,128]{2,1,0:T(8,128)(2,1)S(1)} %all_to_all.10.recv), custom_call_target="tpu_custom_call" | custom-call | tf_op jit(solution)/shard_map/pallas_call | solution.py:230
  58.7 24.1 %all_to_all.11 = bf16[16,384,128]{2,1,0:T(8,128)(2,1)S(1)} all-to-all(bf16[16,384,128]{2,1,0:T(8,128)(2,1)S(1)} %get-tuple-element.42), channel_id=1, replica_groups=mesh['row'=8,'col'=16] {'col'}, dimensions={0} | all-to-all | bytes 3145728 | tf_op jit(solution)/shard_map/all_to_all | solution.py:332
  82.9 2.1 %shard_map.71 = (f32[3,32,32,128]{3,2,1,0:T(8,128)S(1)}, bf16[3,32,32,128]{3,2,1,0:T(8,128)(2,1)S(1)}) custom-call(s32[384]{0:T(512)S(1)} %get-tuple-element.30.codes, s32[5]{0:T(128)S(1)} %pad_add_fusion.1.scal, bf16[384,128,128]{2,1,0:T(8,128)(2,1)S(1)} %get-tuple-element.34.tiles, bf16[192,32,128]{2,1,0:T(8,128)(2,1)S(1)} %bitcast.15), custom_call_target="tpu_custom_call" | custom-call | tf_op jit(solution)/shard_map/pallas_call | solution.py:230
  85.0 5.7 %collective-permute-start.7 = (bf16[3,32,32,128]{3,2,1,0:T(8,128)(2,1)S(1)}, bf16[3,32,32,128]{3,2,1,0:T(8,128)(2,1)S(1)}, u32[]{:S(2)}, u32[]{:S(2)}) collective-permute-start(bf16[3,32,32,128]{3,2,1,0:T(8,128)(2,1)S(1)} %get-tuple-element.44), channel_id=1, source_target_pairs={{0,16},{16,0},{32,48},{48,32},{64,80},{80,64},{96,112},{112,96},{1... | collective-permute-start | bytes 2359304 | tf_op jit(solution)/shard_map/ppermute | solution.py:279
  90.7 1.9 %collective-permute-done.7.got = bf16[3,32,32,128]{3,2,1,0:T(8,128)(2,1)S(1)} collective-permute-done((bf16[3,32,32,128]{3,2,1,0:T(8,128)(2,1)S(1)}, bf16[3,32,32,128]{3,2,1,0:T(8,128)(2,1)S(1)}, u32[]{:S(2)}, u32[]{:S(2)}) %collective-permute-start.7) | collective-permute-done | bytes 786464 | tf_op jit(solution)/shard_map/ppermute | solution.py:279
  92.8 2.7 %collective-permute-start.9 = (bf16[32,32,128]{2,1,0:T(8,128)(2,1)S(1)}, bf16[32,32,128]{2,1,0:T(8,128)(2,1)S(1)}, u32[]{:S(2)}, u32[]{:S(2)}) collective-permute-start(bf16[32,32,128]{2,1,0:T(8,128)(2,1)S(1)} %get-tuple-element.49), channel_id=1, source_target_pairs={{0,96},{16,112},{32,0},{48,16},{64,32},{80,48},{96,64},{112,80},{1... | collective-permute-start | bytes 786440 | tf_op jit(solution)/shard_map/ppermute | solution.py:276
  95.5 1.1 %shard_map.74 = (f32[32,32,128]{2,1,0:T(8,128)S(1)}, bf16[16,32,128]{2,1,0:T(8,128)(2,1)S(1)}, bf16[16,32,128]{2,1,0:T(8,128)(2,1)S(1)}) custom-call(s32[384]{0:T(512)S(1)} %get-tuple-element.28.codes, s32[5]{0:T(128)S(1)} %pad_add_fusion.1.scal, bf16[384,128,128]{2,1,0:T(8,128)(2,1)S(1)} %get-tuple-element.34.tiles, bf16[192,32,128]{2,1,0:T(8,128)(2,1)S(1)} %bitcast.16), custom_call_target="tpu_custom_call" | custom-call | flops 68719476736 | bytes 67108864 | tf_op jit(solution)/shard_map/pallas_call | solution.py:230
  96.6 1.7 %collective-permute-start.10 = (bf16[16,32,128]{2,1,0:T(8,128)(2,1)S(1)}, bf16[16,32,128]{2,1,0:T(8,128)(2,1)S(1)}, u32[]{:S(2)}, u32[]{:S(2)}) collective-permute-start(bf16[16,32,128]{2,1,0:T(8,128)(2,1)S(1)} %get-tuple-element.52), channel_id=1, source_target_pairs={{0,16},{16,0},{32,48},{48,32},{64,80},{80,64},{96,112},{112,96},{1... | collective-permute-start | bytes 393224 | tf_op jit(solution)/shard_map/ppermute | solution.py:279
  98.4 0.9 collective-permute-done.10.rest_0_
  99.8 1.7 %collective-permute-done.8.one = bf16[32,32,128]{2,1,0:T(8,128)(2,1)S(1)} collective-permute-done((bf16[32,32,128]{2,1,0:T(8,128)(2,1)S(1)}, bf16[32,32,128]{2,1,0:T(8,128)(2,1)S(1)}, u32[]{:S(2)}, u32[]{:S(2)}) %collective-permute-start.8) | collective-permute-done | bytes 262176 | tf_op jit(solution)/shard_map/ppermute | solution.py:276
  101.7 7.4 %collective-permute-done.12.two = bf16[32,32,128]{2,1,0:T(8,128)(2,1)S(1)} collective-permute-done((bf16[32,32,128]{2,1,0:T(8,128)(2,1)S(1)}, bf16[32,32,128]{2,1,0:T(8,128)(2,1)S(1)}, u32[]{:S(2)}, u32[]{:S(2)}) %collective-permute-start.12) | collective-permute-done | bytes 262176 | tf_op jit(solution)/shard_map/ppermute | solution.py:276
  109.1 0.8 shard_map.76
  (39 shorter events, 4.3 us)
Async XLA Ops:
  0.6 9.2 %collective-permute-start.1 = (bf16[32,4096]{1,0:T(8,128)(2,1)}, bf16[32,4096]{1,0:T(8,128)(2,1)S(1)}, u32[]{:S(2)}, u32[]{:S(2)}) collective-permute-start(bf16[32,4096]{1,0:T(8,128)(2,1)} %bitcast.18), channel_id=1, source_target_pairs={{0,32},{16,48},{32,64},{48,80},{64,96},{80,112},{96,0},{112,16},{1... | collective-permute-start | bytes 786440 | tf_op jit(solution)/shard_map/ppermute | solution.py:276
  2.7 7.1 %collective-permute-start = (bf16[32,4096]{1,0:T(8,128)(2,1)}, bf16[32,4096]{1,0:T(8,128)(2,1)S(1)}, u32[]{:S(2)}, u32[]{:S(2)}) collective-permute-start(bf16[32,4096]{1,0:T(8,128)(2,1)} %bitcast.19), channel_id=1, source_target_pairs={{0,96},{16,112},{32,0},{48,16},{64,32},{80,48},{96,64},{112,80},{1... | collective-permute-start | bytes 786440 | tf_op jit(solution)/shard_map/ppermute | solution.py:276
  9.8 5.0 %collective-permute-start.4 = (bf16[32,4096]{1,0:T(8,128)(2,1)S(1)}, bf16[32,4096]{1,0:T(8,128)(2,1)S(1)}, u32[]{:S(2)}, u32[]{:S(2)}) collective-permute-start(bf16[32,4096]{1,0:T(8,128)(2,1)S(1)} %collective-permute-done.1.refs_2_), channel_id=1, source_target_pairs={{0,16},{16,0},{32,48},{48,32},{64,80},{80,64},{96,112},{112,96},{1... | collective-permute-start | bytes 786440 | tf_op jit(solution)/shard_map/ppermute | solution.py:279
  11.8 3.1 %collective-permute-start.2 = (bf16[32,4096]{1,0:T(8,128)(2,1)}, bf16[32,4096]{1,0:T(8,128)(2,1)S(1)}, u32[]{:S(2)}, u32[]{:S(2)}) collective-permute-start(bf16[32,4096]{1,0:T(8,128)(2,1)} %bitcast.20), channel_id=1, source_target_pairs={{0,16},{16,0},{32,48},{48,32},{64,80},{80,64},{96,112},{112,96},{1... | collective-permute-start | bytes 786440 | tf_op jit(solution)/shard_map/ppermute | solution.py:279
  11.9 3.0 %collective-permute-start.3 = (bf16[32,4096]{1,0:T(8,128)(2,1)S(1)}, bf16[32,4096]{1,0:T(8,128)(2,1)S(1)}, u32[]{:S(2)}, u32[]{:S(2)}) collective-permute-start(bf16[32,4096]{1,0:T(8,128)(2,1)S(1)} %collective-permute-done.refs_1_), channel_id=1, source_target_pairs={{0,16},{16,0},{32,48},{48,32},{64,80},{80,64},{96,112},{112,96},{1... | collective-permute-start | bytes 786440 | tf_op jit(solution)/shard_map/ppermute | solution.py:279
  12.3 8.2 %collective-permute-start.5 = (bf16[32,4096]{1,0:T(8,128)(2,1)S(1)}, bf16[32,4096]{1,0:T(8,128)(2,1)S(1)}, u32[]{:S(2)}, u32[]{:S(2)}) collective-permute-start(bf16[32,4096]{1,0:T(8,128)(2,1)S(1)} %collective-permute-done.refs_1_), channel_id=1, source_target_pairs={{0,96},{16,112},{32,0},{48,16},{64,32},{80,48},{96,64},{112,80},{1... | collective-permute-start | bytes 786440 | tf_op jit(solution)/shard_map/ppermute | solution.py:276
  14.9 8.7 %collective-permute-start.6 = (bf16[32,4096]{1,0:T(8,128)(2,1)S(1)}, bf16[32,4096]{1,0:T(8,128)(2,1)S(1)}, u32[]{:S(2)}, u32[]{:S(2)}) collective-permute-start(bf16[32,4096]{1,0:T(8,128)(2,1)S(1)} %collective-permute-done.4.refs_5_), channel_id=1, source_target_pairs={{0,32},{16,48},{32,64},{48,80},{64,96},{80,112},{96,0},{112,16},{1... | collective-permute-start | bytes 786440 | tf_op jit(solution)/shard_map/ppermute | solution.py:276
  85.0 7.6 %collective-permute-start.7 = (bf16[3,32,32,128]{3,2,1,0:T(8,128)(2,1)S(1)}, bf16[3,32,32,128]{3,2,1,0:T(8,128)(2,1)S(1)}, u32[]{:S(2)}, u32[]{:S(2)}) collective-permute-start(bf16[3,32,32,128]{3,2,1,0:T(8,128)(2,1)S(1)} %get-tuple-element.44), channel_id=1, source_target_pairs={{0,16},{16,0},{32,48},{48,32},{64,80},{80,64},{96,112},{112,96},{1... | collective-permute-start | bytes 2359304 | tf_op jit(solution)/shard_map/ppermute | solution.py:279
  92.7 8.8 %collective-permute-start.8 = (bf16[32,32,128]{2,1,0:T(8,128)(2,1)S(1)}, bf16[32,32,128]{2,1,0:T(8,128)(2,1)S(1)}, u32[]{:S(2)}, u32[]{:S(2)}) collective-permute-start(bf16[32,32,128]{2,1,0:T(8,128)(2,1)S(1)} %get-tuple-element.48), channel_id=1, source_target_pairs={{0,32},{16,48},{32,64},{48,80},{64,96},{80,112},{96,0},{112,16},{1... | collective-permute-start | bytes 786440 | tf_op jit(solution)/shard_map/ppermute | solution.py:276
  92.8 8.7 %collective-permute-start.9 = (bf16[32,32,128]{2,1,0:T(8,128)(2,1)S(1)}, bf16[32,32,128]{2,1,0:T(8,128)(2,1)S(1)}, u32[]{:S(2)}, u32[]{:S(2)}) collective-permute-start(bf16[32,32,128]{2,1,0:T(8,128)(2,1)S(1)} %get-tuple-element.49), channel_id=1, source_target_pairs={{0,96},{16,112},{32,0},{48,16},{64,32},{80,48},{96,64},{112,80},{1... | collective-permute-start | bytes 786440 | tf_op jit(solution)/shard_map/ppermute | solution.py:276
  96.6 2.7 %collective-permute-start.10 = (bf16[16,32,128]{2,1,0:T(8,128)(2,1)S(1)}, bf16[16,32,128]{2,1,0:T(8,128)(2,1)S(1)}, u32[]{:S(2)}, u32[]{:S(2)}) collective-permute-start(bf16[16,32,128]{2,1,0:T(8,128)(2,1)S(1)} %get-tuple-element.52), channel_id=1, source_target_pairs={{0,16},{16,0},{32,48},{48,32},{64,80},{80,64},{96,112},{112,96},{1... | collective-permute-start | bytes 393224 | tf_op jit(solution)/shard_map/ppermute | solution.py:279
  98.3 1.3 %collective-permute-start.11 = (bf16[16,32,128]{2,1,0:T(8,128)(2,1)S(1)}, bf16[16,32,128]{2,1,0:T(8,128)(2,1)S(1)}, u32[]{:S(2)}, u32[]{:S(2)}) collective-permute-start(bf16[16,32,128]{2,1,0:T(8,128)(2,1)S(1)} %get-tuple-element.53), channel_id=1, source_target_pairs={{0,16},{16,0},{32,48},{48,32},{64,80},{80,64},{96,112},{112,96},{1... | collective-permute-start | bytes 393224 | tf_op jit(solution)/shard_map/ppermute | solution.py:279
  99.7 9.3 %collective-permute-start.12 = (bf16[32,32,128]{2,1,0:T(8,128)(2,1)S(1)}, bf16[32,32,128]{2,1,0:T(8,128)(2,1)S(1)}, u32[]{:S(2)}, u32[]{:S(2)}) collective-permute-start(bf16[32,32,128]{2,1,0:T(8,128)(2,1)S(1)} %shard_map.75), channel_id=1, source_target_pairs={{0,64},{16,80},{32,96},{48,112},{64,0},{80,16},{96,32},{112,48},{1... | collective-permute-start | bytes 786440 | tf_op jit(solution)/shard_map/ppermute | solution.py:276

commit v5 on v4

--- a/solution.py
+++ b/solution.py
@@ -12,7 +12,7 @@
 N_COL = 16
 N_X = 4
 RUN_ROWS = CAP * K
-PAY_ROWS = RUN_ROWS + 16
+PAY_ROWS = RUN_ROWS + 8
 N_NAMED = N_COL * CAP
 GROUP = 32
 CHUNK = 32
@@ -28,6 +28,11 @@
 
 def in_hbm(value):
     return pltpu.with_memory_space_constraint(value, pltpu.HBM)
+
+
+def image_kernel(blocks, image):
+    for b in range(SHARE):
+        image[:, b * TILE:(b + 1) * TILE] = blocks[b]
 
 
 def code_parts(code):
@@ -121,7 +126,7 @@
     lax.fori_loop(0, N_COL, pack, 0)
 
 
-def reduce_kernel(recv, image, send, total, blocks, wide_ids, ids, sem):
+def reduce_kernel(recv, blocks, send, total, wide_ids, ids, sem):
     for c in range(N_COL):
         wide_ids[c:c + 1] = recv[c, RUN_ROWS:][0:1].astype(jnp.float32).astype(jnp.int32)
     copy = pltpu.make_async_copy(wide_ids, ids, sem)
@@ -131,22 +136,22 @@
     copy.wait()
 
     def add(c, _):
-        for q in range(CAP):
-            total[ids[c, q]] += recv[c, q * K:(q + 1) * K].astype(jnp.float32)
+        spots = [ids[c, q] for q in range(CAP)]
+        sums = [total[p] + recv[c, q * K:(q + 1) * K].astype(jnp.float32) for q, p in enumerate(spots)]
+        for p, value in zip(spots, sums):
+            total[p] = value
         return 0
 
     lax.fori_loop(0, N_COL, add, 0)
     for b in range(SHARE):
-        block = total[b].astype(jnp.bfloat16)
-        blocks[b] = block
-        image[:, b * TILE:(b + 1) * TILE] = block
+        blocks[b] = total[b].astype(jnp.bfloat16)
 
     def spread(c, _):
         for q in range(CAP):
             send[c, q * K:(q + 1) * K] = blocks[ids[c, q]]
         return 0
 
-    lax.fori_loop(0, N_COL, spread, 0)
+    lax.fori_loop(0, N_COL, spread, 0, unroll=4)
 
 
 def backward_spots(blocks):
@@ -286,7 +291,7 @@
     scal = jnp.stack([live, x, core, counts[0], counts[1]]).astype(jnp.int32)
     near_codes, far_codes = codes[0], codes[1]
     lanes = jnp.pad(ids, ((0, 0), (0, TILE - CAP))).astype(bf16)
-    id_rows = jnp.broadcast_to(lanes[:, None, :], (N_COL, 16, TILE))
+    id_rows = jnp.broadcast_to(lanes[:, None, :], (N_COL, 8, TILE))
     near, near_codes, far_codes, id_rows, scal = lax.optimization_barrier(
         (near, near_codes, far_codes, id_rows, scal)
     )
@@ -316,19 +321,19 @@
         aliases={6: 1},
     )
     recv = lax.all_to_all(send, "col", 0, 0, tiled=True)
-    image, spread = call(
+    blocks, spread = call(
         reduce_kernel,
-        [shape((K, SHARE * TILE), bf16), shape((N_COL, RUN_ROWS, TILE), bf16)],
+        [shape((SHARE, K, TILE), bf16), shape((N_COL, RUN_ROWS, TILE), bf16)],
         [],
         [recv],
         [
             pltpu.VMEM((SHARE, K, TILE), f32),
-            pltpu.VMEM((SHARE, K, TILE), bf16),
             pltpu.VMEM((N_COL, TILE), jnp.int32),
             pltpu.SMEM((N_COL, TILE), jnp.int32),
             pltpu.SemaphoreType.DMA,
         ],
     )
+    image = call(image_kernel, shape((K, SHARE * TILE), bf16), [], [blocks])
     named = lax.all_to_all(spread, "col", 0, 0, tiled=True).reshape(N_NAMED, K, TILE)
 
     block = (SHARE, K, TILE)

time: 109 us -> 106 us (0.972)
  starting transfers between devices: 18.8 us -> 16.1 us
  Pallas kernels: 11.9 us -> 14.4 us
  waiting for transfers between devices: 17.9 us -> 16.2 us
    ppermute x6, starting transfers between devices: 9.93 us -> 7.2 us  [swap_core(): return lax.ppermute(value, 'row', [(i, i ^ 1) for i in range(8)])]
    pallas_call x9 -> x10, Pallas kernels: 11.9 us -> 14.4 us  [call(): pl.pallas_call(kernel, out_shape=outs, in_specs=specs, out_specs=spec_vme...]
  transfers between devices with their start and end apart: 13 -> 13, of which waited for: 8 -> 8; matrix products, arithmetic and copies ran while one was open for 4% -> 4% of each run, Pallas kernels for 5% -> 7%
where the time goes in v5:
time: 106 us; the launch traced here: 107 us
  blocking collectives  54.4 us (51%)
  waiting for transfers between devices  16.2 us (15%)
  starting transfers between devices  16.1 us (15%)
  Pallas kernels  14.4 us (14%)
  other arithmetic  3.96 us (4%)
  between operations  1.45 us (1%)
    all_to_all x1, blocking collectives, per_device(): recv = lax.all_to_all(send, 'col', 0, 0, tiled=True)  30.5 us
    all_to_all x1, blocking collectives, per_device(): lax.all_to_all(spread, 'col', 0, 0, tiled=True).reshape(N_NAMED, K, TILE)  24 us
    pallas_call x10, Pallas kernels, call(): pl.pallas_call(kernel, out_shape=outs, in_specs=specs, out_specs=spec_vme...  14.4 us
    ppermute x7, waiting for transfers between devices, along_x(): return lax.ppermute(value, 'row', [(i, (i + 2 * d) % 8) for i in range(8)])  13.7 us
    ppermute x7, starting transfers between devices, along_x(): return lax.ppermute(value, 'row', [(i, (i + 2 * d) % 8) for i in range(8)])  8.86 us
    ppermute x6, starting transfers between devices, swap_core(): return lax.ppermute(value, 'row', [(i, i ^ 1) for i in range(8)])  7.2 us
    ppermute x6, waiting for transfers between devices, swap_core(): return lax.ppermute(value, 'row', [(i, i ^ 1) for i in range(8)])  2.43 us
  transfers between devices with their start and end apart: 13, of which 8 were waited for; matrix products, arithmetic and copies ran while one was open for 4% of the time, Pallas kernels for 7%

profile of v5, /device:TPU:1, one launch (start us, length us, event | category | flops | bytes accessed | tf_op | source)
XLA Modules:
  0.0 106.7 jit_solution(12256284257603590924)
XLA Ops:
  0.6 2.1 %collective-permute-start.1 = (bf16[32,4096]{1,0:T(8,128)(2,1)}, bf16[32,4096]{1,0:T(8,128)(2,1)S(1)}, u32[]{:S(2)}, u32[]{:S(2)}) collective-permute-start(bf16[32,4096]{1,0:T(8,128)(2,1)} %bitcast.18), channel_id=1, source_target_pairs={{0,32},{16,48},{32,64},{48,80},{64,96},{80,112},{96,0},{112,16},{1... | collective-permute-start | bytes 786440 | tf_op jit(solution)/shard_map/ppermute | solution.py:281
  2.7 1.4 %collective-permute-start = (bf16[32,4096]{1,0:T(8,128)(2,1)}, bf16[32,4096]{1,0:T(8,128)(2,1)S(1)}, u32[]{:S(2)}, u32[]{:S(2)}) collective-permute-start(bf16[32,4096]{1,0:T(8,128)(2,1)} %bitcast.19), channel_id=1, source_target_pairs={{0,96},{16,112},{32,0},{48,16},{64,32},{80,48},{96,64},{112,80},{1... | collective-permute-start | bytes 786440 | tf_op jit(solution)/shard_map/ppermute | solution.py:281
  4.8 0.7 reduce
  5.7 0.7 shift-left_reduce_fusion
  9.0 0.8 collective-permute-done.1.refs_2_
  9.8 1.9 %collective-permute-start.4 = (bf16[32,4096]{1,0:T(8,128)(2,1)S(1)}, bf16[32,4096]{1,0:T(8,128)(2,1)S(1)}, u32[]{:S(2)}, u32[]{:S(2)}) collective-permute-start(bf16[32,4096]{1,0:T(8,128)(2,1)S(1)} %collective-permute-done.1.refs_2_), channel_id=1, source_target_pairs={{0,16},{16,0},{32,48},{48,32},{64,80},{80,64},{96,112},{112,96},{1... | collective-permute-start | bytes 786440 | tf_op jit(solution)/shard_map/ppermute | solution.py:284
  12.3 2.6 %collective-permute-start.5 = (bf16[32,4096]{1,0:T(8,128)(2,1)S(1)}, bf16[32,4096]{1,0:T(8,128)(2,1)S(1)}, u32[]{:S(2)}, u32[]{:S(2)}) collective-permute-start(bf16[32,4096]{1,0:T(8,128)(2,1)S(1)} %collective-permute-done.refs_1_), channel_id=1, source_target_pairs={{0,96},{16,112},{32,0},{48,16},{64,32},{80,48},{96,64},{112,80},{1... | collective-permute-start | bytes 786440 | tf_op jit(solution)/shard_map/ppermute | solution.py:281
  14.9 4.9 %shard_map.68 = (f32[193,32,128]{2,1,0:T(8,128)S(1)}, bf16[384,128,128]{2,1,0:T(8,128)(2,1)S(1)}) custom-call(s32[384]{0:T(512)S(1)} %get-tuple-element.30.codes, s32[5]{0:T(128)S(1)} %pad_add_fusion.1.scal, bf16[384,128,128]{2,1,0:T(8,128)(2,1)} %bitcast.17, bf16[32,4096]{1,0:T(8,128)(2,1)} %bitcast.21, bf16[32,4096]{1,0:T(8,128)(2,1)S(1)} %collective-permute-done.refs_1_, ...), custom_call_target="tpu_custom_call" | custom-call | tf_op jit(solution)/shard_map/pallas_call | solution.py:235
  19.7 0.8 collective-permute-done.5.here
  20.5 3.1 %collective-permute-done.6.there = bf16[32,4096]{1,0:T(8,128)(2,1)S(1)} collective-permute-done((bf16[32,4096]{1,0:T(8,128)(2,1)S(1)}, bf16[32,4096]{1,0:T(8,128)(2,1)S(1)}, u32[]{:S(2)}, u32[]{:S(2)}) %collective-permute-start.6) | collective-permute-done | bytes 262176 | tf_op jit(solution)/shard_map/ppermute | solution.py:281
  23.6 1.9 %shard_map.69 = (bf16[16,392,128]{2,1,0:T(8,128)(2,1)S(1)}, f32[193,32,128]{2,1,0:T(8,128)S(1)}) custom-call(s32[384]{0:T(512)S(1)} %get-tuple-element.28.codes, s32[5]{0:T(128)S(1)} %pad_add_fusion.1.scal, bf16[384,128,128]{2,1,0:T(8,128)(2,1)S(1)} %get-tuple-element.34.tiles, ...), custom_call_target="tpu_custom_call", output_to_operand_aliasing={{1}: (6, {})} | custom-call | tf_op jit(solution)/shard_map/pallas_call | solution.py:235
  25.5 30.5 %all_to_all.10.recv = bf16[16,392,128]{2,1,0:T(8,128)(2,1)S(1)} all-to-all(bf16[16,392,128]{2,1,0:T(8,128)(2,1)S(1)} %get-tuple-element.40), channel_id=1, replica_groups=mesh['row'=8,'col'=16] {'col'}, dimensions={0} | all-to-all | bytes 3211264 | tf_op jit(solution)/shard_map/all_to_all | solution.py:323
  56.0 1.5 %shard_map.70 = (bf16[32,32,128]{2,1,0:T(8,128)(2,1)S(1)}, bf16[16,384,128]{2,1,0:T(8,128)(2,1)S(1)}) custom-call(bf16[16,392,128]{2,1,0:T(8,128)(2,1)S(1)} %all_to_all.10.recv), custom_call_target="tpu_custom_call" | custom-call | tf_op jit(solution)/shard_map/pallas_call | solution.py:235
  57.5 24.0 %all_to_all.11 = bf16[16,384,128]{2,1,0:T(8,128)(2,1)S(1)} all-to-all(bf16[16,384,128]{2,1,0:T(8,128)(2,1)S(1)} %get-tuple-element.42), channel_id=1, replica_groups=mesh['row'=8,'col'=16] {'col'}, dimensions={0} | all-to-all | bytes 3145728 | tf_op jit(solution)/shard_map/all_to_all | solution.py:337
  81.5 2.8 %shard_map.72 = (f32[3,32,32,128]{3,2,1,0:T(8,128)S(1)}, bf16[3,32,32,128]{3,2,1,0:T(8,128)(2,1)S(1)}) custom-call(s32[384]{0:T(512)S(1)} %get-tuple-element.30.codes, s32[5]{0:T(128)S(1)} %pad_add_fusion.1.scal, bf16[384,128,128]{2,1,0:T(8,128)(2,1)S(1)} %get-tuple-element.34.tiles, bf16[192,32,128]{2,1,0:T(8,128)(2,1)S(1)} %bitcast.15), custom_call_target="tpu_custom_call" | custom-call | tf_op jit(solution)/shard_map/pallas_call | solution.py:235
  84.3 3.7 %collective-permute-start.7 = (bf16[3,32,32,128]{3,2,1,0:T(8,128)(2,1)S(1)}, bf16[3,32,32,128]{3,2,1,0:T(8,128)(2,1)S(1)}, u32[]{:S(2)}, u32[]{:S(2)}) collective-permute-start(bf16[3,32,32,128]{3,2,1,0:T(8,128)(2,1)S(1)} %get-tuple-element.44), channel_id=1, source_target_pairs={{0,16},{16,0},{32,48},{48,32},{64,80},{80,64},{96,112},{112,96},{1... | collective-permute-start | bytes 2359304 | tf_op jit(solution)/shard_map/ppermute | solution.py:284
  87.9 1.9 %collective-permute-done.7.got = bf16[3,32,32,128]{3,2,1,0:T(8,128)(2,1)S(1)} collective-permute-done((bf16[3,32,32,128]{3,2,1,0:T(8,128)(2,1)S(1)}, bf16[3,32,32,128]{3,2,1,0:T(8,128)(2,1)S(1)}, u32[]{:S(2)}, u32[]{:S(2)}) %collective-permute-start.7) | collective-permute-done | bytes 786464 | tf_op jit(solution)/shard_map/ppermute | solution.py:284
  90.1 2.7 %collective-permute-start.9 = (bf16[32,32,128]{2,1,0:T(8,128)(2,1)S(1)}, bf16[32,32,128]{2,1,0:T(8,128)(2,1)S(1)}, u32[]{:S(2)}, u32[]{:S(2)}) collective-permute-start(bf16[32,32,128]{2,1,0:T(8,128)(2,1)S(1)} %get-tuple-element.49), channel_id=1, source_target_pairs={{0,96},{16,112},{32,0},{48,16},{64,32},{80,48},{96,64},{112,80},{1... | collective-permute-start | bytes 786440 | tf_op jit(solution)/shard_map/ppermute | solution.py:281
  92.8 1.5 %shard_map.75 = (f32[32,32,128]{2,1,0:T(8,128)S(1)}, bf16[16,32,128]{2,1,0:T(8,128)(2,1)S(1)}, bf16[16,32,128]{2,1,0:T(8,128)(2,1)S(1)}) custom-call(s32[384]{0:T(512)S(1)} %get-tuple-element.28.codes, s32[5]{0:T(128)S(1)} %pad_add_fusion.1.scal, bf16[384,128,128]{2,1,0:T(8,128)(2,1)S(1)} %get-tuple-element.34.tiles, bf16[192,32,128]{2,1,0:T(8,128)(2,1)S(1)} %bitcast.16), custom_call_target="tpu_custom_call" | custom-call | flops 68719476736 | bytes 67108864 | tf_op jit(solution)/shard_map/pallas_call | solution.py:235
  94.2 1.0 collective-permute-start.10
  95.3 0.7 shard_map.71
  96.8 2.0 %collective-permute-done.8.one = bf16[32,32,128]{2,1,0:T(8,128)(2,1)S(1)} collective-permute-done((bf16[32,32,128]{2,1,0:T(8,128)(2,1)S(1)}, bf16[32,32,128]{2,1,0:T(8,128)(2,1)S(1)}, u32[]{:S(2)}, u32[]{:S(2)}) %collective-permute-start.8) | collective-permute-done | bytes 262176 | tf_op jit(solution)/shard_map/ppermute | solution.py:281
  98.9 7.1 %collective-permute-done.12.two = bf16[32,32,128]{2,1,0:T(8,128)(2,1)S(1)} collective-permute-done((bf16[32,32,128]{2,1,0:T(8,128)(2,1)S(1)}, bf16[32,32,128]{2,1,0:T(8,128)(2,1)S(1)}, u32[]{:S(2)}, u32[]{:S(2)}) %collective-permute-start.12) | collective-permute-done | bytes 262176 | tf_op jit(solution)/shard_map/ppermute | solution.py:281
  106.0 0.8 shard_map.77
  (40 shorter events, 4.5 us)
Async XLA Ops:
  0.6 9.2 %collective-permute-start.1 = (bf16[32,4096]{1,0:T(8,128)(2,1)}, bf16[32,4096]{1,0:T(8,128)(2,1)S(1)}, u32[]{:S(2)}, u32[]{:S(2)}) collective-permute-start(bf16[32,4096]{1,0:T(8,128)(2,1)} %bitcast.18), channel_id=1, source_target_pairs={{0,32},{16,48},{32,64},{48,80},{64,96},{80,112},{96,0},{112,16},{1... | collective-permute-start | bytes 786440 | tf_op jit(solution)/shard_map/ppermute | solution.py:281
  2.7 7.1 %collective-permute-start = (bf16[32,4096]{1,0:T(8,128)(2,1)}, bf16[32,4096]{1,0:T(8,128)(2,1)S(1)}, u32[]{:S(2)}, u32[]{:S(2)}) collective-permute-start(bf16[32,4096]{1,0:T(8,128)(2,1)} %bitcast.19), channel_id=1, source_target_pairs={{0,96},{16,112},{32,0},{48,16},{64,32},{80,48},{96,64},{112,80},{1... | collective-permute-start | bytes 786440 | tf_op jit(solution)/shard_map/ppermute | solution.py:281
  9.8 5.0 %collective-permute-start.4 = (bf16[32,4096]{1,0:T(8,128)(2,1)S(1)}, bf16[32,4096]{1,0:T(8,128)(2,1)S(1)}, u32[]{:S(2)}, u32[]{:S(2)}) collective-permute-start(bf16[32,4096]{1,0:T(8,128)(2,1)S(1)} %collective-permute-done.1.refs_2_), channel_id=1, source_target_pairs={{0,16},{16,0},{32,48},{48,32},{64,80},{80,64},{96,112},{112,96},{1... | collective-permute-start | bytes 786440 | tf_op jit(solution)/shard_map/ppermute | solution.py:284
  11.8 3.1 %collective-permute-start.2 = (bf16[32,4096]{1,0:T(8,128)(2,1)}, bf16[32,4096]{1,0:T(8,128)(2,1)S(1)}, u32[]{:S(2)}, u32[]{:S(2)}) collective-permute-start(bf16[32,4096]{1,0:T(8,128)(2,1)} %bitcast.20), channel_id=1, source_target_pairs={{0,16},{16,0},{32,48},{48,32},{64,80},{80,64},{96,112},{112,96},{1... | collective-permute-start | bytes 786440 | tf_op jit(solution)/shard_map/ppermute | solution.py:284
  11.8 3.0 %collective-permute-start.3 = (bf16[32,4096]{1,0:T(8,128)(2,1)S(1)}, bf16[32,4096]{1,0:T(8,128)(2,1)S(1)}, u32[]{:S(2)}, u32[]{:S(2)}) collective-permute-start(bf16[32,4096]{1,0:T(8,128)(2,1)S(1)} %collective-permute-done.refs_1_), channel_id=1, source_target_pairs={{0,16},{16,0},{32,48},{48,32},{64,80},{80,64},{96,112},{112,96},{1... | collective-permute-start | bytes 786440 | tf_op jit(solution)/shard_map/ppermute | solution.py:284
  12.3 8.2 %collective-permute-start.5 = (bf16[32,4096]{1,0:T(8,128)(2,1)S(1)}, bf16[32,4096]{1,0:T(8,128)(2,1)S(1)}, u32[]{:S(2)}, u32[]{:S(2)}) collective-permute-start(bf16[32,4096]{1,0:T(8,128)(2,1)S(1)} %collective-permute-done.refs_1_), channel_id=1, source_target_pairs={{0,96},{16,112},{32,0},{48,16},{64,32},{80,48},{96,64},{112,80},{1... | collective-permute-start | bytes 786440 | tf_op jit(solution)/shard_map/ppermute | solution.py:281
  14.8 8.7 %collective-permute-start.6 = (bf16[32,4096]{1,0:T(8,128)(2,1)S(1)}, bf16[32,4096]{1,0:T(8,128)(2,1)S(1)}, u32[]{:S(2)}, u32[]{:S(2)}) collective-permute-start(bf16[32,4096]{1,0:T(8,128)(2,1)S(1)} %collective-permute-done.4.refs_5_), channel_id=1, source_target_pairs={{0,32},{16,48},{32,64},{48,80},{64,96},{80,112},{96,0},{112,16},{1... | collective-permute-start | bytes 786440 | tf_op jit(solution)/shard_map/ppermute | solution.py:281
  84.3 5.6 %collective-permute-start.7 = (bf16[3,32,32,128]{3,2,1,0:T(8,128)(2,1)S(1)}, bf16[3,32,32,128]{3,2,1,0:T(8,128)(2,1)S(1)}, u32[]{:S(2)}, u32[]{:S(2)}) collective-permute-start(bf16[3,32,32,128]{3,2,1,0:T(8,128)(2,1)S(1)} %get-tuple-element.44), channel_id=1, source_target_pairs={{0,16},{16,0},{32,48},{48,32},{64,80},{80,64},{96,112},{112,96},{1... | collective-permute-start | bytes 2359304 | tf_op jit(solution)/shard_map/ppermute | solution.py:284
  90.0 8.8 %collective-permute-start.8 = (bf16[32,32,128]{2,1,0:T(8,128)(2,1)S(1)}, bf16[32,32,128]{2,1,0:T(8,128)(2,1)S(1)}, u32[]{:S(2)}, u32[]{:S(2)}) collective-permute-start(bf16[32,32,128]{2,1,0:T(8,128)(2,1)S(1)} %get-tuple-element.48), channel_id=1, source_target_pairs={{0,32},{16,48},{32,64},{48,80},{64,96},{80,112},{96,0},{112,16},{1... | collective-permute-start | bytes 786440 | tf_op jit(solution)/shard_map/ppermute | solution.py:281
  90.1 8.7 %collective-permute-start.9 = (bf16[32,32,128]{2,1,0:T(8,128)(2,1)S(1)}, bf16[32,32,128]{2,1,0:T(8,128)(2,1)S(1)}, u32[]{:S(2)}, u32[]{:S(2)}) collective-permute-start(bf16[32,32,128]{2,1,0:T(8,128)(2,1)S(1)} %get-tuple-element.49), channel_id=1, source_target_pairs={{0,96},{16,112},{32,0},{48,16},{64,32},{80,48},{96,64},{112,80},{1... | collective-permute-start | bytes 786440 | tf_op jit(solution)/shard_map/ppermute | solution.py:281
  94.2 2.0 %collective-permute-start.10 = (bf16[16,32,128]{2,1,0:T(8,128)(2,1)S(1)}, bf16[16,32,128]{2,1,0:T(8,128)(2,1)S(1)}, u32[]{:S(2)}, u32[]{:S(2)}) collective-permute-start(bf16[16,32,128]{2,1,0:T(8,128)(2,1)S(1)} %get-tuple-element.52), channel_id=1, source_target_pairs={{0,16},{16,0},{32,48},{48,32},{64,80},{80,64},{96,112},{112,96},{1... | collective-permute-start | bytes 393224 | tf_op jit(solution)/shard_map/ppermute | solution.py:284
  95.2 1.3 %collective-permute-start.11 = (bf16[16,32,128]{2,1,0:T(8,128)(2,1)S(1)}, bf16[16,32,128]{2,1,0:T(8,128)(2,1)S(1)}, u32[]{:S(2)}, u32[]{:S(2)}) collective-permute-start(bf16[16,32,128]{2,1,0:T(8,128)(2,1)S(1)} %get-tuple-element.53), channel_id=1, source_target_pairs={{0,16},{16,0},{32,48},{48,32},{64,80},{80,64},{96,112},{112,96},{1... | collective-permute-start | bytes 393224 | tf_op jit(solution)/shard_map/ppermute | solution.py:284
  96.7 9.3 %collective-permute-start.12 = (bf16[32,32,128]{2,1,0:T(8,128)(2,1)S(1)}, bf16[32,32,128]{2,1,0:T(8,128)(2,1)S(1)}, u32[]{:S(2)}, u32[]{:S(2)}) collective-permute-start(bf16[32,32,128]{2,1,0:T(8,128)(2,1)S(1)} %shard_map.76), channel_id=1, source_target_pairs={{0,64},{16,80},{32,96},{48,112},{64,0},{80,16},{96,32},{112,48},{1... | collective-permute-start | bytes 786440 | tf_op jit(solution)/shard_map/ppermute | solution.py:281

commit v6 on v5

--- a/solution.py
+++ b/solution.py
@@ -98,13 +98,18 @@
     fetch.start()
     lax.fori_loop(0, chunks, start, 0)
     clear_blocks(total, N_NAMED)
-    fetch.wait()
+
+    def load(i, d, other):
+        first = (((x + d) % N_X) * 2 + (core + other) % 2) * SHARE
+        for b in range(SHARE):
+            vec[first + b] = pieces[i + 3 * other][:, b * TILE:(b + 1) * TILE]
+
     for i, d in enumerate(NEAR):
         for other in range(2):
-            piece = pieces[i + 3 * other]
-            first = (((x + d) % N_X) * 2 + (core + other) % 2) * SHARE
-            for b in range(SHARE):
-                vec[first + b] = piece[:, b * TILE:(b + 1) * TILE]
+            if i + other:
+                load(i, d, other)
+    fetch.wait()
+    load(0, 0, 0)
     seen = sweep(scal[3], codes, held, vec, total, forward_spots(2 * N_X * SHARE), 1, ready)
     lax.fori_loop(seen, chunks, wait, 0)
 
@@ -123,7 +128,7 @@
         send[c, RUN_ROWS:] = ids[c]
         return 0
 
-    lax.fori_loop(0, N_COL, pack, 0)
+    lax.fori_loop(0, N_COL, pack, 0, unroll=4)
 
 
 def reduce_kernel(recv, blocks, send, total, wide_ids, ids, sem):
@@ -158,7 +163,7 @@
     return lambda slot, row, col, spare: (slot, row, (col & (blocks - 1)) + blocks * spare)
 
 
-def backward_near_kernel(codes, scal, tiles, recv, keep, give, total):
+def backward_near_kernel(codes, scal, tiles, recv, keep, give, give_own, total):
     x, core = scal[1], scal[2]
     for d in NEAR:
         clear_blocks(total.at[pl.ds(((x + d) % N_X) * 2 * SHARE, 2 * SHARE)], 2 * SHARE)
@@ -168,7 +173,11 @@
         for i, d in enumerate(NEAR):
             first = ((x + d) % N_X) * 2 * SHARE + b
             keep[i, b] = total[first + core * SHARE]
-            give[i, b] = total[first + (1 - core) * SHARE].astype(give.dtype)
+            swap = total[first + (1 - core) * SHARE].astype(give.dtype)
+            if i:
+                give[i - 1, b] = swap
+            else:
+                give_own[b] = swap
         return 0
 
     lax.fori_loop(0, SHARE, split, 0, unroll=4)
@@ -190,10 +199,10 @@
     lax.fori_loop(0, part, split, 0, unroll=2)
 
 
-def near_pair_kernel(keep, got, own, one, three):
+def side_pair_kernel(keep, got, one, three):
     def step(b, _):
-        for i, out in enumerate((own, one, three)):
-            out[b] = (keep[i, b] + got[i, b].astype(jnp.float32)).astype(out.dtype)
+        for i, out in enumerate((one, three)):
+            out[b] = (keep[i + 1, b] + got[i, b].astype(jnp.float32)).astype(out.dtype)
         return 0
 
     lax.fori_loop(0, SHARE, step, 0, unroll=4)
@@ -211,9 +220,14 @@
     lax.fori_loop(0, part, step, 0, unroll=2)
 
 
-def near_sum_kernel(own, one, three, out):
+def near_sum_kernel(keep, got, one, three, out):
     def step(b, _):
-        out[b] = own[b] + one[b].astype(jnp.float32) + three[b].astype(jnp.float32)
+        out[b] = (
+            keep[0, b]
+            + got[b].astype(jnp.float32)
+            + one[b].astype(jnp.float32)
+            + three[b].astype(jnp.float32)
+        )
         return 0
 
     lax.fori_loop(0, SHARE, step, 0, unroll=4)
@@ -292,11 +306,12 @@
     near_codes, far_codes = codes[0], codes[1]
     lanes = jnp.pad(ids, ((0, 0), (0, TILE - CAP))).astype(bf16)
     id_rows = jnp.broadcast_to(lanes[:, None, :], (N_COL, 8, TILE))
-    near, near_codes, far_codes, id_rows, scal = lax.optimization_barrier(
-        (near, near_codes, far_codes, id_rows, scal)
-    )
-
-    swapped = [swap_core(v) for v in near]
+    there = swap_core(mine)
+    near, there, near_codes, far_codes, id_rows, scal = lax.optimization_barrier(
+        (near, there, near_codes, far_codes, id_rows, scal)
+    )
+
+    swapped = [there] + [swap_core(v) for v in near[1:]]
     far = along_x(near[1], -1)
     begun, held = call(
         forward_near_kernel,
@@ -338,14 +353,14 @@
 
     block = (SHARE, K, TILE)
     wide, narrow = shape(block, f32), shape(block, bf16)
-    keep, give = call(
+    near_keep, give, give_own = call(
         backward_near_kernel,
-        [shape((3,) + block, f32), shape((3,) + block, bf16)],
+        [shape((3,) + block, f32), shape((2,) + block, bf16), narrow],
         [near_codes, scal],
         [held, named],
         [pltpu.VMEM((2 * N_X * SHARE + 1, K, TILE), f32)],
     )
-    own, one, three = call(near_pair_kernel, [wide, narrow, narrow], [], [keep, swap_core(give)])
+    one, three = call(side_pair_kernel, [narrow, narrow], [], [near_keep, swap_core(give)])
     one, three, named = lax.optimization_barrier((one, three, named))
     one, three = along_x(one, 1), along_x(three, -1)
     keep, *gives = call(
@@ -358,7 +373,7 @@
     )
     away = call(far_pair_kernel, narrow, [], [keep] + [swap_core(v) for v in gives])
     two = along_x(away, 2)
-    begun = call(near_sum_kernel, wide, [], [own, one, three], cost=LONG)
+    begun = call(near_sum_kernel, wide, [], [near_keep, swap_core(give_own), one, three], cost=LONG)
     back = call(final_kernel, shape((K, SHARE * TILE), bf16), [], [begun, two])
     return image, back.reshape(vectors.shape)
 

time: 106 us -> 106 us (level)
  blocking collectives: 54.4 us -> 52.3 us
  starting transfers between devices: 16.1 us -> 17.2 us
    ppermute x6 -> x7, starting transfers between devices: 7.2 us -> 9.11 us  [swap_core(): return lax.ppermute(value, 'row', [(i, i ^ 1) for i in range(8)])]
    all_to_all x1, blocking collectives: 24 us -> 22.3 us  [per_device(): lax.all_to_all(spread, 'col', 0, 0, tiled=True).reshape(N_NAMED, K, TILE)]
    ppermute x6 -> x7, waiting for transfers between devices: 2.43 us -> 1.96 us  [swap_core(): return lax.ppermute(value, 'row', [(i, i ^ 1) for i in range(8)])]
  transfers between devices with their start and end apart: 13 -> 14, of which waited for: 8 -> 7; matrix products, arithmetic and copies ran while one was open for 4% -> 4% of each run, Pallas kernels for 7% -> 8%
where the time goes in v6:
time: 106 us
  blocking collectives  52.3 us (49%)
  starting transfers between devices  17.2 us (16%)
  waiting for transfers between devices  15.6 us (15%)
  Pallas kernels  15.2 us (14%)
  other arithmetic  3.96 us (4%)
  between operations  1.46 us (1%)
    all_to_all x1, blocking collectives, per_device(): recv = lax.all_to_all(send, 'col', 0, 0, tiled=True)  29.9 us
    all_to_all x1, blocking collectives, per_device(): lax.all_to_all(spread, 'col', 0, 0, tiled=True).reshape(N_NAMED, K, TILE)  22.3 us
    pallas_call x10, Pallas kernels, call(): pl.pallas_call(kernel, out_shape=outs, in_specs=specs, out_specs=spec_vme...  15.2 us
    ppermute x7, waiting for transfers between devices, along_x(): return lax.ppermute(value, 'row', [(i, (i + 2 * d) % 8) for i in range(8)])  13.7 us
    ppermute x7, starting transfers between devices, swap_core(): return lax.ppermute(value, 'row', [(i, i ^ 1) for i in range(8)])  9.11 us
    ppermute x7, starting transfers between devices, along_x(): return lax.ppermute(value, 'row', [(i, (i + 2 * d) % 8) for i in range(8)])  8.11 us
  transfers between devices with their start and end apart: 14, of which 7 were waited for; matrix products, arithmetic and copies ran while one was open for 4% of the time, Pallas kernels for 8%

profile of v6, /device:TPU:1, one launch (start us, length us, event | category | flops | bytes accessed | tf_op | source)
XLA Modules:
  0.0 106.0 jit_solution(2897770962669403344)
XLA Ops:
  0.6 1.5 %collective-permute-start.2 = (bf16[32,4096]{1,0:T(8,128)(2,1)}, bf16[32,4096]{1,0:T(8,128)(2,1)S(1)}, u32[]{:S(2)}, u32[]{:S(2)}) collective-permute-start(bf16[32,4096]{1,0:T(8,128)(2,1)} %bitcast.18), channel_id=1, source_target_pairs={{0,16},{16,0},{32,48},{48,32},{64,80},{80,64},{96,112},{112,96},{1... | collective-permute-start | bytes 786440 | tf_op jit(solution)/shard_map/ppermute | solution.py:298
  2.1 1.3 %collective-permute-start.1 = (bf16[32,4096]{1,0:T(8,128)(2,1)}, bf16[32,4096]{1,0:T(8,128)(2,1)S(1)}, u32[]{:S(2)}, u32[]{:S(2)}) collective-permute-start(bf16[32,4096]{1,0:T(8,128)(2,1)} %bitcast.19), channel_id=1, source_target_pairs={{0,32},{16,48},{32,64},{48,80},{64,96},{80,112},{96,0},{112,16},{1... | collective-permute-start | bytes 786440 | tf_op jit(solution)/shard_map/ppermute | solution.py:295
  3.4 1.4 %collective-permute-start = (bf16[32,4096]{1,0:T(8,128)(2,1)}, bf16[32,4096]{1,0:T(8,128)(2,1)S(1)}, u32[]{:S(2)}, u32[]{:S(2)}) collective-permute-start(bf16[32,4096]{1,0:T(8,128)(2,1)} %bitcast.20), channel_id=1, source_target_pairs={{0,96},{16,112},{32,0},{48,16},{64,32},{80,48},{96,64},{112,80},{1... | collective-permute-start | bytes 786440 | tf_op jit(solution)/shard_map/ppermute | solution.py:295
  5.5 0.7 reduce
  6.4 0.7 shift-left_reduce_fusion
  9.8 1.6 %collective-permute-done.1.refs_2_ = bf16[32,4096]{1,0:T(8,128)(2,1)S(1)} collective-permute-done((bf16[32,4096]{1,0:T(8,128)(2,1)}, bf16[32,4096]{1,0:T(8,128)(2,1)S(1)}, u32[]{:S(2)}, u32[]{:S(2)}) %collective-permute-start.1) | collective-permute-done | bytes 262176 | tf_op jit(solution)/shard_map/ppermute | solution.py:295
  11.4 1.0 collective-permute-start.4
  12.5 2.6 %collective-permute-start.5 = (bf16[32,4096]{1,0:T(8,128)(2,1)S(1)}, bf16[32,4096]{1,0:T(8,128)(2,1)S(1)}, u32[]{:S(2)}, u32[]{:S(2)}) collective-permute-start(bf16[32,4096]{1,0:T(8,128)(2,1)S(1)} %collective-permute-done.refs_1_), channel_id=1, source_target_pairs={{0,96},{16,112},{32,0},{48,16},{64,32},{80,48},{96,64},{112,80},{1... | collective-permute-start | bytes 786440 | tf_op jit(solution)/shard_map/ppermute | solution.py:295
  15.2 5.4 %shard_map.68 = (f32[193,32,128]{2,1,0:T(8,128)S(1)}, bf16[384,128,128]{2,1,0:T(8,128)(2,1)S(1)}) custom-call(s32[384]{0:T(512)S(1)} %get-tuple-element.30.codes, s32[5]{0:T(128)S(1)} %pad_add_fusion.1.scal, bf16[384,128,128]{2,1,0:T(8,128)(2,1)} %bitcast.17, bf16[32,4096]{1,0:T(8,128)(2,1)} %bitcast.21, bf16[32,4096]{1,0:T(8,128)(2,1)S(1)} %collective-permute-done.refs_1_, ...), custom_call_target="tpu_custom_call" | custom-call | tf_op jit(solution)/shard_map/pallas_call | solution.py:249
  20.5 3.0 %collective-permute-done.6.there = bf16[32,4096]{1,0:T(8,128)(2,1)S(1)} collective-permute-done((bf16[32,4096]{1,0:T(8,128)(2,1)S(1)}, bf16[32,4096]{1,0:T(8,128)(2,1)S(1)}, u32[]{:S(2)}, u32[]{:S(2)}) %collective-permute-start.6) | collective-permute-done | bytes 262176 | tf_op jit(solution)/shard_map/ppermute | solution.py:295
  23.5 1.8 %shard_map.69 = (bf16[16,392,128]{2,1,0:T(8,128)(2,1)S(1)}, f32[193,32,128]{2,1,0:T(8,128)S(1)}) custom-call(s32[384]{0:T(512)S(1)} %get-tuple-element.28.codes, s32[5]{0:T(128)S(1)} %pad_add_fusion.1.scal, bf16[384,128,128]{2,1,0:T(8,128)(2,1)S(1)} %get-tuple-element.34.tiles, ...), custom_call_target="tpu_custom_call", output_to_operand_aliasing={{1}: (6, {})} | custom-call | tf_op jit(solution)/shard_map/pallas_call | solution.py:249
  25.4 29.9 %all_to_all.10.recv = bf16[16,392,128]{2,1,0:T(8,128)(2,1)S(1)} all-to-all(bf16[16,392,128]{2,1,0:T(8,128)(2,1)S(1)} %get-tuple-element.40), channel_id=1, replica_groups=mesh['row'=8,'col'=16] {'col'}, dimensions={0} | all-to-all | bytes 3211264 | tf_op jit(solution)/shard_map/all_to_all | solution.py:338
  55.3 1.5 %shard_map.70 = (bf16[32,32,128]{2,1,0:T(8,128)(2,1)S(1)}, bf16[16,384,128]{2,1,0:T(8,128)(2,1)S(1)}) custom-call(bf16[16,392,128]{2,1,0:T(8,128)(2,1)S(1)} %all_to_all.10.recv), custom_call_target="tpu_custom_call" | custom-call | tf_op jit(solution)/shard_map/pallas_call | solution.py:249
  56.8 22.3 %all_to_all.11 = bf16[16,384,128]{2,1,0:T(8,128)(2,1)S(1)} all-to-all(bf16[16,384,128]{2,1,0:T(8,128)(2,1)S(1)} %get-tuple-element.42), channel_id=1, replica_groups=mesh['row'=8,'col'=16] {'col'}, dimensions={0} | all-to-all | bytes 3145728 | tf_op jit(solution)/shard_map/all_to_all | solution.py:352
  79.1 3.2 %shard_map.72 = (f32[3,32,32,128]{3,2,1,0:T(8,128)S(1)}, bf16[2,32,32,128]{3,2,1,0:T(8,128)(2,1)S(1)}, bf16[32,32,128]{2,1,0:T(8,128)(2,1)S(1)}) custom-call(s32[384]{0:T(512)S(1)} %get-tuple-element.30.codes, s32[5]{0:T(128)S(1)} %pad_add_fusion.1.scal, bf16[384,128,128]{2,1,0:T(8,128)(2,1)S(1)} %get-tuple-element.34.tiles, bf16[192,32,128]{2,1,0:T(8,128)(2,1)S(1)} %bitcast.15), custom_call_target="tpu_custom_call" | custom-call | tf_op jit(solution)/shard_map/pallas_call | solution.py:249
  82.3 4.9 %collective-permute-start.8 = (bf16[2,32,32,128]{3,2,1,0:T(8,128)(2,1)S(1)}, bf16[2,32,32,128]{3,2,1,0:T(8,128)(2,1)S(1)}, u32[]{:S(2)}, u32[]{:S(2)}) collective-permute-start(bf16[2,32,32,128]{3,2,1,0:T(8,128)(2,1)S(1)} %get-tuple-element.45), channel_id=1, source_target_pairs={{0,16},{16,0},{32,48},{48,32},{64,80},{80,64},{96,112},{112,96},{1... | collective-permute-start | bytes 1572872 | tf_op jit(solution)/shard_map/ppermute | solution.py:298
  87.3 1.4 %collective-permute-done.8.got = bf16[2,32,32,128]{3,2,1,0:T(8,128)(2,1)S(1)} collective-permute-done((bf16[2,32,32,128]{3,2,1,0:T(8,128)(2,1)S(1)}, bf16[2,32,32,128]{3,2,1,0:T(8,128)(2,1)S(1)}, u32[]{:S(2)}, u32[]{:S(2)}) %collective-permute-start.8) | collective-permute-done | bytes 524320 | tf_op jit(solution)/shard_map/ppermute | solution.py:298
  89.0 2.7 %collective-permute-start.10 = (bf16[32,32,128]{2,1,0:T(8,128)(2,1)S(1)}, bf16[32,32,128]{2,1,0:T(8,128)(2,1)S(1)}, u32[]{:S(2)}, u32[]{:S(2)}) collective-permute-start(bf16[32,32,128]{2,1,0:T(8,128)(2,1)S(1)} %get-tuple-element.49), channel_id=1, source_target_pairs={{0,96},{16,112},{32,0},{48,16},{64,32},{80,48},{96,64},{112,80},{1... | collective-permute-start | bytes 786440 | tf_op jit(solution)/shard_map/ppermute | solution.py:295
  91.7 1.5 %shard_map.75 = (f32[32,32,128]{2,1,0:T(8,128)S(1)}, bf16[16,32,128]{2,1,0:T(8,128)(2,1)S(1)}, bf16[16,32,128]{2,1,0:T(8,128)(2,1)S(1)}) custom-call(s32[384]{0:T(512)S(1)} %get-tuple-element.28.codes, s32[5]{0:T(128)S(1)} %pad_add_fusion.1.scal, bf16[384,128,128]{2,1,0:T(8,128)(2,1)S(1)} %get-tuple-element.34.tiles, bf16[192,32,128]{2,1,0:T(8,128)(2,1)S(1)} %bitcast.16), custom_call_target="tpu_custom_call" | custom-call | flops 68719476736 | bytes 67108864 | tf_op jit(solution)/shard_map/pallas_call | solution.py:249
  93.1 1.4 %collective-permute-start.11 = (bf16[16,32,128]{2,1,0:T(8,128)(2,1)S(1)}, bf16[16,32,128]{2,1,0:T(8,128)(2,1)S(1)}, u32[]{:S(2)}, u32[]{:S(2)}) collective-permute-start(bf16[16,32,128]{2,1,0:T(8,128)(2,1)S(1)} %get-tuple-element.52), channel_id=1, source_target_pairs={{0,16},{16,0},{32,48},{48,32},{64,80},{80,64},{96,112},{112,96},{1... | collective-permute-start | bytes 393224 | tf_op jit(solution)/shard_map/ppermute | solution.py:298
  94.6 0.7 shard_map.71
  96.1 1.7 %collective-permute-done.9.one = bf16[32,32,128]{2,1,0:T(8,128)(2,1)S(1)} collective-permute-done((bf16[32,32,128]{2,1,0:T(8,128)(2,1)S(1)}, bf16[32,32,128]{2,1,0:T(8,128)(2,1)S(1)}, u32[]{:S(2)}, u32[]{:S(2)}) %collective-permute-start.9) | collective-permute-done | bytes 262176 | tf_op jit(solution)/shard_map/ppermute | solution.py:295
  97.9 7.4 %collective-permute-done.13.two = bf16[32,32,128]{2,1,0:T(8,128)(2,1)S(1)} collective-permute-done((bf16[32,32,128]{2,1,0:T(8,128)(2,1)S(1)}, bf16[32,32,128]{2,1,0:T(8,128)(2,1)S(1)}, u32[]{:S(2)}, u32[]{:S(2)}) %collective-permute-start.13) | collective-permute-done | bytes 262176 | tf_op jit(solution)/shard_map/ppermute | solution.py:295
  105.3 0.8 shard_map.77
  (42 shorter events, 4.2 us)
Async XLA Ops:
  0.6 9.1 %collective-permute-start.2 = (bf16[32,4096]{1,0:T(8,128)(2,1)}, bf16[32,4096]{1,0:T(8,128)(2,1)S(1)}, u32[]{:S(2)}, u32[]{:S(2)}) collective-permute-start(bf16[32,4096]{1,0:T(8,128)(2,1)} %bitcast.18), channel_id=1, source_target_pairs={{0,16},{16,0},{32,48},{48,32},{64,80},{80,64},{96,112},{112,96},{1... | collective-permute-start | bytes 786440 | tf_op jit(solution)/shard_map/ppermute | solution.py:298
  2.1 9.3 %collective-permute-start.1 = (bf16[32,4096]{1,0:T(8,128)(2,1)}, bf16[32,4096]{1,0:T(8,128)(2,1)S(1)}, u32[]{:S(2)}, u32[]{:S(2)}) collective-permute-start(bf16[32,4096]{1,0:T(8,128)(2,1)} %bitcast.19), channel_id=1, source_target_pairs={{0,32},{16,48},{32,64},{48,80},{64,96},{80,112},{96,0},{112,16},{1... | collective-permute-start | bytes 786440 | tf_op jit(solution)/shard_map/ppermute | solution.py:295
  3.4 8.0 %collective-permute-start = (bf16[32,4096]{1,0:T(8,128)(2,1)}, bf16[32,4096]{1,0:T(8,128)(2,1)S(1)}, u32[]{:S(2)}, u32[]{:S(2)}) collective-permute-start(bf16[32,4096]{1,0:T(8,128)(2,1)} %bitcast.20), channel_id=1, source_target_pairs={{0,96},{16,112},{32,0},{48,16},{64,32},{80,48},{96,64},{112,80},{1... | collective-permute-start | bytes 786440 | tf_op jit(solution)/shard_map/ppermute | solution.py:295
  11.4 3.7 %collective-permute-start.4 = (bf16[32,4096]{1,0:T(8,128)(2,1)S(1)}, bf16[32,4096]{1,0:T(8,128)(2,1)S(1)}, u32[]{:S(2)}, u32[]{:S(2)}) collective-permute-start(bf16[32,4096]{1,0:T(8,128)(2,1)S(1)} %collective-permute-done.1.refs_2_), channel_id=1, source_target_pairs={{0,16},{16,0},{32,48},{48,32},{64,80},{80,64},{96,112},{112,96},{1... | collective-permute-start | bytes 786440 | tf_op jit(solution)/shard_map/ppermute | solution.py:298
  12.5 2.7 %collective-permute-start.3 = (bf16[32,4096]{1,0:T(8,128)(2,1)S(1)}, bf16[32,4096]{1,0:T(8,128)(2,1)S(1)}, u32[]{:S(2)}, u32[]{:S(2)}) collective-permute-start(bf16[32,4096]{1,0:T(8,128)(2,1)S(1)} %collective-permute-done.refs_1_), channel_id=1, source_target_pairs={{0,16},{16,0},{32,48},{48,32},{64,80},{80,64},{96,112},{112,96},{1... | collective-permute-start | bytes 786440 | tf_op jit(solution)/shard_map/ppermute | solution.py:298
  12.5 8.0 %collective-permute-start.5 = (bf16[32,4096]{1,0:T(8,128)(2,1)S(1)}, bf16[32,4096]{1,0:T(8,128)(2,1)S(1)}, u32[]{:S(2)}, u32[]{:S(2)}) collective-permute-start(bf16[32,4096]{1,0:T(8,128)(2,1)S(1)} %collective-permute-done.refs_1_), channel_id=1, source_target_pairs={{0,96},{16,112},{32,0},{48,16},{64,32},{80,48},{96,64},{112,80},{1... | collective-permute-start | bytes 786440 | tf_op jit(solution)/shard_map/ppermute | solution.py:295
  15.1 8.4 %collective-permute-start.6 = (bf16[32,4096]{1,0:T(8,128)(2,1)S(1)}, bf16[32,4096]{1,0:T(8,128)(2,1)S(1)}, u32[]{:S(2)}, u32[]{:S(2)}) collective-permute-start(bf16[32,4096]{1,0:T(8,128)(2,1)S(1)} %collective-permute-done.4.refs_5_), channel_id=1, source_target_pairs={{0,32},{16,48},{32,64},{48,80},{64,96},{80,112},{96,0},{112,16},{1... | collective-permute-start | bytes 786440 | tf_op jit(solution)/shard_map/ppermute | solution.py:295
  82.3 6.5 %collective-permute-start.8 = (bf16[2,32,32,128]{3,2,1,0:T(8,128)(2,1)S(1)}, bf16[2,32,32,128]{3,2,1,0:T(8,128)(2,1)S(1)}, u32[]{:S(2)}, u32[]{:S(2)}) collective-permute-start(bf16[2,32,32,128]{3,2,1,0:T(8,128)(2,1)S(1)} %get-tuple-element.45), channel_id=1, source_target_pairs={{0,16},{16,0},{32,48},{48,32},{64,80},{80,64},{96,112},{112,96},{1... | collective-permute-start | bytes 1572872 | tf_op jit(solution)/shard_map/ppermute | solution.py:298
  87.2 8.8 %collective-permute-start.7 = (bf16[32,32,128]{2,1,0:T(8,128)(2,1)S(1)}, bf16[32,32,128]{2,1,0:T(8,128)(2,1)S(1)}, u32[]{:S(2)}, u32[]{:S(2)}) collective-permute-start(bf16[32,32,128]{2,1,0:T(8,128)(2,1)S(1)} %get-tuple-element.44), channel_id=1, source_target_pairs={{0,16},{16,0},{32,48},{48,32},{64,80},{80,64},{96,112},{112,96},{1... | collective-permute-start | bytes 786440 | tf_op jit(solution)/shard_map/ppermute | solution.py:298
  88.9 8.8 %collective-permute-start.9 = (bf16[32,32,128]{2,1,0:T(8,128)(2,1)S(1)}, bf16[32,32,128]{2,1,0:T(8,128)(2,1)S(1)}, u32[]{:S(2)}, u32[]{:S(2)}) collective-permute-start(bf16[32,32,128]{2,1,0:T(8,128)(2,1)S(1)} %get-tuple-element.48), channel_id=1, source_target_pairs={{0,32},{16,48},{32,64},{48,80},{64,96},{80,112},{96,0},{112,16},{1... | collective-permute-start | bytes 786440 | tf_op jit(solution)/shard_map/ppermute | solution.py:295
  89.0 8.7 %collective-permute-start.10 = (bf16[32,32,128]{2,1,0:T(8,128)(2,1)S(1)}, bf16[32,32,128]{2,1,0:T(8,128)(2,1)S(1)}, u32[]{:S(2)}, u32[]{:S(2)}) collective-permute-start(bf16[32,32,128]{2,1,0:T(8,128)(2,1)S(1)} %get-tuple-element.49), channel_id=1, source_target_pairs={{0,96},{16,112},{32,0},{48,16},{64,32},{80,48},{96,64},{112,80},{1... | collective-permute-start | bytes 786440 | tf_op jit(solution)/shard_map/ppermute | solution.py:295
  93.1 2.4 %collective-permute-start.11 = (bf16[16,32,128]{2,1,0:T(8,128)(2,1)S(1)}, bf16[16,32,128]{2,1,0:T(8,128)(2,1)S(1)}, u32[]{:S(2)}, u32[]{:S(2)}) collective-permute-start(bf16[16,32,128]{2,1,0:T(8,128)(2,1)S(1)} %get-tuple-element.52), channel_id=1, source_target_pairs={{0,16},{16,0},{32,48},{48,32},{64,80},{80,64},{96,112},{112,96},{1... | collective-permute-start | bytes 393224 | tf_op jit(solution)/shard_map/ppermute | solution.py:298
  94.5 1.3 %collective-permute-start.12 = (bf16[16,32,128]{2,1,0:T(8,128)(2,1)S(1)}, bf16[16,32,128]{2,1,0:T(8,128)(2,1)S(1)}, u32[]{:S(2)}, u32[]{:S(2)}) collective-permute-start(bf16[16,32,128]{2,1,0:T(8,128)(2,1)S(1)} %get-tuple-element.53), channel_id=1, source_target_pairs={{0,16},{16,0},{32,48},{48,32},{64,80},{80,64},{96,112},{112,96},{1... | collective-permute-start | bytes 393224 | tf_op jit(solution)/shard_map/ppermute | solution.py:298
  95.9 9.3 %collective-permute-start.13 = (bf16[32,32,128]{2,1,0:T(8,128)(2,1)S(1)}, bf16[32,32,128]{2,1,0:T(8,128)(2,1)S(1)}, u32[]{:S(2)}, u32[]{:S(2)}) collective-permute-start(bf16[32,32,128]{2,1,0:T(8,128)(2,1)S(1)} %shard_map.76), channel_id=1, source_target_pairs={{0,64},{16,80},{32,96},{48,112},{64,0},{80,16},{96,32},{112,48},{1... | collective-permute-start | bytes 786440 | tf_op jit(solution)/shard_map/ppermute | solution.py:295

commit v7 on v6

--- a/solution.py
+++ b/solution.py
@@ -147,7 +147,7 @@
             total[p] = value
         return 0
 
-    lax.fori_loop(0, N_COL, add, 0)
+    lax.fori_loop(0, N_COL, add, 0, unroll=4)
     for b in range(SHARE):
         blocks[b] = total[b].astype(jnp.bfloat16)
 
@@ -156,7 +156,7 @@
             send[c, q * K:(q + 1) * K] = blocks[ids[c, q]]
         return 0
 
-    lax.fori_loop(0, N_COL, spread, 0, unroll=4)
+    lax.fori_loop(0, N_COL, spread, 0, unroll=8)
 
 
 def backward_spots(blocks):

time: 106 us -> 105 us (level)
  Pallas kernels: 15.2 us -> 18.5 us
  starting transfers between devices: 17.2 us -> 14.9 us
  waiting for transfers between devices: 15.6 us -> 14.1 us
    pallas_call x10, Pallas kernels: 15.2 us -> 18.5 us  [call(): pl.pallas_call(kernel, out_shape=outs, in_specs=specs, out_specs=spec_vme...]
    ppermute x7, starting transfers between devices: 9.11 us -> 6.75 us  [swap_core(): return lax.ppermute(value, 'row', [(i, i ^ 1) for i in range(8)])]
    ppermute x7, waiting for transfers between devices: 13.7 us -> 12.1 us  [along_x(): return lax.ppermute(value, 'row', [(i, (i + 2 * d) % 8) for i in range(8)])]
  transfers between devices with their start and end apart: 14 -> 14, of which waited for: 7 -> 7; matrix products, arithmetic and copies ran while one was open for 4% -> 4% of each run, Pallas kernels for 8% -> 9%
where the time goes in v7:
time: 105 us; the launch traced here: 106 us
  blocking collectives  52.6 us (50%)
  Pallas kernels  18.5 us (18%)
  starting transfers between devices  14.9 us (14%)
  waiting for transfers between devices  14.1 us (13%)
  other arithmetic  3.96 us (4%)
  between operations  1.46 us (1%)
    all_to_all x1, blocking collectives, per_device(): recv = lax.all_to_all(send, 'col', 0, 0, tiled=True)  29.6 us
    all_to_all x1, blocking collectives, per_device(): lax.all_to_all(spread, 'col', 0, 0, tiled=True).reshape(N_NAMED, K, TILE)  22.9 us
    pallas_call x10, Pallas kernels, call(): pl.pallas_call(kernel, out_shape=outs, in_specs=specs, out_specs=spec_vme...  18.5 us
    ppermute x7, waiting for transfers between devices, along_x(): return lax.ppermute(value, 'row', [(i, (i + 2 * d) % 8) for i in range(8)])  12.1 us
    ppermute x7, starting transfers between devices, along_x(): return lax.ppermute(value, 'row', [(i, (i + 2 * d) % 8) for i in range(8)])  8.11 us
    ppermute x7, starting transfers between devices, swap_core(): return lax.ppermute(value, 'row', [(i, i ^ 1) for i in range(8)])  6.75 us
  transfers between devices with their start and end apart: 14, of which 7 were waited for; matrix products, arithmetic and copies ran while one was open for 4% of the time, Pallas kernels for 9%

profile of v7, /device:TPU:1, one launch (start us, length us, event | category | flops | bytes accessed | tf_op | source)
XLA Modules:
  0.0 105.7 jit_solution(1659391100172414868)
XLA Ops:
  0.6 1.5 %collective-permute-start.2 = (bf16[32,4096]{1,0:T(8,128)(2,1)}, bf16[32,4096]{1,0:T(8,128)(2,1)S(1)}, u32[]{:S(2)}, u32[]{:S(2)}) collective-permute-start(bf16[32,4096]{1,0:T(8,128)(2,1)} %bitcast.18), channel_id=1, source_target_pairs={{0,16},{16,0},{32,48},{48,32},{64,80},{80,64},{96,112},{112,96},{1... | collective-permute-start | bytes 786440 | tf_op jit(solution)/shard_map/ppermute | solution.py:298
  2.1 1.3 %collective-permute-start.1 = (bf16[32,4096]{1,0:T(8,128)(2,1)}, bf16[32,4096]{1,0:T(8,128)(2,1)S(1)}, u32[]{:S(2)}, u32[]{:S(2)}) collective-permute-start(bf16[32,4096]{1,0:T(8,128)(2,1)} %bitcast.19), channel_id=1, source_target_pairs={{0,32},{16,48},{32,64},{48,80},{64,96},{80,112},{96,0},{112,16},{1... | collective-permute-start | bytes 786440 | tf_op jit(solution)/shard_map/ppermute | solution.py:295
  3.4 1.4 %collective-permute-start = (bf16[32,4096]{1,0:T(8,128)(2,1)}, bf16[32,4096]{1,0:T(8,128)(2,1)S(1)}, u32[]{:S(2)}, u32[]{:S(2)}) collective-permute-start(bf16[32,4096]{1,0:T(8,128)(2,1)} %bitcast.20), channel_id=1, source_target_pairs={{0,96},{16,112},{32,0},{48,16},{64,32},{80,48},{96,64},{112,80},{1... | collective-permute-start | bytes 786440 | tf_op jit(solution)/shard_map/ppermute | solution.py:295
  5.5 0.7 reduce
  6.4 0.7 shift-left_reduce_fusion
  9.8 1.6 %collective-permute-done.1.refs_2_ = bf16[32,4096]{1,0:T(8,128)(2,1)S(1)} collective-permute-done((bf16[32,4096]{1,0:T(8,128)(2,1)}, bf16[32,4096]{1,0:T(8,128)(2,1)S(1)}, u32[]{:S(2)}, u32[]{:S(2)}) %collective-permute-start.1) | collective-permute-done | bytes 262176 | tf_op jit(solution)/shard_map/ppermute | solution.py:295
  11.4 1.0 collective-permute-start.4
  12.5 2.6 %collective-permute-start.5 = (bf16[32,4096]{1,0:T(8,128)(2,1)S(1)}, bf16[32,4096]{1,0:T(8,128)(2,1)S(1)}, u32[]{:S(2)}, u32[]{:S(2)}) collective-permute-start(bf16[32,4096]{1,0:T(8,128)(2,1)S(1)} %collective-permute-done.refs_1_), channel_id=1, source_target_pairs={{0,96},{16,112},{32,0},{48,16},{64,32},{80,48},{96,64},{112,80},{1... | collective-permute-start | bytes 786440 | tf_op jit(solution)/shard_map/ppermute | solution.py:295
  15.2 6.9 %shard_map.68 = (f32[193,32,128]{2,1,0:T(8,128)S(1)}, bf16[384,128,128]{2,1,0:T(8,128)(2,1)S(1)}) custom-call(s32[384]{0:T(512)S(1)} %get-tuple-element.30.codes, s32[5]{0:T(128)S(1)} %pad_add_fusion.1.scal, bf16[384,128,128]{2,1,0:T(8,128)(2,1)} %bitcast.17, bf16[32,4096]{1,0:T(8,128)(2,1)} %bitcast.21, bf16[32,4096]{1,0:T(8,128)(2,1)S(1)} %collective-permute-done.refs_1_, ...), custom_call_target="tpu_custom_call" | custom-call | tf_op jit(solution)/shard_map/pallas_call | solution.py:249
  22.1 1.4 %collective-permute-done.6.there = bf16[32,4096]{1,0:T(8,128)(2,1)S(1)} collective-permute-done((bf16[32,4096]{1,0:T(8,128)(2,1)S(1)}, bf16[32,4096]{1,0:T(8,128)(2,1)S(1)}, u32[]{:S(2)}, u32[]{:S(2)}) %collective-permute-start.6) | collective-permute-done | bytes 262176 | tf_op jit(solution)/shard_map/ppermute | solution.py:295
  23.5 2.3 %shard_map.69 = (bf16[16,392,128]{2,1,0:T(8,128)(2,1)S(1)}, f32[193,32,128]{2,1,0:T(8,128)S(1)}) custom-call(s32[384]{0:T(512)S(1)} %get-tuple-element.28.codes, s32[5]{0:T(128)S(1)} %pad_add_fusion.1.scal, bf16[384,128,128]{2,1,0:T(8,128)(2,1)S(1)} %get-tuple-element.34.tiles, ...), custom_call_target="tpu_custom_call", output_to_operand_aliasing={{1}: (6, {})} | custom-call | tf_op jit(solution)/shard_map/pallas_call | solution.py:249
  25.9 29.6 %all_to_all.10.recv = bf16[16,392,128]{2,1,0:T(8,128)(2,1)S(1)} all-to-all(bf16[16,392,128]{2,1,0:T(8,128)(2,1)S(1)} %get-tuple-element.40), channel_id=1, replica_groups=mesh['row'=8,'col'=16] {'col'}, dimensions={0} | all-to-all | bytes 3211264 | tf_op jit(solution)/shard_map/all_to_all | solution.py:338
  55.5 1.4 %shard_map.70 = (bf16[32,32,128]{2,1,0:T(8,128)(2,1)S(1)}, bf16[16,384,128]{2,1,0:T(8,128)(2,1)S(1)}) custom-call(bf16[16,392,128]{2,1,0:T(8,128)(2,1)S(1)} %all_to_all.10.recv), custom_call_target="tpu_custom_call" | custom-call | tf_op jit(solution)/shard_map/pallas_call | solution.py:249
  56.9 22.9 %all_to_all.11 = bf16[16,384,128]{2,1,0:T(8,128)(2,1)S(1)} all-to-all(bf16[16,384,128]{2,1,0:T(8,128)(2,1)S(1)} %get-tuple-element.42), channel_id=1, replica_groups=mesh['row'=8,'col'=16] {'col'}, dimensions={0} | all-to-all | bytes 3145728 | tf_op jit(solution)/shard_map/all_to_all | solution.py:352
  79.8 4.2 %shard_map.72 = (f32[3,32,32,128]{3,2,1,0:T(8,128)S(1)}, bf16[2,32,32,128]{3,2,1,0:T(8,128)(2,1)S(1)}, bf16[32,32,128]{2,1,0:T(8,128)(2,1)S(1)}) custom-call(s32[384]{0:T(512)S(1)} %get-tuple-element.30.codes, s32[5]{0:T(128)S(1)} %pad_add_fusion.1.scal, bf16[384,128,128]{2,1,0:T(8,128)(2,1)S(1)} %get-tuple-element.34.tiles, bf16[192,32,128]{2,1,0:T(8,128)(2,1)S(1)} %bitcast.15), custom_call_target="tpu_custom_call" | custom-call | tf_op jit(solution)/shard_map/pallas_call | solution.py:249
  84.0 2.9 %collective-permute-start.8 = (bf16[2,32,32,128]{3,2,1,0:T(8,128)(2,1)S(1)}, bf16[2,32,32,128]{3,2,1,0:T(8,128)(2,1)S(1)}, u32[]{:S(2)}, u32[]{:S(2)}) collective-permute-start(bf16[2,32,32,128]{3,2,1,0:T(8,128)(2,1)S(1)} %get-tuple-element.45), channel_id=1, source_target_pairs={{0,16},{16,0},{32,48},{48,32},{64,80},{80,64},{96,112},{112,96},{1... | collective-permute-start | bytes 1572872 | tf_op jit(solution)/shard_map/ppermute | solution.py:298
  87.0 1.4 %collective-permute-done.8.got = bf16[2,32,32,128]{3,2,1,0:T(8,128)(2,1)S(1)} collective-permute-done((bf16[2,32,32,128]{3,2,1,0:T(8,128)(2,1)S(1)}, bf16[2,32,32,128]{3,2,1,0:T(8,128)(2,1)S(1)}, u32[]{:S(2)}, u32[]{:S(2)}) %collective-permute-start.8) | collective-permute-done | bytes 524320 | tf_op jit(solution)/shard_map/ppermute | solution.py:298
  88.7 2.7 %collective-permute-start.10 = (bf16[32,32,128]{2,1,0:T(8,128)(2,1)S(1)}, bf16[32,32,128]{2,1,0:T(8,128)(2,1)S(1)}, u32[]{:S(2)}, u32[]{:S(2)}) collective-permute-start(bf16[32,32,128]{2,1,0:T(8,128)(2,1)S(1)} %get-tuple-element.49), channel_id=1, source_target_pairs={{0,96},{16,112},{32,0},{48,16},{64,32},{80,48},{96,64},{112,80},{1... | collective-permute-start | bytes 786440 | tf_op jit(solution)/shard_map/ppermute | solution.py:295
  91.3 1.8 %shard_map.75 = (f32[32,32,128]{2,1,0:T(8,128)S(1)}, bf16[16,32,128]{2,1,0:T(8,128)(2,1)S(1)}, bf16[16,32,128]{2,1,0:T(8,128)(2,1)S(1)}) custom-call(s32[384]{0:T(512)S(1)} %get-tuple-element.28.codes, s32[5]{0:T(128)S(1)} %pad_add_fusion.1.scal, bf16[384,128,128]{2,1,0:T(8,128)(2,1)S(1)} %get-tuple-element.34.tiles, bf16[192,32,128]{2,1,0:T(8,128)(2,1)S(1)} %bitcast.16), custom_call_target="tpu_custom_call" | custom-call | flops 68719476736 | bytes 67108864 | tf_op jit(solution)/shard_map/pallas_call | solution.py:249
  93.1 1.1 collective-permute-start.11
  94.3 0.7 shard_map.71
  95.7 1.7 %collective-permute-done.9.one = bf16[32,32,128]{2,1,0:T(8,128)(2,1)S(1)} collective-permute-done((bf16[32,32,128]{2,1,0:T(8,128)(2,1)S(1)}, bf16[32,32,128]{2,1,0:T(8,128)(2,1)S(1)}, u32[]{:S(2)}, u32[]{:S(2)}) %collective-permute-start.9) | collective-permute-done | bytes 262176 | tf_op jit(solution)/shard_map/ppermute | solution.py:295
  97.6 7.4 %collective-permute-done.13.two = bf16[32,32,128]{2,1,0:T(8,128)(2,1)S(1)} collective-permute-done((bf16[32,32,128]{2,1,0:T(8,128)(2,1)S(1)}, bf16[32,32,128]{2,1,0:T(8,128)(2,1)S(1)}, u32[]{:S(2)}, u32[]{:S(2)}) %collective-permute-start.13) | collective-permute-done | bytes 262176 | tf_op jit(solution)/shard_map/ppermute | solution.py:295
  104.9 0.8 shard_map.77
  (42 shorter events, 4.2 us)
Async XLA Ops:
  0.6 9.1 %collective-permute-start.2 = (bf16[32,4096]{1,0:T(8,128)(2,1)}, bf16[32,4096]{1,0:T(8,128)(2,1)S(1)}, u32[]{:S(2)}, u32[]{:S(2)}) collective-permute-start(bf16[32,4096]{1,0:T(8,128)(2,1)} %bitcast.18), channel_id=1, source_target_pairs={{0,16},{16,0},{32,48},{48,32},{64,80},{80,64},{96,112},{112,96},{1... | collective-permute-start | bytes 786440 | tf_op jit(solution)/shard_map/ppermute | solution.py:298
  2.1 9.3 %collective-permute-start.1 = (bf16[32,4096]{1,0:T(8,128)(2,1)}, bf16[32,4096]{1,0:T(8,128)(2,1)S(1)}, u32[]{:S(2)}, u32[]{:S(2)}) collective-permute-start(bf16[32,4096]{1,0:T(8,128)(2,1)} %bitcast.19), channel_id=1, source_target_pairs={{0,32},{16,48},{32,64},{48,80},{64,96},{80,112},{96,0},{112,16},{1... | collective-permute-start | bytes 786440 | tf_op jit(solution)/shard_map/ppermute | solution.py:295
  3.4 8.0 %collective-permute-start = (bf16[32,4096]{1,0:T(8,128)(2,1)}, bf16[32,4096]{1,0:T(8,128)(2,1)S(1)}, u32[]{:S(2)}, u32[]{:S(2)}) collective-permute-start(bf16[32,4096]{1,0:T(8,128)(2,1)} %bitcast.20), channel_id=1, source_target_pairs={{0,96},{16,112},{32,0},{48,16},{64,32},{80,48},{96,64},{112,80},{1... | collective-permute-start | bytes 786440 | tf_op jit(solution)/shard_map/ppermute | solution.py:295
  11.4 3.7 %collective-permute-start.4 = (bf16[32,4096]{1,0:T(8,128)(2,1)S(1)}, bf16[32,4096]{1,0:T(8,128)(2,1)S(1)}, u32[]{:S(2)}, u32[]{:S(2)}) collective-permute-start(bf16[32,4096]{1,0:T(8,128)(2,1)S(1)} %collective-permute-done.1.refs_2_), channel_id=1, source_target_pairs={{0,16},{16,0},{32,48},{48,32},{64,80},{80,64},{96,112},{112,96},{1... | collective-permute-start | bytes 786440 | tf_op jit(solution)/shard_map/ppermute | solution.py:298
  12.5 2.7 %collective-permute-start.3 = (bf16[32,4096]{1,0:T(8,128)(2,1)S(1)}, bf16[32,4096]{1,0:T(8,128)(2,1)S(1)}, u32[]{:S(2)}, u32[]{:S(2)}) collective-permute-start(bf16[32,4096]{1,0:T(8,128)(2,1)S(1)} %collective-permute-done.refs_1_), channel_id=1, source_target_pairs={{0,16},{16,0},{32,48},{48,32},{64,80},{80,64},{96,112},{112,96},{1... | collective-permute-start | bytes 786440 | tf_op jit(solution)/shard_map/ppermute | solution.py:298
  12.5 9.5 %collective-permute-start.5 = (bf16[32,4096]{1,0:T(8,128)(2,1)S(1)}, bf16[32,4096]{1,0:T(8,128)(2,1)S(1)}, u32[]{:S(2)}, u32[]{:S(2)}) collective-permute-start(bf16[32,4096]{1,0:T(8,128)(2,1)S(1)} %collective-permute-done.refs_1_), channel_id=1, source_target_pairs={{0,96},{16,112},{32,0},{48,16},{64,32},{80,48},{96,64},{112,80},{1... | collective-permute-start | bytes 786440 | tf_op jit(solution)/shard_map/ppermute | solution.py:295
  15.1 8.4 %collective-permute-start.6 = (bf16[32,4096]{1,0:T(8,128)(2,1)S(1)}, bf16[32,4096]{1,0:T(8,128)(2,1)S(1)}, u32[]{:S(2)}, u32[]{:S(2)}) collective-permute-start(bf16[32,4096]{1,0:T(8,128)(2,1)S(1)} %collective-permute-done.4.refs_5_), channel_id=1, source_target_pairs={{0,32},{16,48},{32,64},{48,80},{64,96},{80,112},{96,0},{112,16},{1... | collective-permute-start | bytes 786440 | tf_op jit(solution)/shard_map/ppermute | solution.py:295
  84.0 4.4 %collective-permute-start.8 = (bf16[2,32,32,128]{3,2,1,0:T(8,128)(2,1)S(1)}, bf16[2,32,32,128]{3,2,1,0:T(8,128)(2,1)S(1)}, u32[]{:S(2)}, u32[]{:S(2)}) collective-permute-start(bf16[2,32,32,128]{3,2,1,0:T(8,128)(2,1)S(1)} %get-tuple-element.45), channel_id=1, source_target_pairs={{0,16},{16,0},{32,48},{48,32},{64,80},{80,64},{96,112},{112,96},{1... | collective-permute-start | bytes 1572872 | tf_op jit(solution)/shard_map/ppermute | solution.py:298
  86.9 8.8 %collective-permute-start.7 = (bf16[32,32,128]{2,1,0:T(8,128)(2,1)S(1)}, bf16[32,32,128]{2,1,0:T(8,128)(2,1)S(1)}, u32[]{:S(2)}, u32[]{:S(2)}) collective-permute-start(bf16[32,32,128]{2,1,0:T(8,128)(2,1)S(1)} %get-tuple-element.44), channel_id=1, source_target_pairs={{0,16},{16,0},{32,48},{48,32},{64,80},{80,64},{96,112},{112,96},{1... | collective-permute-start | bytes 786440 | tf_op jit(solution)/shard_map/ppermute | solution.py:298
  88.6 8.8 %collective-permute-start.9 = (bf16[32,32,128]{2,1,0:T(8,128)(2,1)S(1)}, bf16[32,32,128]{2,1,0:T(8,128)(2,1)S(1)}, u32[]{:S(2)}, u32[]{:S(2)}) collective-permute-start(bf16[32,32,128]{2,1,0:T(8,128)(2,1)S(1)} %get-tuple-element.48), channel_id=1, source_target_pairs={{0,32},{16,48},{32,64},{48,80},{64,96},{80,112},{96,0},{112,16},{1... | collective-permute-start | bytes 786440 | tf_op jit(solution)/shard_map/ppermute | solution.py:295
  88.7 8.7 %collective-permute-start.10 = (bf16[32,32,128]{2,1,0:T(8,128)(2,1)S(1)}, bf16[32,32,128]{2,1,0:T(8,128)(2,1)S(1)}, u32[]{:S(2)}, u32[]{:S(2)}) collective-permute-start(bf16[32,32,128]{2,1,0:T(8,128)(2,1)S(1)} %get-tuple-element.49), channel_id=1, source_target_pairs={{0,96},{16,112},{32,0},{48,16},{64,32},{80,48},{96,64},{112,80},{1... | collective-permute-start | bytes 786440 | tf_op jit(solution)/shard_map/ppermute | solution.py:295
  93.1 2.0 %collective-permute-start.11 = (bf16[16,32,128]{2,1,0:T(8,128)(2,1)S(1)}, bf16[16,32,128]{2,1,0:T(8,128)(2,1)S(1)}, u32[]{:S(2)}, u32[]{:S(2)}) collective-permute-start(bf16[16,32,128]{2,1,0:T(8,128)(2,1)S(1)} %get-tuple-element.52), channel_id=1, source_target_pairs={{0,16},{16,0},{32,48},{48,32},{64,80},{80,64},{96,112},{112,96},{1... | collective-permute-start | bytes 393224 | tf_op jit(solution)/shard_map/ppermute | solution.py:298
  94.2 1.3 %collective-permute-start.12 = (bf16[16,32,128]{2,1,0:T(8,128)(2,1)S(1)}, bf16[16,32,128]{2,1,0:T(8,128)(2,1)S(1)}, u32[]{:S(2)}, u32[]{:S(2)}) collective-permute-start(bf16[16,32,128]{2,1,0:T(8,128)(2,1)S(1)} %get-tuple-element.53), channel_id=1, source_target_pairs={{0,16},{16,0},{32,48},{48,32},{64,80},{80,64},{96,112},{112,96},{1... | collective-permute-start | bytes 393224 | tf_op jit(solution)/shard_map/ppermute | solution.py:298
  95.6 9.3 %collective-permute-start.13 = (bf16[32,32,128]{2,1,0:T(8,128)(2,1)S(1)}, bf16[32,32,128]{2,1,0:T(8,128)(2,1)S(1)}, u32[]{:S(2)}, u32[]{:S(2)}) collective-permute-start(bf16[32,32,128]{2,1,0:T(8,128)(2,1)S(1)} %shard_map.76), channel_id=1, source_target_pairs={{0,64},{16,80},{32,96},{48,112},{64,0},{80,16},{96,32},{112,48},{1... | collective-permute-start | bytes 786440 | tf_op jit(solution)/shard_map/ppermute | solution.py:295
